TPU v7x, 256 devices: a whole 4x4x8 slice. The times are simulated.
256 devices in a mesh: dp: 64 (over z, y, core), section: 4 (over x).
Axes of the slice: x: 4, y: 4, z: 8, core: 2. Of those that a mesh axis runs over, the one named last changes fastest.
Arguments:
- query_hidden: bfloat16 [32768, 4096], P('dp', 'section'), may hold values from -0.5 to 0.5
- tool_hidden: bfloat16 [32768, 4096], P('dp', 'section'), may hold values from -0.5 to 0.5
- norm_gain: float32 [4096], P('section'), may hold values from 0.5 to 1.5
- positive_tool: int32 [32768], P('dp'), may hold values from 0 to 511
- hard_owner: int32 [32768, 2], P('dp'), may hold values from 0 to 63, as said below
- hard_row: int32 [32768, 2], P('dp'), may hold values from 0 to 511
- hard_valid: int32 [32768, 2], P('dp'), may hold values from 0 to 1
Outputs:
- query_grad: bfloat16 [32768, 4096], P('dp', 'section')
- tool_grad: bfloat16 [32768, 4096], P('dp', 'section')
- gain_grad: float32 [4096], P('section')
Inputs may be any that keep to these rules, and one draw needn't show every extreme that they name: `hard_owner`: each dp index's valid slots name any one owner at most 32 times; two owners, the same for every dp index and drawn from the seed, are named exactly 32 times by the valid slots of every dp index.
All inputs are finite; a program needn't handle non-finite values.
Results may differ from a plain program's by a relative error of at most 0.0067.
Values may be sent and summed in bfloat16 or wider, within the bound.
A program may use at most 128 MiB of HBM per device.

v0:
```python
import jax
import jax.numpy as jnp
from jax import lax
from jax.sharding import PartitionSpec as P

EPSILON = 1e-06
SOFTMAX_TEMP = 0.05


def softmax_grads(shard_scores, negative_scores, positive, valid_mask):
    selected_rows = lax.broadcasted_iota(jnp.int32, shard_scores.shape, 1) == positive[:, None]
    softmax_weights = jnp.exp(shard_scores / SOFTMAX_TEMP)
    shard_probabilities = softmax_weights / jnp.sum(softmax_weights, axis=1, keepdims=True)
    positive_score = jnp.sum(jnp.where(selected_rows, shard_scores, 0.0), axis=1)
    positive_weight = jnp.exp(positive_score / SOFTMAX_TEMP)
    negative_weights = jnp.where(valid_mask > 0, jnp.exp(negative_scores / SOFTMAX_TEMP), 0.0)
    negative_weight_sum = positive_weight + jnp.sum(negative_weights, axis=1)
    shard_gradients = (
        (
            shard_probabilities
            + jnp.where(selected_rows, (positive_weight / negative_weight_sum - 2.0)[:, None], 0.0)
        )
        / SOFTMAX_TEMP
    ).astype(jnp.bfloat16)
    negative_gradients = (negative_weights / (negative_weight_sum[:, None] * SOFTMAX_TEMP)).astype(
        jnp.bfloat16
    )
    return (shard_gradients, negative_gradients)


def body(query_hidden, tool_hidden, norm_gain, positive_tool, hard_owner, hard_row, hard_valid):
    query_count, features = query_hidden.shape
    per_query = hard_owner.shape[1]
    group_size = lax.axis_size("dp")
    capacity = max(2, 2 * query_count * per_query // group_size)
    query_scaled = query_hidden.astype(jnp.float32) * norm_gain
    tool_scaled = tool_hidden.astype(jnp.float32) * norm_gain
    query_squares, tool_squares = lax.psum(
        (jnp.sum(query_scaled * query_scaled, axis=1), jnp.sum(tool_scaled * tool_scaled, axis=1)),
        "section",
    )
    query_norm = jnp.sqrt(query_squares + EPSILON)
    tool_norm = jnp.sqrt(tool_squares + EPSILON)
    query_unit32 = query_scaled / query_norm[:, None]
    tool_unit32 = tool_scaled / tool_norm[:, None]
    query_unit = query_unit32.astype(jnp.bfloat16)
    tool_unit = tool_unit32.astype(jnp.bfloat16)
    owners = hard_owner.reshape(-1)
    wanted_rows = hard_row.reshape(-1)
    usable = hard_valid.reshape(-1) > 0
    owner_table = (
        (owners[:, None] == jnp.arange(group_size, dtype=jnp.int32)[None, :]) & usable[:, None]
    ).astype(jnp.int32)
    earlier = jnp.cumsum(owner_table, axis=0) - owner_table
    slot_place = jnp.sum(earlier * owner_table, axis=1)
    target = jnp.where(usable, owners * capacity + slot_place, group_size * capacity)
    requests = (
        jnp.zeros((group_size * capacity,), jnp.int32)
        .at[target]
        .set(wanted_rows, mode="drop")
        .reshape(group_size, capacity)
    )
    indices = lax.all_to_all(requests, "dp", split_axis=0, concat_axis=0, tiled=True)
    answers = tool_unit[indices]
    back = lax.all_to_all(answers, "dp", split_axis=0, concat_axis=0, tiled=True)
    lookup = jnp.where(usable, target, 0)
    hard_units = back.reshape(group_size * capacity, features)[lookup].reshape(
        query_count, per_query, features
    )
    local_part = lax.dot_general(
        query_unit, tool_unit, (((1,), (1,)), ((), ())), preferred_element_type=jnp.float32
    )
    hard_part = jnp.einsum("qd,qkd->qk", query_unit, hard_units, preferred_element_type=jnp.float32)
    shard_scores, negative_scores = (
        lax.psum(local_part.astype(jnp.bfloat16), "section").astype(jnp.float32),
        lax.psum(hard_part.astype(jnp.bfloat16), "section").astype(jnp.float32),
    )
    shard_gradients, negative_gradients = softmax_grads(
        shard_scores, negative_scores, positive_tool, hard_valid
    )
    query_pull = jnp.dot(shard_gradients, tool_unit, preferred_element_type=jnp.float32)
    query_pull = query_pull + jnp.einsum(
        "qk,qkd->qd", negative_gradients, hard_units, preferred_element_type=jnp.float32
    )
    tool_pull = lax.dot_general(
        shard_gradients, query_unit, (((0,), (0,)), ((), ())), preferred_element_type=jnp.float32
    )
    slot_queries = jnp.repeat(query_unit, per_query, axis=0)
    returned = negative_gradients.reshape(-1)[:, None].astype(jnp.float32) * slot_queries.astype(
        jnp.float32
    )
    outgoing = (
        jnp.zeros((group_size * capacity, features), jnp.float32)
        .at[target]
        .set(returned, mode="drop")
    )
    arrived = lax.all_to_all(
        outgoing.reshape(group_size, capacity, features).astype(jnp.bfloat16),
        "dp",
        split_axis=0,
        concat_axis=0,
        tiled=True,
    ).astype(jnp.float32)
    tool_pull = tool_pull.at[indices.reshape(-1)].add(arrived.reshape(-1, features))
    query_inner, tool_inner = lax.psum(
        (jnp.sum(query_unit32 * query_pull, axis=1), jnp.sum(tool_unit32 * tool_pull, axis=1)),
        "section",
    )
    query_back = (query_pull - query_unit32 * query_inner[:, None]) / query_norm[:, None]
    tool_back = (tool_pull - tool_unit32 * tool_inner[:, None]) / tool_norm[:, None]
    query_grad = (query_back * norm_gain).astype(jnp.bfloat16)
    tool_grad = (tool_back * norm_gain).astype(jnp.bfloat16)
    gain_terms = jnp.sum(query_back * query_hidden.astype(jnp.float32), axis=0) + jnp.sum(
        tool_back * tool_hidden.astype(jnp.float32), axis=0
    )
    gain_grad = lax.psum(gain_terms, "dp")
    return (query_grad, tool_grad, gain_grad)


def solution(mesh):
    return jax.shard_map(
        body,
        mesh=mesh,
        in_specs=(
            P("dp", "section"),
            P("dp", "section"),
            P("section"),
            P("dp"),
            P("dp", None),
            P("dp", None),
            P("dp", None),
        ),
        out_specs=(P("dp", "section"), P("dp", "section"), P("section")),
        check_vma=False,
    )
```

profile of v0, /device:TPU:1, one launch (start us, length us, event | category | flops | bytes accessed | tf_op | source)
XLA Modules:
  0.0 498.0 jit_solution(5765499487373668806)
XLA Ops:
  8.4 0.8 copy.22
  9.8 0.8 broadcast_multiply_fusion
  10.7 18.0 %reduce-window.6 = s32[64,8,128]{2,1,0:T(8,128)S(1)} reduce-window(s32[64,8,128]{2,1,0:T(8,128)S(1)} %fusion.28, s32[]{:T(128)} %constant.12.clone.1), window={size=1x1x128 pad=0_0x0_0x127_0}, to_apply=%region_7.8 | reduce-window | flops 8323072 | bytes 524292 | tf_op jit(solution)/shard_map/reduce-window
  30.0 4.3 scatter_custom_fusion
  35.0 13.1 %all-to-all-start = ((s32[64,1,32]{2,1,0:T(1,128)}), s32[64,1,32]{2,1,0:T(1,128)S(1)}, u32[]{:S(2)}, u32[]{:S(2)}) async-start(s32[64,1,32]{2,1,0:T(1,128)} %bitcast.5), calls=%async_computation | async-start | bytes 65536 | tf_op jit(solution)/shard_map/all_to_all | solution.py:63
  48.8 9.0 %all-reduce.1 = (f32[512]{0:T(512)S(1)}, f32[512]{0:T(512)S(1)}) all-reduce(f32[512]{0:T(512)S(1)} %get-tuple-element.8, f32[512]{0:T(512)S(1)} %get-tuple-element.7), channel_id=1, replica_groups=mesh['dp'=64,'section'=4] {'section'}, use_global_device_ids=true, to_apply=%region_3.0 | all-reduce | flops 1024 | bytes 8192 | tf_op jit(solution)/shard_map/psum | solution.py:38
  57.8 1.8 fusion.33
  59.7 9.7 %gather_fusion = bf16[2048,1024]{1,0:T(8,128)(2,1)} fusion(bf16[512,1024]{1,0:T(8,128)(2,1)S(1)} %get-tuple-element.23, s32[2048]{0:T(1024)S(1)} %broadcast_clamp_fusion), kind=kCustom, calls=%fused_computation | custom fusion | bytes 8396800 | tf_op jit(solution)/shard_map/gather | solution.py:64
  69.4 12.0 %all-to-all-start.1 = ((bf16[64,32,1024]{2,1,0:T(8,128)(2,1)}), bf16[64,32,1024]{2,1,0:T(8,128)(2,1)}, u32[]{:S(2)}, u32[]{:S(2)}) async-start(bf16[64,32,1024]{2,1,0:T(8,128)(2,1)} %bitcast.46), calls=%async_computation.1 | async-start | bytes 8388608 | tf_op jit(solution)/shard_map/all_to_all | solution.py:65
  81.6 2.8 convolution_convert_fusion
  84.4 4.3 broadcast_in_dim.32
  88.7 6.0 %convert_element_type.86 = f32[1024,1024]{1,0:T(8,128)} reshape(f32[512,2,1024]{2,1,0:T(2,128)} %broadcast_in_dim.32) | data formatting | bytes 8388608 | tf_op jit(solution)/shard_map/convert_element_type | solution.py:89
  94.7 35.9 %all-reduce.4.cloned.1.call-done = bf16[512,512]{1,0:T(8,128)(2,1)} async-done(((bf16[512,512]{1,0:T(8,128)(2,1)}), bf16[512,512]{1,0:T(8,128)(2,1)}) %all-reduce.4.cloned.1.call-update) | async-done | bytes 524304 | tf_op jit(solution)/shard_map/psum | solution.py:75
  130.7 1.5 fusion.18
  132.2 43.9 %all-to-all-done.1 = bf16[64,32,1024]{2,1,0:T(8,128)(2,1)} async-done(((bf16[64,32,1024]{2,1,0:T(8,128)(2,1)}), bf16[64,32,1024]{2,1,0:T(8,128)(2,1)}, u32[]{:S(2)}, u32[]{:S(2)}) %all-to-all-start.1) | async-done | bytes 4194336 | tf_op jit(solution)/shard_map/all_to_all | solution.py:65
  176.1 8.8 %gather_fusion.1 = bf16[1024,1024]{1,0:T(8,128)(2,1)} fusion(bf16[2048,1024]{1,0:T(8,128)(2,1)} %bitcast.8, s32[1024]{0:T(1024)S(1)} %broadcast_clamp_fusion.1), kind=kCustom, calls=%fused_computation.1 | custom fusion | bytes 4198400 | tf_op jit(solution)/shard_map/gather | solution.py:67
  184.9 4.1 reshape.222
  189.0 6.3 %fusion.14 = bf16[512,1,2]{2,1,0:T(2,128)(2,1)S(1)} fusion(bf16[512,2,1024]{2,1,0:T(2,128)(2,1)} %reshape.222, bf16[512,1024,1]{1,0,2:T(8,128)(2,1)} %bitcast.47), kind=kOutput, calls=%fused_computation.30 | convolution fusion | flops 2097152 | bytes 3147776 | tf_op jit(solution)/shard_map/qd,qkd->qk/dot_general | solution.py:73
  195.5 6.0 %psum.52 = bf16[512,2]{0,1:T(2,128)(2,1)S(1)} all-reduce(bf16[512,2]{0,1:T(2,128)(2,1)S(1)} %bitcast.54), channel_id=1, replica_groups=mesh['dp'=64,'section'=4] {'section'}, use_global_device_ids=true, to_apply=%region_11.12 | all-reduce | flops 1024 | bytes 4096 | tf_op jit(solution)/shard_map/psum | solution.py:76
  201.9 10.1 %scatter_custom_fusion.1 = f32[2048,1024]{1,0:T(8,128)} fusion(s32[1024]{0:T(1024)S(1)} %bitcast.57, f32[1024,1024]{1,0:T(8,128)} %convert_element_type.86, f32[]{:T(128)} %constant.9.clone.1, f32[1024]{0:T(1024)S(1)} %reshape.226), kind=kCustom, calls=%fused_computation.7 | custom fusion | flops 1048576 | bytes 12587012 | tf_op jit(solution)/shard_map/scatter | solution.py:95
  212.0 6.0 %convert_element_type.87 = bf16[2048,1024]{1,0:T(8,128)(2,1)} convert(f32[2048,1024]{1,0:T(8,128)} %scatter_custom_fusion.1) | non-fusion elementwise | flops 2097152 | bytes 12582912 | tf_op jit(solution)/shard_map/convert_element_type | solution.py:98
  218.0 8.8 %all-to-all-start.2 = ((bf16[64,32,1024]{2,1,0:T(8,128)(2,1)}), bf16[64,32,1024]{2,1,0:T(8,128)(2,1)}, u32[]{:S(2)}, u32[]{:S(2)}) async-start(bf16[64,32,1024]{2,1,0:T(8,128)(2,1)} %bitcast.45), calls=%async_computation.2 | async-start | bytes 8388608 | tf_op jit(solution)/shard_map/all_to_all | solution.py:97
  228.4 3.8 fusion.34
  232.2 3.7 fusion.37
  235.9 85.9 %all-to-all-done.2 = bf16[64,32,1024]{2,1,0:T(8,128)(2,1)} async-done(((bf16[64,32,1024]{2,1,0:T(8,128)(2,1)}), bf16[64,32,1024]{2,1,0:T(8,128)(2,1)}, u32[]{:S(2)}, u32[]{:S(2)}) %all-to-all-start.2) | async-done | bytes 4194336 | tf_op jit(solution)/shard_map/all_to_all | solution.py:97
  321.7 21.0 %scatter_custom_fusion.2 = f32[512,1024]{1,0:T(8,128)} fusion(f32[512,1024]{1,0:T(8,128)} %fusion.34, s32[2048]{0:T(1024)S(1)} %bitcast.55, bf16[2048,1024]{1,0:T(8,128)(2,1)} %bitcast.16), kind=kCustom, calls=%fused_computation.5 | custom fusion | flops 4194304 | bytes 6291456 | tf_op jit(solution)/shard_map/scatter-add | solution.py:104
  342.7 5.2 %multiply_reduce_fusion = (f32[512]{0:T(512)S(1)}, f32[512]{0:T(512)S(1)}, f32[512,1024]{1,0:T(8,128)}) fusion(f32[512,1024]{1,0:T(8,128)} %scatter_custom_fusion.2, f32[512]{0:T(512)S(1)} %get-tuple-element.25, f32[1024]{0:T(1024)S(1)} %copy-done.4, bf16[512,1024]{1,0:T(8,128)(2,1)S(1)} %copy-done.1, f32[512]{0:T(512)S(1)} %get-tuple-element.26, ...), kind=kOutput, calls=%fused_computation.25 | convolution fusion | flops 544734208 | bytes 9979904 | tf_op jit(solution)/shard_map/dot_general | solution.py:81
  347.9 7.7 %all-reduce = (f32[512]{0:T(512)S(1)}, f32[512]{0:T(512)S(1)}) all-reduce(f32[512]{0:T(512)S(1)} %get-tuple-element.6, f32[512]{0:T(512)S(1)} %get-tuple-element.5), channel_id=1, replica_groups=mesh['dp'=64,'section'=4] {'section'}, use_global_device_ids=true, to_apply=%region_14.15 | all-reduce | flops 1024 | bytes 8192 | tf_op jit(solution)/shard_map/psum | solution.py:105
  355.6 2.4 fusion.12
  358.0 2.3 fusion.11
  360.4 128.0 %psum.55 = f32[1024]{0:T(1024)} all-reduce(f32[1024]{0:T(1024)S(1)} %add.119), channel_id=1, replica_groups=mesh['dp'=64,'section'=4] {'dp'}, use_global_device_ids=true, to_apply=%region_21.22 | all-reduce | flops 1024 | bytes 8192 | tf_op jit(solution)/shard_map/psum | solution.py:116
  488.3 2.8 multiply_convert_fusion.1
  (58 shorter events, 6.8 us)
Async XLA Ops:
  7.2 22.4 %copy-start.6 = (s32[512,2]{0,1:T(2,128)S(1)}, s32[512,2]{0,1:T(2,128)}, u32[]{:S(2)}) copy-start(s32[512,2]{0,1:T(2,128)} %param.12) | copy-start | bytes 12292
  9.3 38.9 %copy-start = (bf16[512,1024]{1,0:T(8,128)(2,1)S(1)}, bf16[512,1024]{1,0:T(8,128)(2,1)}, u32[]{:S(2)}) copy-start(bf16[512,1024]{1,0:T(8,128)(2,1)} %param.7) | copy-start | bytes 3145732
  9.3 38.9 %copy-start.1 = (bf16[512,1024]{1,0:T(8,128)(2,1)S(1)}, bf16[512,1024]{1,0:T(8,128)(2,1)}, u32[]{:S(2)}) copy-start(bf16[512,1024]{1,0:T(8,128)(2,1)} %param.8) | copy-start | bytes 3145732
  9.3 38.9 %copy-start.4 = (f32[1024]{0:T(1024)S(1)}, f32[1024]{0:T(1024)}, u32[]{:S(2)}) copy-start(f32[1024]{0:T(1024)} %param.9) | copy-start | bytes 12292
  35.0 24.6 %all-to-all-start = ((s32[64,1,32]{2,1,0:T(1,128)}), s32[64,1,32]{2,1,0:T(1,128)S(1)}, u32[]{:S(2)}, u32[]{:S(2)}) async-start(s32[64,1,32]{2,1,0:T(1,128)} %bitcast.5), calls=%async_computation | async-start | bytes 65536 | tf_op jit(solution)/shard_map/all_to_all | solution.py:63
  69.4 106.7 %all-to-all-start.1 = ((bf16[64,32,1024]{2,1,0:T(8,128)(2,1)}), bf16[64,32,1024]{2,1,0:T(8,128)(2,1)}, u32[]{:S(2)}, u32[]{:S(2)}) async-start(bf16[64,32,1024]{2,1,0:T(8,128)(2,1)} %bitcast.46), calls=%async_computation.1 | async-start | bytes 8388608 | tf_op jit(solution)/shard_map/all_to_all | solution.py:65
  81.4 49.3 %all-reduce.4.cloned.1.call-start = ((), (), s32[]{:S(2)}) async-start(), calls=%async_computation.3 | async-start | bytes 1048576 | tf_op jit(solution)/shard_map/psum | solution.py:75
  88.7 42.0 %copy-start.7 = (s32[512]{0:T(512)S(1)}, s32[512]{0:T(512)}, u32[]{:S(2)}) copy-start(s32[512]{0:T(512)} %param.10) | copy-start | bytes 6148
  189.0 12.5 %copy-start.5 = (s32[512,2]{0,1:T(2,128)S(1)}, s32[512,2]{0,1:T(2,128)}, u32[]{:S(2)}) copy-start(s32[512,2]{0,1:T(2,128)} %param.13) | copy-start | bytes 12292
  218.0 103.7 %all-to-all-start.2 = ((bf16[64,32,1024]{2,1,0:T(8,128)(2,1)}), bf16[64,32,1024]{2,1,0:T(8,128)(2,1)}, u32[]{:S(2)}, u32[]{:S(2)}) async-start(bf16[64,32,1024]{2,1,0:T(8,128)(2,1)} %bitcast.45), calls=%async_computation.2 | async-start | bytes 8388608 | tf_op jit(solution)/shard_map/all_to_all | solution.py:97
  228.4 3.8 copy-start.3
  355.6 2.4 copy-start.2
Sparse Core Ops, SparseCore 0:
  85.1 45.5 all-reduce.3
where the time goes:
time: 499 us; the launch traced here: 498 us
  waiting for transfers between devices  166 us (33%)
  blocking collectives  151 us (30%)
  other arithmetic  69.2 us (14%)
  local copies, waits for them, and re-layouts  42.2 us (8%)
  starting transfers between devices  34.2 us (7%)
  matrix products  21.8 us (4%)
  between operations  14.3 us (3%)
    psum x1, blocking collectives, body(): gain_grad = lax.psum(gain_terms, 'dp')  128 us
    all_to_all x1, waiting for transfers between devices, body(): lax.all_to_all(outgoing.reshape(group_size, capacity, features).astype(jn...  85.9 us
    all_to_all x1, waiting for transfers between devices, body(): lax.all_to_all(answers, 'dp', split_axis=0, concat_axis=0, tiled=True)  43.9 us
    psum x1, waiting for transfers between devices, body(): lax.psum(local_part.astype(jnp.bfloat16), 'section').astype(jnp.float32)  35.9 us
    scatter-add x1, other arithmetic, body(): tool_pull.at[indices.reshape(-1)].add(arrived.reshape(-1, features))  21 us
    another operation x3, other arithmetic  18.2 us
    all_to_all x1, starting transfers between devices, body(): lax.all_to_all(requests, 'dp', split_axis=0, concat_axis=0, tiled=True)  13.1 us
    all_to_all x1, starting transfers between devices, body(): lax.all_to_all(answers, 'dp', split_axis=0, concat_axis=0, tiled=True)  12 us
  transfers between devices with their start and end apart: 4, of which 3 were waited for; matrix products, arithmetic and copies ran while one was open for 5% of the time, Pallas kernels for 0%

commit v1 on v0

v1 whole, which is shorter than its diff:
```python
import jax
import jax.numpy as jnp
import numpy as np
from jax import lax
from jax.sharding import Mesh
from jax.sharding import PartitionSpec as P

EPSILON = 1e-06
SOFTMAX_TEMP = 0.05
DP = ("dz", "dy", "dc")


def softmax_grads(shard_scores, negative_scores, positive, valid_mask):
    selected_rows = lax.broadcasted_iota(jnp.int32, shard_scores.shape, 1) == positive[:, None]
    softmax_weights = jnp.exp(shard_scores / SOFTMAX_TEMP)
    shard_probabilities = softmax_weights / jnp.sum(softmax_weights, axis=1, keepdims=True)
    positive_score = jnp.sum(jnp.where(selected_rows, shard_scores, 0.0), axis=1)
    positive_weight = jnp.exp(positive_score / SOFTMAX_TEMP)
    negative_weights = jnp.where(valid_mask > 0, jnp.exp(negative_scores / SOFTMAX_TEMP), 0.0)
    negative_weight_sum = positive_weight + jnp.sum(negative_weights, axis=1)
    shard_gradients = (
        (
            shard_probabilities
            + jnp.where(selected_rows, (positive_weight / negative_weight_sum - 2.0)[:, None], 0.0)
        )
        / SOFTMAX_TEMP
    ).astype(jnp.bfloat16)
    negative_gradients = (negative_weights / (negative_weight_sum[:, None] * SOFTMAX_TEMP)).astype(
        jnp.bfloat16
    )
    return (shard_gradients, negative_gradients)


def body(query_hidden, tool_hidden, norm_gain, positive_tool, hard_owner, hard_row, hard_valid):
    query_count, features = query_hidden.shape
    tool_count = tool_hidden.shape[0]
    per_query = hard_owner.shape[1]
    slots = query_count * per_query
    group_size = lax.axis_size(DP)
    capacity = max(2, 2 * query_count * per_query // group_size)
    places = group_size * capacity

    owners = hard_owner.reshape(-1)
    wanted_rows = hard_row.reshape(-1)
    usable = hard_valid.reshape(-1) > 0
    slot_ids = jnp.arange(slots, dtype=jnp.int32)
    same_earlier = (
        (owners[:, None] == owners[None, :]) & usable[None, :] & (slot_ids[None, :] < slot_ids[:, None])
    )
    slot_place = jnp.sum(same_earlier.astype(jnp.int32), axis=1)
    target = jnp.where(usable, owners * capacity + slot_place, places)
    place_ids = jnp.arange(places, dtype=jnp.int32)
    slot_at = target[:, None] == place_ids[None, :]
    requests = jnp.sum(jnp.where(slot_at, wanted_rows[:, None], 0), axis=0).reshape(group_size, capacity)
    indices = lax.all_to_all(requests, DP, 0, 0, tiled=True).reshape(-1)

    query_scaled = query_hidden.astype(jnp.float32) * norm_gain
    tool_scaled = tool_hidden.astype(jnp.float32) * norm_gain
    query_squares, tool_squares = lax.psum(
        (jnp.sum(query_scaled * query_scaled, axis=1), jnp.sum(tool_scaled * tool_scaled, axis=1)),
        "section",
    )
    query_norm = jnp.sqrt(query_squares + EPSILON)
    tool_norm = jnp.sqrt(tool_squares + EPSILON)
    query_unit32 = query_scaled / query_norm[:, None]
    tool_unit32 = tool_scaled / tool_norm[:, None]
    query_unit = query_unit32.astype(jnp.bfloat16)
    tool_unit = tool_unit32.astype(jnp.bfloat16)

    pick_tool = (indices[:, None] == jnp.arange(tool_count, dtype=jnp.int32)[None, :]).astype(jnp.bfloat16)
    answers = jnp.dot(pick_tool, tool_unit, preferred_element_type=jnp.float32).astype(jnp.bfloat16)
    slot_of_query = slot_at.reshape(query_count, per_query, places).any(axis=1)
    pick_query = slot_of_query.T.astype(jnp.bfloat16)
    sent_queries = jnp.dot(pick_query, query_unit, preferred_element_type=jnp.float32).astype(jnp.bfloat16)
    payload = jnp.concatenate(
        [answers.reshape(group_size, capacity, features), sent_queries.reshape(group_size, capacity, features)],
        axis=1,
    )
    received = lax.all_to_all(payload, DP, 0, 0, tiled=True)
    back = received[:, :capacity].reshape(places, features)
    arrived = received[:, capacity:].reshape(places, features)

    local_part = lax.dot_general(
        query_unit, tool_unit, (((1,), (1,)), ((), ())), preferred_element_type=jnp.float32
    )
    hard_units = jnp.dot(slot_at.astype(jnp.bfloat16), back, preferred_element_type=jnp.float32).reshape(
        query_count, per_query, features
    )
    hard_part = jnp.einsum(
        "qd,qkd->qk", query_unit.astype(jnp.float32), hard_units, preferred_element_type=jnp.float32
    )
    shard_scores, negative_scores = (
        lax.psum(local_part.astype(jnp.bfloat16), "section").astype(jnp.float32),
        lax.psum(hard_part.astype(jnp.bfloat16), "section").astype(jnp.float32),
    )
    shard_gradients, negative_gradients = softmax_grads(
        shard_scores, negative_scores, positive_tool, hard_valid
    )
    query_pull = jnp.dot(shard_gradients, tool_unit, preferred_element_type=jnp.float32)
    query_pull = query_pull + jnp.einsum(
        "qk,qkd->qd", negative_gradients.astype(jnp.float32), hard_units, preferred_element_type=jnp.float32
    )

    sent_grads = jnp.sum(
        jnp.where(slot_at, negative_gradients.reshape(-1)[:, None].astype(jnp.float32), 0.0), axis=0
    ).astype(jnp.bfloat16)
    arrived_grads = lax.all_to_all(sent_grads.reshape(group_size, capacity), DP, 0, 0, tiled=True).reshape(-1)
    weights = jnp.where(
        jnp.arange(tool_count, dtype=jnp.int32)[:, None] == indices[None, :], arrived_grads[None, :], 0.0
    ).astype(jnp.bfloat16)
    tool_pull = lax.dot_general(
        shard_gradients, query_unit, (((0,), (0,)), ((), ())), preferred_element_type=jnp.float32
    )
    tool_pull = tool_pull + jnp.dot(weights, arrived, preferred_element_type=jnp.float32)

    query_inner, tool_inner = lax.psum(
        (jnp.sum(query_unit32 * query_pull, axis=1), jnp.sum(tool_unit32 * tool_pull, axis=1)),
        "section",
    )
    query_back = (query_pull - query_unit32 * query_inner[:, None]) / query_norm[:, None]
    tool_back = (tool_pull - tool_unit32 * tool_inner[:, None]) / tool_norm[:, None]
    query_grad = (query_back * norm_gain).astype(jnp.bfloat16)
    tool_grad = (tool_back * norm_gain).astype(jnp.bfloat16)
    gain_terms = jnp.sum(query_back * query_hidden.astype(jnp.float32), axis=0) + jnp.sum(
        tool_back * tool_hidden.astype(jnp.float32), axis=0
    )
    gain_grad = lax.psum(lax.psum(lax.psum(gain_terms, "dc"), "dy"), "dz")
    return (query_grad, tool_grad, gain_grad)


def split_dp(mesh):
    dp = mesh.shape["dp"]
    cores = 2 if dp % 2 == 0 else 1
    rest = dp // cores
    ys = 4 if rest % 4 == 0 else 1
    devices = np.asarray(mesh.devices).reshape(rest // ys, ys, cores, mesh.shape["section"])
    return Mesh(devices, DP + ("section",))


def solution(mesh):
    fine = split_dp(mesh)
    return jax.shard_map(
        body,
        mesh=fine,
        in_specs=(
            P(DP, "section"),
            P(DP, "section"),
            P("section"),
            P(DP),
            P(DP, None),
            P(DP, None),
            P(DP, None),
        ),
        out_specs=(P(DP, "section"), P(DP, "section"), P("section")),
        check_vma=False,
    )
```

time: 499 us -> 357 us (0.72)
  blocking collectives: 151 us -> 47 us
  other arithmetic: 69.2 us -> 23.3 us
  local copies, waits for them, and re-layouts: 42.2 us -> 12.2 us
  matrix products: 21.8 us -> 38.2 us
  waiting for transfers between devices: 166 us -> 181 us
    psum x1 -> x3, blocking collectives: 128 us -> 24.5 us  [body(): gain_grad = lax.psum(lax.psum(lax.psum(gain_terms, 'dc'), 'dy'), 'dz')]
    dot_general x2 -> x6, matrix products: 9.99 us -> 31.1 us  [the longest x1 8.83 us: body(): jnp.einsum('qd,qkd->qk', query_unit.astype(jnp.float32), hard_units, pref...]
    scatter-add x1 -> x0, other arithmetic: 21 us -> none  [body(): tool_pull.at[indices.reshape(-1)].add(arrived.reshape(-1, features))]
    gather x2 -> x0, local copies, waits for them, and re-layouts: 18.4 us -> none  [the longest x1 9.65 us: body(): answers = tool_unit[indices]]
    another operation x3 -> x0, other arithmetic: 18.2 us -> none
    psum x1, waiting for transfers between devices: 35.9 us -> 47.1 us  [body(): lax.psum(local_part.astype(jnp.bfloat16), 'section').astype(jnp.float32)]
    scatter x1 -> x0, other arithmetic: 10.1 us -> none  [body(): outgoing = jnp.zeros((group_size * capacity, features), jnp.float32).at[t...]
    concatenate x0 -> x1, other arithmetic: none -> 8.49 us  [body(): jnp.concatenate([answers.reshape(group_size, capacity, features), sent_qu...]
where the time goes in v1:
time: 357 us; the launch traced here: 354 us
  waiting for transfers between devices  181 us (51%)
  blocking collectives  47 us (13%)
  matrix products  38.2 us (11%)
  starting transfers between devices  37.4 us (10%)
  other arithmetic  23.3 us (7%)
  between operations  14.3 us (4%)
  local copies, waits for them, and re-layouts  12.2 us (3%)
    all_to_all x1, waiting for transfers between devices, body(): received = lax.all_to_all(payload, DP, 0, 0, tiled=True)  132 us
    psum x1, waiting for transfers between devices, body(): lax.psum(local_part.astype(jnp.bfloat16), 'section').astype(jnp.float32)  47.1 us
    psum x3, blocking collectives, body(): gain_grad = lax.psum(lax.psum(lax.psum(gain_terms, 'dc'), 'dy'), 'dz')  24.5 us
    all_to_all x1, starting transfers between devices, body(): indices = lax.all_to_all(requests, DP, 0, 0, tiled=True).reshape(-1)  13.1 us
    all_to_all x1, starting transfers between devices, body(): received = lax.all_to_all(payload, DP, 0, 0, tiled=True)  12.2 us
    all_to_all x1, starting transfers between devices, body(): lax.all_to_all(sent_grads.reshape(group_size, capacity), DP, 0, 0, tiled=...  11.8 us
    dot_general x1, matrix products, body(): jnp.einsum('qd,qkd->qk', query_unit.astype(jnp.float32), hard_units, pref...  8.83 us
    psum x1, blocking collectives, body(): lax.psum((jnp.sum(query_scaled * query_scaled, axis=1), jnp.sum(tool_scal...  8.77 us
  transfers between devices with their start and end apart: 4, of which 3 were waited for; matrix products, arithmetic and copies ran while one was open for 5% of the time, Pallas kernels for 0%

profile of v1, /device:TPU:1, one launch (start us, length us, event | category | flops | bytes accessed | tf_op | source)
XLA Modules:
  0.0 353.5 jit_solution(10480050438670012715)
XLA Ops:
  11.0 1.1 select_reduce_fusion.1
  12.8 13.1 %all-to-all-start = ((s32[64,1,32]{2,1,0:T(1,128)}), s32[64,1,32]{2,1,0:T(1,128)S(1)}, u32[]{:S(2)}, u32[]{:S(2)}) async-start(s32[64,1,32]{2,1,0:T(1,128)} %bitcast.2), calls=%async_computation | async-start | bytes 65536 | tf_op jit(solution)/shard_map/all_to_all | solution.py:55
  26.2 1.8 fusion.17
  28.0 8.8 %all-reduce.1 = (f32[512]{0:T(512)S(1)}, f32[512]{0:T(512)S(1)}) all-reduce(f32[512]{0:T(512)S(1)} %get-tuple-element.8, f32[512]{0:T(512)S(1)} %get-tuple-element.7), channel_id=1, replica_groups=mesh['dz'=8,'dy'=4,'dc'=2,'section'=4] {'section'}, use_global_device_ids=true, to_apply=%region_1.2 | all-reduce | flops 1024 | bytes 8192 | tf_op jit(solution)/shard_map/psum | solution.py:59
  37.0 1.1 fusion.3
  38.1 4.5 %convolution_convert_fusion = bf16[2048,1024]{1,0:T(8,128)(2,1)} fusion(pred[512,2048]{1,0:T(8,128)(4,1)S(1)} %fusion.3, f32[512]{0:T(512)S(1)} %add_sqrt_fusion.1, f32[1024]{0:T(1024)S(1)} %copy-done.5, bf16[512,1024]{1,0:T(8,128)(2,1)S(1)} %copy-done), kind=kOutput, calls=%fused_computation.18 | convolution fusion | flops 2151677952 | bytes 6297600 | tf_op jit(solution)/shard_map/dot_general | solution.py:74
  43.9 4.2 %fusion.8 = bf16[2048,1024]{1,0:T(8,128)(2,1)} fusion(s32[2048]{0:T(1024)S(1)} %eq.106, bf16[512,1024]{1,0:T(8,128)(2,1)S(1)} %copy-done.1, f32[512]{0:T(512)S(1)} %add_sqrt_fusion, f32[1024]{0:T(1024)S(1)} %copy-done.5), kind=kOutput, calls=%fused_computation.17 | convolution fusion | flops 2152726528 | bytes 5257216 | tf_op jit(solution)/shard_map/dot_general | solution.py:71
  48.1 8.5 %pad_maximum_fusion = bf16[64,64,1024]{2,1,0:T(8,128)(2,1)} fusion(bf16[64,32,1024]{2,1,0:T(8,128)(2,1)} %bitcast.23, bf16[64,32,1024]{2,1,0:T(8,128)(2,1)} %bitcast.25), kind=kLoop, calls=%fused_computation | loop fusion | flops 16777216 | bytes 16777216 | tf_op jit(solution)/shard_map/concatenate | solution.py:75
  56.6 12.2 %all-to-all-start.1 = ((bf16[64,64,1024]{2,1,0:T(8,128)(2,1)}), bf16[64,64,1024]{2,1,0:T(8,128)(2,1)}, u32[]{:S(2)}, u32[]{:S(2)}) async-start(bf16[64,64,1024]{2,1,0:T(8,128)(2,1)} %pad_maximum_fusion), calls=%async_computation.1 | async-start | bytes 16777216 | tf_op jit(solution)/shard_map/all_to_all | solution.py:79
  69.1 1.6 convolution_convert_fusion.1
  71.0 47.1 %all-reduce.4.cloned.1.call-done = bf16[512,512]{1,0:T(8,128)(2,1)} async-done(((bf16[512,512]{1,0:T(8,128)(2,1)}), bf16[512,512]{1,0:T(8,128)(2,1)}) %all-reduce.4.cloned.1.call-update) | async-done | bytes 524304 | tf_op jit(solution)/shard_map/psum | solution.py:93
  118.1 1.5 fusion.28
  119.6 131.5 %all-to-all-done.1 = bf16[64,64,1024]{2,1,0:T(8,128)(2,1)} async-done(((bf16[64,64,1024]{2,1,0:T(8,128)(2,1)}), bf16[64,64,1024]{2,1,0:T(8,128)(2,1)}, u32[]{:S(2)}, u32[]{:S(2)}) %all-to-all-start.1) | async-done | bytes 8388640 | tf_op jit(solution)/shard_map/all_to_all | solution.py:79
  251.1 5.4 %fusion.50 = (bf16[64,32,1024]{2,1,0:T(8,128)(2,1)}, bf16[64,32,1024]{2,1,0:T(8,128)(2,1)S(1)}) fusion(bf16[64,64,1024]{2,1,0:T(8,128)(2,1)} %all-to-all-done.1), kind=kLoop, calls=%fused_computation.78 | loop fusion | bytes 16777216 | tf_op jit(solution)/shard_map/slice | solution.py:81
  256.5 4.8 %fusion.1 = bf16[512,2,1024]{2,0,1:T(8,128)(2,1)S(1)} fusion(bf16[2048,1024,1]{1,0,2:T(8,128)(2,1)S(1)} %bitcast.24, s32[512,2]{0,1:T(2,128)S(1)} %add_select_fusion.1), kind=kOutput, calls=%fused_computation.7 | convolution fusion | flops 4297064448 | bytes 6295552 | tf_op jit(solution)/shard_map/dot_general | solution.py:86
  261.4 1.3 copy-done.9
  262.7 8.8 %fusion.11 = bf16[512,1,2]{2,1,0:T(2,128)(2,1)S(1)} fusion(bf16[512,2,1024]{2,0,1:T(8,128)(2,1)S(1)} %fusion.1, bf16[512,1024,1]{1,0,2:T(8,128)(2,1)S(1)} %fusion.47), kind=kOutput, calls=%fused_computation.21 | convolution fusion | flops 2097152 | bytes 3147776 | tf_op jit(solution)/shard_map/qd,qkd->qk/dot_general | solution.py:89
  271.6 6.0 %psum.66 = bf16[512,2]{0,1:T(2,128)(2,1)S(1)} all-reduce(bf16[512,2]{0,1:T(2,128)(2,1)S(1)} %bitcast.27), channel_id=1, replica_groups=mesh['dz'=8,'dy'=4,'dc'=2,'section'=4] {'section'}, use_global_device_ids=true, to_apply=%region_10.11 | all-reduce | flops 1024 | bytes 4096 | tf_op jit(solution)/shard_map/psum | solution.py:94
  278.0 1.2 select_reduce_fusion
  280.0 11.8 %all-to-all-start.2 = ((bf16[64,1,32]{2,1,0:T(2,128)(2,1)}), bf16[64,1,32]{2,1,0:T(2,128)(2,1)S(1)}, u32[]{:S(2)}, u32[]{:S(2)}) async-start(bf16[64,1,32]{2,1,0:T(2,128)(2,1)} %convert_element_type.99), calls=%async_computation.2 | async-start | bytes 65536 | tf_op jit(solution)/shard_map/all_to_all | solution.py:107
  292.0 4.1 %fusion.9 = f32[512,1,1024]{2,1,0:T(1,128)S(1)} fusion(bf16[512,2,1]{1,2,0:T(2,128)(2,1)S(1)} %copy.44, bf16[512,2,1024]{2,0,1:T(8,128)(2,1)} %copy-done.9), kind=kOutput, calls=%fused_computation.19 | convolution fusion | flops 2097152 | bytes 4196352 | tf_op jit(solution)/shard_map/qk,qkd->qd/dot_general | solution.py:100
  296.1 2.5 bitcast_add_fusion
  298.6 2.5 all-to-all-done.2
  301.3 4.7 %fusion.21 = f32[512,1024]{1,0:T(8,128)S(1)} fusion(bf16[2048,1024]{1,0:T(8,128)(2,1)} %bitcast.22, s32[2048]{0:T(1024)S(1)} %eq.106, bf16[2048]{0:T(1024)(128)(2,1)S(1)} %broadcast_in_dim.95), kind=kOutput, calls=%fused_computation.35 | convolution fusion | flops 2149580800 | bytes 6303744 | tf_op jit(solution)/shard_map/dot_general | solution.py:114
  306.0 2.9 multiply_reduce_fusion
  308.9 7.7 %all-reduce = (f32[512]{0:T(512)S(1)}, f32[512]{0:T(512)S(1)}) all-reduce(f32[512]{0:T(512)S(1)} %get-tuple-element.6, f32[512]{0:T(512)S(1)} %get-tuple-element.5), channel_id=1, replica_groups=mesh['dz'=8,'dy'=4,'dc'=2,'section'=4] {'section'}, use_global_device_ids=true, to_apply=%region_13.14 | all-reduce | flops 1024 | bytes 8192 | tf_op jit(solution)/shard_map/psum | solution.py:116
  316.7 2.4 fusion.20
  319.1 1.9 fusion.19
  320.9 4.8 %psum.69 = f32[1024]{0:T(1024)S(1)} all-reduce(f32[1024]{0:T(1024)S(1)} %add.69), channel_id=1, replica_groups=mesh['dz'=8,'dy'=4,'dc'=2,'section'=4] {'dc'}, use_global_device_ids=true, to_apply=%region_19.20 | all-reduce | flops 1024 | bytes 8192 | tf_op jit(solution)/shard_map/psum | solution.py:127
  325.7 6.7 %psum.70 = f32[1024]{0:T(1024)S(1)} all-reduce(f32[1024]{0:T(1024)S(1)} %psum.69), channel_id=1, replica_groups=mesh['dz'=8,'dy'=4,'dc'=2,'section'=4] {'dy'}, use_global_device_ids=true, to_apply=%region_20.21 | all-reduce | flops 1024 | bytes 8192 | tf_op jit(solution)/shard_map/psum | solution.py:127
  332.5 13.0 %psum.71 = f32[1024]{0:T(1024)} all-reduce(f32[1024]{0:T(1024)S(1)} %psum.70), channel_id=1, replica_groups=mesh['dz'=8,'dy'=4,'dc'=2,'section'=4] {'dz'}, use_global_device_ids=true, to_apply=%region_21.22 | all-reduce | flops 1024 | bytes 8192 | tf_op jit(solution)/shard_map/psum | solution.py:127
  345.4 1.2 multiply_convert_fusion.1
  (52 shorter events, 8.3 us)
Async XLA Ops:
  7.2 29.8 %copy-start.7 = (s32[512,2]{0,1:T(2,128)S(1)}, s32[512,2]{0,1:T(2,128)}, u32[]{:S(2)}) copy-start(s32[512,2]{0,1:T(2,128)} %param.11) | copy-start | bytes 12292
  7.2 29.8 %copy-start.6 = (s32[512,2]{0,1:T(2,128)S(1)}, s32[512,2]{0,1:T(2,128)}, u32[]{:S(2)}) copy-start(s32[512,2]{0,1:T(2,128)} %param.13) | copy-start | bytes 12292
  7.2 19.0 %copy-start = (bf16[512,1024]{1,0:T(8,128)(2,1)S(1)}, bf16[512,1024]{1,0:T(8,128)(2,1)}, u32[]{:S(2)}) copy-start(bf16[512,1024]{1,0:T(8,128)(2,1)} %param.7) | copy-start | bytes 3145732
  10.8 27.3 %copy-start.5 = (f32[1024]{0:T(1024)S(1)}, f32[1024]{0:T(1024)}, u32[]{:S(2)}) copy-start(f32[1024]{0:T(1024)} %param.9) | copy-start | bytes 12292
  12.8 29.8 %all-to-all-start = ((s32[64,1,32]{2,1,0:T(1,128)}), s32[64,1,32]{2,1,0:T(1,128)S(1)}, u32[]{:S(2)}, u32[]{:S(2)}) async-start(s32[64,1,32]{2,1,0:T(1,128)} %bitcast.2), calls=%async_computation | async-start | bytes 65536 | tf_op jit(solution)/shard_map/all_to_all | solution.py:55
  38.1 5.8 %copy-start.1 = (bf16[512,1024]{1,0:T(8,128)(2,1)S(1)}, bf16[512,1024]{1,0:T(8,128)(2,1)}, u32[]{:S(2)}) copy-start(bf16[512,1024]{1,0:T(8,128)(2,1)} %param.8) | copy-start | bytes 3145732
  56.6 194.5 %all-to-all-start.1 = ((bf16[64,64,1024]{2,1,0:T(8,128)(2,1)}), bf16[64,64,1024]{2,1,0:T(8,128)(2,1)}, u32[]{:S(2)}, u32[]{:S(2)}) async-start(bf16[64,64,1024]{2,1,0:T(8,128)(2,1)} %pad_maximum_fusion), calls=%async_computation.1 | async-start | bytes 16777216 | tf_op jit(solution)/shard_map/all_to_all | solution.py:79
  68.8 49.3 %all-reduce.4.cloned.1.call-start = ((), (), s32[]{:S(2)}) async-start(), calls=%async_computation.3 | async-start | bytes 1048576 | tf_op jit(solution)/shard_map/psum | solution.py:93
  70.7 47.4 %copy-start.8 = (s32[512]{0:T(512)S(1)}, s32[512]{0:T(512)}, u32[]{:S(2)}) copy-start(s32[512]{0:T(512)} %param.10) | copy-start | bytes 6148
  261.3 1.3 copy-start.9
  280.0 21.2 %all-to-all-start.2 = ((bf16[64,1,32]{2,1,0:T(2,128)(2,1)}), bf16[64,1,32]{2,1,0:T(2,128)(2,1)S(1)}, u32[]{:S(2)}, u32[]{:S(2)}) async-start(bf16[64,1,32]{2,1,0:T(2,128)(2,1)} %convert_element_type.99), calls=%async_computation.2 | async-start | bytes 65536 | tf_op jit(solution)/shard_map/all_to_all | solution.py:107
  292.0 4.1 %copy-start.4 = (bf16[512,512]{1,0:T(8,128)(2,1)S(1)}, bf16[512,512]{1,0:T(8,128)(2,1)}, u32[]{:S(2)}) copy-start(bf16[512,512]{1,0:T(8,128)(2,1)} %all-reduce.4.cloned.1.call-done) | copy-start | bytes 1572868
  301.3 4.7 %copy-start.2 = (f32[512,1024]{1,0:T(8,128)S(1)}, f32[512,1024]{1,0:T(8,128)}, u32[]{:S(2)}) copy-start(f32[512,1024]{1,0:T(8,128)} %bitcast_add_fusion) | copy-start | bytes 6291460
  316.7 2.4 copy-start.3
Sparse Core Ops, SparseCore 0:
  72.5 45.5 all-reduce.3

commit v2 on v1

--- a/solution.py
+++ b/solution.py
@@ -67,28 +67,28 @@
     query_unit = query_unit32.astype(jnp.bfloat16)
     tool_unit = tool_unit32.astype(jnp.bfloat16)
 
-    pick_tool = (indices[:, None] == jnp.arange(tool_count, dtype=jnp.int32)[None, :]).astype(jnp.bfloat16)
-    answers = jnp.dot(pick_tool, tool_unit, preferred_element_type=jnp.float32).astype(jnp.bfloat16)
     slot_of_query = slot_at.reshape(query_count, per_query, places).any(axis=1)
     pick_query = slot_of_query.T.astype(jnp.bfloat16)
     sent_queries = jnp.dot(pick_query, query_unit, preferred_element_type=jnp.float32).astype(jnp.bfloat16)
-    payload = jnp.concatenate(
-        [answers.reshape(group_size, capacity, features), sent_queries.reshape(group_size, capacity, features)],
-        axis=1,
-    )
-    received = lax.all_to_all(payload, DP, 0, 0, tiled=True)
-    back = received[:, :capacity].reshape(places, features)
-    arrived = received[:, capacity:].reshape(places, features)
+    arrived_unit = lax.all_to_all(
+        sent_queries.reshape(group_size, capacity, features), DP, 0, 0, tiled=True
+    ).reshape(places, features)
+    arrived_unit, indices, tool_picked = lax.optimization_barrier((arrived_unit, indices, tool_unit))
+    tool_ids = jnp.arange(tool_count, dtype=jnp.int32)
+    pick_tool = (indices[:, None] == tool_ids[None, :]).astype(jnp.bfloat16)
+    answers = jnp.dot(pick_tool, tool_picked, preferred_element_type=jnp.float32).astype(jnp.bfloat16)
+    back_unit = lax.all_to_all(
+        answers.reshape(group_size, capacity, features), DP, 0, 0, tiled=True
+    ).reshape(places, features)
 
     local_part = lax.dot_general(
         query_unit, tool_unit, (((1,), (1,)), ((), ())), preferred_element_type=jnp.float32
     )
-    hard_units = jnp.dot(slot_at.astype(jnp.bfloat16), back, preferred_element_type=jnp.float32).reshape(
-        query_count, per_query, features
+    slot_grid = slot_at.reshape(query_count, per_query, places)
+    every_place = lax.dot_general(
+        query_unit, back_unit, (((1,), (1,)), ((), ())), preferred_element_type=jnp.float32
     )
-    hard_part = jnp.einsum(
-        "qd,qkd->qk", query_unit.astype(jnp.float32), hard_units, preferred_element_type=jnp.float32
-    )
+    hard_part = jnp.sum(jnp.where(slot_grid, every_place[:, None, :], 0.0), axis=2)
     shard_scores, negative_scores = (
         lax.psum(local_part.astype(jnp.bfloat16), "section").astype(jnp.float32),
         lax.psum(hard_part.astype(jnp.bfloat16), "section").astype(jnp.float32),
@@ -96,22 +96,19 @@
     shard_gradients, negative_gradients = softmax_grads(
         shard_scores, negative_scores, positive_tool, hard_valid
     )
+    spread_grads = jnp.sum(
+        jnp.where(slot_grid, negative_gradients.astype(jnp.float32)[:, :, None], 0.0), axis=1
+    ).astype(jnp.bfloat16)
     query_pull = jnp.dot(shard_gradients, tool_unit, preferred_element_type=jnp.float32)
-    query_pull = query_pull + jnp.einsum(
-        "qk,qkd->qd", negative_gradients.astype(jnp.float32), hard_units, preferred_element_type=jnp.float32
-    )
+    query_pull = query_pull + jnp.dot(spread_grads, back_unit, preferred_element_type=jnp.float32)
 
-    sent_grads = jnp.sum(
-        jnp.where(slot_at, negative_gradients.reshape(-1)[:, None].astype(jnp.float32), 0.0), axis=0
-    ).astype(jnp.bfloat16)
+    sent_grads = jnp.sum(spread_grads.astype(jnp.float32), axis=0).astype(jnp.bfloat16)
     arrived_grads = lax.all_to_all(sent_grads.reshape(group_size, capacity), DP, 0, 0, tiled=True).reshape(-1)
-    weights = jnp.where(
-        jnp.arange(tool_count, dtype=jnp.int32)[:, None] == indices[None, :], arrived_grads[None, :], 0.0
-    ).astype(jnp.bfloat16)
+    weights = jnp.where(tool_ids[:, None] == indices[None, :], arrived_grads[None, :], 0.0).astype(jnp.bfloat16)
     tool_pull = lax.dot_general(
         shard_gradients, query_unit, (((0,), (0,)), ((), ())), preferred_element_type=jnp.float32
     )
-    tool_pull = tool_pull + jnp.dot(weights, arrived, preferred_element_type=jnp.float32)
+    tool_pull = tool_pull + jnp.dot(weights, arrived_unit, preferred_element_type=jnp.float32)
 
     query_inner, tool_inner = lax.psum(
         (jnp.sum(query_unit32 * query_pull, axis=1), jnp.sum(tool_unit32 * tool_pull, axis=1)),

time: 357 us -> 350 us (0.980)
  waiting for transfers between devices: 181 us -> 190 us
  local copies, waits for them, and re-layouts: 12.2 us -> 4.93 us
  other arithmetic: 23.3 us -> 16.7 us
  matrix products: 38.2 us -> 32.2 us
  starting transfers between devices: 37.4 us -> 41.1 us
    concatenate x1 -> x0, other arithmetic: 8.49 us -> none  [body(): jnp.concatenate([answers.reshape(group_size, capacity, features), sent_qu...]
    dot_general x5 -> x4, matrix products: 26.6 us -> 19.1 us  [the longest x1 5.95 us: body(): jnp.dot(spread_grads, back_unit, preferred_element_type=jnp.float32)]
    all_to_all x1 -> x2, starting transfers between devices: 12.2 us -> 19.3 us  [the longest x1 12.2 us: body(): lax.all_to_all(sent_queries.reshape(group_size, capacity, features), DP,...]
    all_to_all x1 -> x2, waiting for transfers between devices: 132 us -> 137 us  [the longest x1 93 us: body(): lax.all_to_all(sent_queries.reshape(group_size, capacity, features), DP,...]
    slice x1 -> x0, local copies, waits for them, and re-layouts: 5.38 us -> none  [body(): arrived = received[:, capacity:].reshape(places, features)]
  transfers between devices with their start and end apart: 4 -> 5, of which waited for: 3 -> 4; matrix products, arithmetic and copies ran while one was open for 5% -> 5% of each run, Pallas kernels for 0% -> 0%
where the time goes in v2:
time: 350 us; the launch traced here: 345 us
  waiting for transfers between devices  190 us (54%)
  blocking collectives  45.8 us (13%)
  starting transfers between devices  41.1 us (12%)
  matrix products  32.2 us (9%)
  other arithmetic  16.7 us (5%)
  between operations  14.3 us (4%)
  local copies, waits for them, and re-layouts  4.93 us (1%)
    all_to_all x1, waiting for transfers between devices, body(): lax.all_to_all(sent_queries.reshape(group_size, capacity, features), DP,...  93 us
    psum x1, waiting for transfers between devices, body(): lax.psum(local_part.astype(jnp.bfloat16), 'section').astype(jnp.float32)  47.6 us
    all_to_all x1, waiting for transfers between devices, body(): lax.all_to_all(answers.reshape(group_size, capacity, features), DP, 0, 0,...  44 us
    psum x3, blocking collectives, body(): gain_grad = lax.psum(lax.psum(lax.psum(gain_terms, 'dc'), 'dy'), 'dz')  23.3 us
    all_to_all x1, starting transfers between devices, body(): indices = lax.all_to_all(requests, DP, 0, 0, tiled=True).reshape(-1)  13.1 us
    all_to_all x1, starting transfers between devices, body(): lax.all_to_all(sent_queries.reshape(group_size, capacity, features), DP,...  12.2 us
    psum x1, blocking collectives, body(): lax.psum((jnp.sum(query_scaled * query_scaled, axis=1), jnp.sum(tool_scal...  8.77 us
    all_to_all x1, starting transfers between devices, body(): lax.all_to_all(sent_grads.reshape(group_size, capacity), DP, 0, 0, tiled=...  8.47 us
  transfers between devices with their start and end apart: 5, of which 4 were waited for; matrix products, arithmetic and copies ran while one was open for 5% of the time, Pallas kernels for 0%

profile of v2, /device:TPU:1, one launch (start us, length us, event | category | flops | bytes accessed | tf_op | source)
XLA Modules:
  0.0 344.9 jit_solution(3491735345348525745)
XLA Ops:
  7.2 1.0 copy.24
  9.4 0.8 copy.27
  11.1 1.1 select_reduce_fusion.2
  12.9 13.1 %all-to-all-start.1 = ((s32[64,1,32]{2,1,0:T(1,128)}), s32[64,1,32]{2,1,0:T(1,128)S(1)}, u32[]{:S(2)}, u32[]{:S(2)}) async-start(s32[64,1,32]{2,1,0:T(1,128)} %bitcast.2), calls=%async_computation.1 | async-start | bytes 65536 | tf_op jit(solution)/shard_map/all_to_all | solution.py:55
  27.1 1.1 fusion
  28.8 8.8 %all-reduce.1 = (f32[512]{0:T(512)S(1)}, f32[512]{0:T(512)S(1)}) all-reduce(f32[512]{0:T(512)S(1)} %get-tuple-element.14, f32[512]{0:T(512)S(1)} %get-tuple-element.13), channel_id=1, replica_groups=mesh['dz'=8,'dy'=4,'dc'=2,'section'=4] {'section'}, use_global_device_ids=true, to_apply=%region_1.2 | all-reduce | flops 1024 | bytes 8192 | tf_op jit(solution)/shard_map/psum | solution.py:59
  37.6 4.4 %convolution_convert_fusion = bf16[2048,1024]{1,0:T(8,128)(2,1)} fusion(pred[512,2048]{1,0:T(8,128)(4,1)S(1)} %fusion, f32[512]{0:T(512)S(1)} %add_sqrt_fusion.1, f32[1024]{0:T(1024)S(1)} %copy-done.5, bf16[512,1024]{1,0:T(8,128)(2,1)S(1)} %copy-done.1), kind=kOutput, calls=%fused_computation.14 | convolution fusion | flops 2151677952 | bytes 6297600 | tf_op jit(solution)/shard_map/dot_general | solution.py:72
  42.1 12.2 %all-to-all-start = ((bf16[64,32,1024]{2,1,0:T(8,128)(2,1)}), bf16[64,32,1024]{2,1,0:T(8,128)(2,1)}, u32[]{:S(2)}, u32[]{:S(2)}) async-start(bf16[64,32,1024]{2,1,0:T(8,128)(2,1)} %bitcast.14), calls=%async_computation | async-start | bytes 8388608 | tf_op jit(solution)/shard_map/all_to_all | solution.py:73
  56.0 93.0 %all-to-all-done = bf16[64,32,1024]{2,1,0:T(8,128)(2,1)} async-done(((bf16[64,32,1024]{2,1,0:T(8,128)(2,1)}), bf16[64,32,1024]{2,1,0:T(8,128)(2,1)}, u32[]{:S(2)}, u32[]{:S(2)}) %all-to-all-start) | async-done | bytes 4194336 | tf_op jit(solution)/shard_map/all_to_all | solution.py:73
  149.0 3.9 %fusion.4 = bf16[2048,1024]{1,0:T(8,128)(2,1)} fusion(bf16[512,1024]{1,0:T(8,128)(2,1)S(1)} %fusion.31, s32[2048]{0:T(1024)S(1)} %reshape.97), kind=kOutput, calls=%fused_computation.13 | convolution fusion | flops 2150629376 | bytes 5251072 | tf_op jit(solution)/shard_map/dot_general | solution.py:79
  152.9 7.1 %all-to-all-start.2 = ((bf16[64,32,1024]{2,1,0:T(8,128)(2,1)}), bf16[64,32,1024]{2,1,0:T(8,128)(2,1)}, u32[]{:S(2)}, u32[]{:S(2)}) async-start(bf16[64,32,1024]{2,1,0:T(8,128)(2,1)} %bitcast.13), calls=%async_computation.2 | async-start | bytes 8388608 | tf_op jit(solution)/shard_map/all_to_all | solution.py:80
  160.3 1.6 convolution_convert_fusion.1
  161.8 47.6 %all-reduce.4.cloned.1.call-done = bf16[512,512]{1,0:T(8,128)(2,1)} async-done(((bf16[512,512]{1,0:T(8,128)(2,1)}), bf16[512,512]{1,0:T(8,128)(2,1)}) %all-reduce.4.cloned.1.call-update) | async-done | bytes 524304 | tf_op jit(solution)/shard_map/psum | solution.py:93
  209.4 1.5 fusion.19
  210.9 44.0 %all-to-all-done.2 = bf16[64,32,1024]{2,1,0:T(8,128)(2,1)} async-done(((bf16[64,32,1024]{2,1,0:T(8,128)(2,1)}), bf16[64,32,1024]{2,1,0:T(8,128)(2,1)}, u32[]{:S(2)}, u32[]{:S(2)}) %all-to-all-start.2) | async-done | bytes 4194336 | tf_op jit(solution)/shard_map/all_to_all | solution.py:80
  254.9 4.6 %fusion.36 = f32[512,2048]{1,0:T(8,128)S(1)} fusion(bf16[2048,1024]{1,0:T(8,128)(2,1)} %bitcast.4, f32[512]{0:T(512)S(1)} %add_sqrt_fusion.1, f32[1024]{0:T(1024)S(1)} %copy-done.5, bf16[512,1024]{1,0:T(8,128)(2,1)S(1)} %copy-done.1), kind=kOutput, calls=%fused_computation.69 | convolution fusion | flops 2149580800 | bytes 9443328 | tf_op jit(solution)/shard_map/dot_general | solution.py:88
  259.5 1.4 select_reduce_fusion.1
  260.9 6.0 %psum.66 = bf16[512,2]{0,1:T(2,128)(2,1)S(1)} all-reduce(bf16[512,2]{0,1:T(2,128)(2,1)S(1)} %select_reduce_fusion.1), channel_id=1, replica_groups=mesh['dz'=8,'dy'=4,'dc'=2,'section'=4] {'section'}, use_global_device_ids=true, to_apply=%region_11.12 | all-reduce | flops 1024 | bytes 4096 | tf_op jit(solution)/shard_map/psum | solution.py:94
  267.0 1.9 select_reduce_fusion
  268.9 6.0 %fusion.40 = f32[512,1024]{1,0:T(8,128)} fusion(bf16[512,2048]{1,0:T(8,128)(2,1)S(1)} %select_reduce_fusion, bf16[2048,1024]{1,0:T(8,128)(2,1)} %bitcast.4), kind=kOutput, calls=%fused_computation.70 | convolution fusion | flops 2147483648 | bytes 8388608 | tf_op jit(solution)/shard_map/dot_general | solution.py:103
  275.9 8.5 %all-to-all-start.3 = ((bf16[64,1,32]{2,1,0:T(2,128)(2,1)}), bf16[64,1,32]{2,1,0:T(2,128)(2,1)S(1)}, u32[]{:S(2)}, u32[]{:S(2)}) async-start(bf16[64,1,32]{2,1,0:T(2,128)(2,1)} %all_to_all.24), calls=%async_computation.3 | async-start | bytes 65536 | tf_op jit(solution)/shard_map/all_to_all | solution.py:106
  284.4 4.1 %convolution_add_fusion.1 = f32[512,1024]{1,0:T(8,128)} fusion(f32[512,1024]{1,0:T(8,128)} %fusion.40, bf16[512,1024]{1,0:T(8,128)(2,1)S(1)} %fusion.31, bf16[512,512]{1,0:T(8,128)(2,1)} %all-reduce.4.cloned.1.call-done, f32[512]{0:T(512)S(1)} %get-tuple-element.24, s32[512]{0:T(512)S(1)} %copy-done.7, f32[512]{0:T(512)S(1)} %get-tuple-element.9), kind=kOutput, calls=%fused_computation.37 | convolution fusion | flops 539492352 | bytes 5773312 | tf_op jit(solution)/shard_map/dot_general | solution.py:102
  288.5 5.2 %all-to-all-done.3 = bf16[64,1,32]{2,1,0:T(2,128)(2,1)S(1)} async-done(((bf16[64,1,32]{2,1,0:T(2,128)(2,1)}), bf16[64,1,32]{2,1,0:T(2,128)(2,1)S(1)}, u32[]{:S(2)}, u32[]{:S(2)}) %all-to-all-start.3) | async-done | bytes 4128 | tf_op jit(solution)/shard_map/all_to_all | solution.py:106
  293.9 4.7 %fusion.13 = f32[512,1024]{1,0:T(8,128)S(1)} fusion(bf16[2048,1024]{1,0:T(8,128)(2,1)} %bitcast.1, s32[2048]{0:T(1024)S(1)} %reshape.97, bf16[2048]{0:T(1024)(128)(2,1)S(1)} %broadcast_in_dim.110), kind=kOutput, calls=%fused_computation.27 | convolution fusion | flops 2149580800 | bytes 6303744 | tf_op jit(solution)/shard_map/dot_general | solution.py:111
  298.6 3.0 multiply_reduce_fusion
  301.6 7.7 %all-reduce = (f32[512]{0:T(512)S(1)}, f32[512]{0:T(512)S(1)}) all-reduce(f32[512]{0:T(512)S(1)} %get-tuple-element.12, f32[512]{0:T(512)S(1)} %get-tuple-element.11), channel_id=1, replica_groups=mesh['dz'=8,'dy'=4,'dc'=2,'section'=4] {'section'}, use_global_device_ids=true, to_apply=%region_15.16 | all-reduce | flops 1024 | bytes 8192 | tf_op jit(solution)/shard_map/psum | solution.py:113
  309.3 2.4 fusion.12
  311.7 1.9 fusion.11
  313.6 1.2 multiply_convert_fusion.1
  314.8 4.8 %psum.69 = f32[1024]{0:T(1024)S(1)} all-reduce(f32[1024]{0:T(1024)S(1)} %add.69), channel_id=1, replica_groups=mesh['dz'=8,'dy'=4,'dc'=2,'section'=4] {'dc'}, use_global_device_ids=true, to_apply=%region_21.22 | all-reduce | flops 1024 | bytes 8192 | tf_op jit(solution)/shard_map/psum | solution.py:124
  319.6 6.7 %psum.70 = f32[1024]{0:T(1024)S(1)} all-reduce(f32[1024]{0:T(1024)S(1)} %psum.69), channel_id=1, replica_groups=mesh['dz'=8,'dy'=4,'dc'=2,'section'=4] {'dy'}, use_global_device_ids=true, to_apply=%region_22.23 | all-reduce | flops 1024 | bytes 8192 | tf_op jit(solution)/shard_map/psum | solution.py:124
  326.3 11.7 %psum.71 = f32[1024]{0:T(1024)} all-reduce(f32[1024]{0:T(1024)S(1)} %psum.70), channel_id=1, replica_groups=mesh['dz'=8,'dy'=4,'dc'=2,'section'=4] {'dz'}, use_global_device_ids=true, to_apply=%region_23.24 | all-reduce | flops 1024 | bytes 8192 | tf_op jit(solution)/shard_map/psum | solution.py:124
  (45 shorter events, 7.6 us)
Async XLA Ops:
  7.2 21.0 %copy-start.1 = (bf16[512,1024]{1,0:T(8,128)(2,1)S(1)}, bf16[512,1024]{1,0:T(8,128)(2,1)}, u32[]{:S(2)}) copy-start(bf16[512,1024]{1,0:T(8,128)(2,1)} %param.7) | copy-start | bytes 3145732
  7.2 21.0 %copy-start = (bf16[512,1024]{1,0:T(8,128)(2,1)S(1)}, bf16[512,1024]{1,0:T(8,128)(2,1)}, u32[]{:S(2)}) copy-start(bf16[512,1024]{1,0:T(8,128)(2,1)} %param.8) | copy-start | bytes 3145732
  7.2 21.0 %copy-start.5 = (f32[1024]{0:T(1024)S(1)}, f32[1024]{0:T(1024)}, u32[]{:S(2)}) copy-start(f32[1024]{0:T(1024)} %param.9) | copy-start | bytes 12292
  12.9 29.2 %all-to-all-start.1 = ((s32[64,1,32]{2,1,0:T(1,128)}), s32[64,1,32]{2,1,0:T(1,128)S(1)}, u32[]{:S(2)}, u32[]{:S(2)}) async-start(s32[64,1,32]{2,1,0:T(1,128)} %bitcast.2), calls=%async_computation.1 | async-start | bytes 65536 | tf_op jit(solution)/shard_map/all_to_all | solution.py:55
  42.1 106.9 %all-to-all-start = ((bf16[64,32,1024]{2,1,0:T(8,128)(2,1)}), bf16[64,32,1024]{2,1,0:T(8,128)(2,1)}, u32[]{:S(2)}, u32[]{:S(2)}) async-start(bf16[64,32,1024]{2,1,0:T(8,128)(2,1)} %bitcast.14), calls=%async_computation | async-start | bytes 8388608 | tf_op jit(solution)/shard_map/all_to_all | solution.py:73
  152.9 102.0 %all-to-all-start.2 = ((bf16[64,32,1024]{2,1,0:T(8,128)(2,1)}), bf16[64,32,1024]{2,1,0:T(8,128)(2,1)}, u32[]{:S(2)}, u32[]{:S(2)}) async-start(bf16[64,32,1024]{2,1,0:T(8,128)(2,1)} %bitcast.13), calls=%async_computation.2 | async-start | bytes 8388608 | tf_op jit(solution)/shard_map/all_to_all | solution.py:80
  160.0 49.4 %copy-start.7 = (s32[512]{0:T(512)S(1)}, s32[512]{0:T(512)}, u32[]{:S(2)}) copy-start(s32[512]{0:T(512)} %param.10) | copy-start | bytes 6148
  160.0 49.4 %all-reduce.4.cloned.1.call-start = ((), (), s32[]{:S(2)}) async-start(), calls=%async_computation.4 | async-start | bytes 1048576 | tf_op jit(solution)/shard_map/psum | solution.py:93
  259.5 7.4 %copy-start.6 = (s32[512,2]{0,1:T(2,128)S(1)}, s32[512,2]{0,1:T(2,128)}, u32[]{:S(2)}) copy-start(s32[512,2]{0,1:T(2,128)} %param.13) | copy-start | bytes 12292
  275.9 17.8 %all-to-all-start.3 = ((bf16[64,1,32]{2,1,0:T(2,128)(2,1)}), bf16[64,1,32]{2,1,0:T(2,128)(2,1)S(1)}, u32[]{:S(2)}, u32[]{:S(2)}) async-start(bf16[64,1,32]{2,1,0:T(2,128)(2,1)} %all_to_all.24), calls=%async_computation.3 | async-start | bytes 65536 | tf_op jit(solution)/shard_map/all_to_all | solution.py:106
  293.9 4.7 %copy-start.2 = (f32[512,1024]{1,0:T(8,128)S(1)}, f32[512,1024]{1,0:T(8,128)}, u32[]{:S(2)}) copy-start(f32[512,1024]{1,0:T(8,128)} %convolution_add_fusion.1) | copy-start | bytes 6291460
  293.9 4.7 %copy-start.4 = (bf16[512,512]{1,0:T(8,128)(2,1)S(1)}, bf16[512,512]{1,0:T(8,128)(2,1)}, u32[]{:S(2)}) copy-start(bf16[512,512]{1,0:T(8,128)(2,1)} %all-reduce.4.cloned.1.call-done) | copy-start | bytes 1572868
  309.3 2.4 copy-start.3
Sparse Core Ops, SparseCore 0:
  163.7 45.6 all-reduce.3

commit v3 on v2

--- a/solution.py
+++ b/solution.py
@@ -67,16 +67,9 @@
     query_unit = query_unit32.astype(jnp.bfloat16)
     tool_unit = tool_unit32.astype(jnp.bfloat16)
 
-    slot_of_query = slot_at.reshape(query_count, per_query, places).any(axis=1)
-    pick_query = slot_of_query.T.astype(jnp.bfloat16)
-    sent_queries = jnp.dot(pick_query, query_unit, preferred_element_type=jnp.float32).astype(jnp.bfloat16)
-    arrived_unit = lax.all_to_all(
-        sent_queries.reshape(group_size, capacity, features), DP, 0, 0, tiled=True
-    ).reshape(places, features)
-    arrived_unit, indices, tool_picked = lax.optimization_barrier((arrived_unit, indices, tool_unit))
     tool_ids = jnp.arange(tool_count, dtype=jnp.int32)
     pick_tool = (indices[:, None] == tool_ids[None, :]).astype(jnp.bfloat16)
-    answers = jnp.dot(pick_tool, tool_picked, preferred_element_type=jnp.float32).astype(jnp.bfloat16)
+    answers = jnp.dot(pick_tool, tool_unit, preferred_element_type=jnp.float32).astype(jnp.bfloat16)
     back_unit = lax.all_to_all(
         answers.reshape(group_size, capacity, features), DP, 0, 0, tiled=True
     ).reshape(places, features)
@@ -99,16 +92,22 @@
     spread_grads = jnp.sum(
         jnp.where(slot_grid, negative_gradients.astype(jnp.float32)[:, :, None], 0.0), axis=1
     ).astype(jnp.bfloat16)
+
+    sent_terms = lax.dot_general(
+        spread_grads, query_unit, (((0,), (0,)), ((), ())), preferred_element_type=jnp.float32
+    ).astype(jnp.bfloat16)
+    arrived_terms = lax.all_to_all(
+        sent_terms.reshape(group_size, capacity, features), DP, 0, 0, tiled=True
+    ).reshape(places, features)
+
     query_pull = jnp.dot(shard_gradients, tool_unit, preferred_element_type=jnp.float32)
     query_pull = query_pull + jnp.dot(spread_grads, back_unit, preferred_element_type=jnp.float32)
-
-    sent_grads = jnp.sum(spread_grads.astype(jnp.float32), axis=0).astype(jnp.bfloat16)
-    arrived_grads = lax.all_to_all(sent_grads.reshape(group_size, capacity), DP, 0, 0, tiled=True).reshape(-1)
-    weights = jnp.where(tool_ids[:, None] == indices[None, :], arrived_grads[None, :], 0.0).astype(jnp.bfloat16)
     tool_pull = lax.dot_general(
         shard_gradients, query_unit, (((0,), (0,)), ((), ())), preferred_element_type=jnp.float32
     )
-    tool_pull = tool_pull + jnp.dot(weights, arrived_unit, preferred_element_type=jnp.float32)
+    tool_pull = tool_pull + lax.dot_general(
+        pick_tool, arrived_terms, (((0,), (0,)), ((), ())), preferred_element_type=jnp.float32
+    )
 
     query_inner, tool_inner = lax.psum(
         (jnp.sum(query_unit32 * query_pull, axis=1), jnp.sum(tool_unit32 * tool_pull, axis=1)),

time: 350 us -> 330 us (0.943)
  waiting for transfers between devices: 190 us -> 178 us
  starting transfers between devices: 41.1 us -> 34.4 us
    all_to_all x2 -> x1, starting transfers between devices: 20.7 us -> 8.84 us  [body(): lax.all_to_all(sent_terms.reshape(group_size, capacity, features), DP, 0,...]
    all_to_all x2 -> x1, waiting for transfers between devices: 98.3 us -> 87.2 us  [body(): lax.all_to_all(sent_terms.reshape(group_size, capacity, features), DP, 0,...]
    all_to_all x1, starting transfers between devices: 7.1 us -> 12.3 us  [body(): lax.all_to_all(answers.reshape(group_size, capacity, features), DP, 0, 0,...]
  transfers between devices with their start and end apart: 5 -> 4, of which waited for: 4 -> 3; matrix products, arithmetic and copies ran while one was open for 5% -> 4% of each run, Pallas kernels for 0% -> 0%
where the time goes in v3:
time: 330 us; the launch traced here: 326 us
  waiting for transfers between devices  178 us (54%)
  blocking collectives  48.6 us (15%)
  starting transfers between devices  34.4 us (10%)
  matrix products  30.2 us (9%)
  other arithmetic  15.8 us (5%)
  between operations  14.3 us (4%)
  local copies, waits for them, and re-layouts  4.01 us (1%)
    all_to_all x1, waiting for transfers between devices, body(): lax.all_to_all(sent_terms.reshape(group_size, capacity, features), DP, 0,...  87.2 us
    psum x1, waiting for transfers between devices, body(): lax.psum(local_part.astype(jnp.bfloat16), 'section').astype(jnp.float32)  47.2 us
    all_to_all x1, waiting for transfers between devices, body(): lax.all_to_all(answers.reshape(group_size, capacity, features), DP, 0, 0,...  43.9 us
    psum x3, blocking collectives, body(): gain_grad = lax.psum(lax.psum(lax.psum(gain_terms, 'dc'), 'dy'), 'dz')  25.9 us
    all_to_all x1, starting transfers between devices, body(): indices = lax.all_to_all(requests, DP, 0, 0, tiled=True).reshape(-1)  13.1 us
    all_to_all x1, starting transfers between devices, body(): lax.all_to_all(answers.reshape(group_size, capacity, features), DP, 0, 0,...  12.3 us
    all_to_all x1, starting transfers between devices, body(): lax.all_to_all(sent_terms.reshape(group_size, capacity, features), DP, 0,...  8.84 us
    psum x1, blocking collectives, body(): lax.psum((jnp.sum(query_scaled * query_scaled, axis=1), jnp.sum(tool_scal...  8.77 us
  transfers between devices with their start and end apart: 4, of which 3 were waited for; matrix products, arithmetic and copies ran while one was open for 4% of the time, Pallas kernels for 0%

profile of v3, /device:TPU:1, one launch (start us, length us, event | category | flops | bytes accessed | tf_op | source)
XLA Modules:
  0.0 325.6 jit_solution(5737720087220885142)
XLA Ops:
  7.2 0.8 broadcast_compare_fusion
  8.4 0.8 copy.26
  9.4 0.8 copy.23
  11.0 1.1 select_reduce_fusion.2
  12.8 13.1 %all-to-all-start = ((s32[64,1,32]{2,1,0:T(1,128)}), s32[64,1,32]{2,1,0:T(1,128)S(1)}, u32[]{:S(2)}, u32[]{:S(2)}) async-start(s32[64,1,32]{2,1,0:T(1,128)} %bitcast), calls=%async_computation | async-start | bytes 65536 | tf_op jit(solution)/shard_map/all_to_all | solution.py:55
  26.0 2.2 fusion.9
  28.1 8.8 %all-reduce.1 = (f32[512]{0:T(512)S(1)}, f32[512]{0:T(512)S(1)}) all-reduce(f32[512]{0:T(512)S(1)} %get-tuple-element.8, f32[512]{0:T(512)S(1)} %get-tuple-element.7), channel_id=1, replica_groups=mesh['dz'=8,'dy'=4,'dc'=2,'section'=4] {'section'}, use_global_device_ids=true, to_apply=%region_3.4 | all-reduce | flops 1024 | bytes 8192 | tf_op jit(solution)/shard_map/psum | solution.py:59
  37.4 0.7 reduce.3
  38.2 4.2 %fusion.3 = bf16[2048,1024]{1,0:T(8,128)(2,1)} fusion(s32[2048]{0:T(1024)S(1)} %eq.70, bf16[512,1024]{1,0:T(8,128)(2,1)S(1)} %copy-done.1, f32[512]{0:T(512)S(1)} %add_sqrt_fusion, f32[1024]{0:T(1024)S(1)} %copy-done.7), kind=kOutput, calls=%fused_computation.11 | convolution fusion | flops 2152726528 | bytes 5257216 | tf_op jit(solution)/shard_map/dot_general | solution.py:72
  42.5 12.3 %all-to-all-start.1 = ((bf16[64,32,1024]{2,1,0:T(8,128)(2,1)}), bf16[64,32,1024]{2,1,0:T(8,128)(2,1)}, u32[]{:S(2)}, u32[]{:S(2)}) async-start(bf16[64,32,1024]{2,1,0:T(8,128)(2,1)} %bitcast.10), calls=%async_computation.1 | async-start | bytes 8388608 | tf_op jit(solution)/shard_map/all_to_all | solution.py:73
  54.9 1.6 convolution_convert_fusion.1
  56.9 47.2 %all-reduce.4.cloned.1.call-done = bf16[512,512]{1,0:T(8,128)(2,1)} async-done(((bf16[512,512]{1,0:T(8,128)(2,1)}), bf16[512,512]{1,0:T(8,128)(2,1)}) %all-reduce.4.cloned.1.call-update) | async-done | bytes 524304 | tf_op jit(solution)/shard_map/psum | solution.py:86
  104.1 1.5 fusion.16
  105.6 43.9 %all-to-all-done.1 = bf16[64,32,1024]{2,1,0:T(8,128)(2,1)} async-done(((bf16[64,32,1024]{2,1,0:T(8,128)(2,1)}), bf16[64,32,1024]{2,1,0:T(8,128)(2,1)}, u32[]{:S(2)}, u32[]{:S(2)}) %all-to-all-start.1) | async-done | bytes 4194336 | tf_op jit(solution)/shard_map/all_to_all | solution.py:73
  149.5 4.6 %fusion.37 = f32[512,2048]{1,0:T(8,128)S(1)} fusion(bf16[2048,1024]{1,0:T(8,128)(2,1)} %bitcast.2, f32[512]{0:T(512)S(1)} %add_sqrt_fusion.1, f32[1024]{0:T(1024)S(1)} %copy-done.7, bf16[512,1024]{1,0:T(8,128)(2,1)S(1)} %copy-done), kind=kOutput, calls=%fused_computation.65 | convolution fusion | flops 2149580800 | bytes 9443328 | tf_op jit(solution)/shard_map/dot_general | solution.py:81
  154.1 1.4 select_reduce_fusion.1
  155.5 6.2 %psum.66 = bf16[512,2]{0,1:T(2,128)(2,1)S(1)} all-reduce(bf16[512,2]{0,1:T(2,128)(2,1)S(1)} %select_reduce_fusion.1), channel_id=1, replica_groups=mesh['dz'=8,'dy'=4,'dc'=2,'section'=4] {'section'}, use_global_device_ids=true, to_apply=%region_10.11 | all-reduce | flops 1024 | bytes 4096 | tf_op jit(solution)/shard_map/psum | solution.py:87
  161.8 1.9 select_reduce_fusion
  163.7 4.5 %convolution_convert_fusion = bf16[2048,1024]{1,0:T(8,128)(2,1)} fusion(bf16[512,2048]{1,0:T(8,128)(2,1)S(1)} %select_reduce_fusion, f32[512]{0:T(512)S(1)} %add_sqrt_fusion.1, f32[1024]{0:T(1024)S(1)} %copy-done.7, bf16[512,1024]{1,0:T(8,128)(2,1)S(1)} %copy-done), kind=kOutput, calls=%fused_computation.12 | convolution fusion | flops 2151677952 | bytes 7346176 | tf_op jit(solution)/shard_map/dot_general | solution.py:96
  168.2 8.8 %all-to-all-start.2 = ((bf16[64,32,1024]{2,1,0:T(8,128)(2,1)}), bf16[64,32,1024]{2,1,0:T(8,128)(2,1)}, u32[]{:S(2)}, u32[]{:S(2)}) async-start(bf16[64,32,1024]{2,1,0:T(8,128)(2,1)} %bitcast.11), calls=%async_computation.2 | async-start | bytes 8388608 | tf_op jit(solution)/shard_map/all_to_all | solution.py:99
  177.0 5.2 %fusion.40 = f32[512,1024]{1,0:T(8,128)S(1)} fusion(bf16[512,2048]{1,0:T(8,128)(2,1)} %copy-done.4, bf16[2048,1024]{1,0:T(8,128)(2,1)} %bitcast.2), kind=kOutput, calls=%fused_computation.66 | convolution fusion | flops 2147483648 | bytes 8388608 | tf_op jit(solution)/shard_map/dot_general | solution.py:104
  182.2 2.4 convolution_add_fusion.1
  184.7 87.2 %all-to-all-done.2 = bf16[64,32,1024]{2,1,0:T(8,128)(2,1)} async-done(((bf16[64,32,1024]{2,1,0:T(8,128)(2,1)}), bf16[64,32,1024]{2,1,0:T(8,128)(2,1)}, u32[]{:S(2)}, u32[]{:S(2)}) %all-to-all-start.2) | async-done | bytes 4194336 | tf_op jit(solution)/shard_map/all_to_all | solution.py:99
  271.9 4.8 %fusion = f32[512,1024]{1,0:T(8,128)S(1)} fusion(bf16[2048,1024]{1,0:T(8,128)(2,1)} %bitcast.4, s32[2048]{0:T(1024)S(1)} %eq.70), kind=kOutput, calls=%fused_computation.6 | convolution fusion | flops 2148532224 | bytes 6299648 | tf_op jit(solution)/shard_map/dot_general | solution.py:108
  276.7 2.9 multiply_reduce_fusion
  279.6 7.7 %all-reduce = (f32[512]{0:T(512)S(1)}, f32[512]{0:T(512)S(1)}) all-reduce(f32[512]{0:T(512)S(1)} %get-tuple-element.6, f32[512]{0:T(512)S(1)} %get-tuple-element.5), channel_id=1, replica_groups=mesh['dz'=8,'dy'=4,'dc'=2,'section'=4] {'section'}, use_global_device_ids=true, to_apply=%region_14.15 | all-reduce | flops 1024 | bytes 8192 | tf_op jit(solution)/shard_map/psum | solution.py:112
  287.3 2.4 fusion.11
  289.7 1.9 fusion.10
  291.6 6.1 %psum.69 = f32[1024]{0:T(1024)S(1)} all-reduce(f32[1024]{0:T(1024)S(1)} %add.69), channel_id=1, replica_groups=mesh['dz'=8,'dy'=4,'dc'=2,'section'=4] {'dc'}, use_global_device_ids=true, to_apply=%region_19.20 | all-reduce | flops 1024 | bytes 8192 | tf_op jit(solution)/shard_map/psum | solution.py:123
  297.6 8.3 %psum.70 = f32[1024]{0:T(1024)S(1)} all-reduce(f32[1024]{0:T(1024)S(1)} %psum.69), channel_id=1, replica_groups=mesh['dz'=8,'dy'=4,'dc'=2,'section'=4] {'dy'}, use_global_device_ids=true, to_apply=%region_20.21 | all-reduce | flops 1024 | bytes 8192 | tf_op jit(solution)/shard_map/psum | solution.py:123
  305.9 11.6 %psum.71 = f32[1024]{0:T(1024)} all-reduce(f32[1024]{0:T(1024)S(1)} %psum.70), channel_id=1, replica_groups=mesh['dz'=8,'dy'=4,'dc'=2,'section'=4] {'dz'}, use_global_device_ids=true, to_apply=%region_21.22 | all-reduce | flops 1024 | bytes 8192 | tf_op jit(solution)/shard_map/psum | solution.py:123
  317.5 1.2 multiply_convert_fusion.1
  (41 shorter events, 3.1 us)
Async XLA Ops:
  7.2 31.1 %copy-start.7 = (f32[1024]{0:T(1024)S(1)}, f32[1024]{0:T(1024)}, u32[]{:S(2)}) copy-start(f32[1024]{0:T(1024)} %param.9) | copy-start | bytes 12292
  7.2 31.1 %copy-start.1 = (bf16[512,1024]{1,0:T(8,128)(2,1)S(1)}, bf16[512,1024]{1,0:T(8,128)(2,1)}, u32[]{:S(2)}) copy-start(bf16[512,1024]{1,0:T(8,128)(2,1)} %param.8) | copy-start | bytes 3145732
  12.8 24.1 %all-to-all-start = ((s32[64,1,32]{2,1,0:T(1,128)}), s32[64,1,32]{2,1,0:T(1,128)S(1)}, u32[]{:S(2)}, u32[]{:S(2)}) async-start(s32[64,1,32]{2,1,0:T(1,128)} %bitcast), calls=%async_computation | async-start | bytes 65536 | tf_op jit(solution)/shard_map/all_to_all | solution.py:55
  42.5 12.4 %copy-start = (bf16[512,1024]{1,0:T(8,128)(2,1)S(1)}, bf16[512,1024]{1,0:T(8,128)(2,1)}, u32[]{:S(2)}) copy-start(bf16[512,1024]{1,0:T(8,128)(2,1)} %param.7) | copy-start | bytes 3145732
  42.5 107.1 %all-to-all-start.1 = ((bf16[64,32,1024]{2,1,0:T(8,128)(2,1)}), bf16[64,32,1024]{2,1,0:T(8,128)(2,1)}, u32[]{:S(2)}, u32[]{:S(2)}) async-start(bf16[64,32,1024]{2,1,0:T(8,128)(2,1)} %bitcast.10), calls=%async_computation.1 | async-start | bytes 8388608 | tf_op jit(solution)/shard_map/all_to_all | solution.py:73
  54.8 49.3 %all-reduce.4.cloned.1.call-start = ((), (), s32[]{:S(2)}) async-start(), calls=%async_computation.3 | async-start | bytes 1048576 | tf_op jit(solution)/shard_map/psum | solution.py:86
  54.9 2.0 copy-start.6
  54.9 2.0 copy-start.8
  54.9 49.2 %copy-start.9 = (s32[512]{0:T(512)S(1)}, s32[512]{0:T(512)}, u32[]{:S(2)}) copy-start(s32[512]{0:T(512)} %param.10) | copy-start | bytes 6148
  163.7 4.5 %copy-start.4 = (bf16[512,2048]{1,0:T(8,128)(2,1)}, bf16[512,2048]{1,0:T(8,128)(2,1)S(1)}, u32[]{:S(2)}) copy-start(bf16[512,2048]{1,0:T(8,128)(2,1)S(1)} %select_reduce_fusion) | copy-start | bytes 6291460
  168.2 103.8 %all-to-all-start.2 = ((bf16[64,32,1024]{2,1,0:T(8,128)(2,1)}), bf16[64,32,1024]{2,1,0:T(8,128)(2,1)}, u32[]{:S(2)}, u32[]{:S(2)}) async-start(bf16[64,32,1024]{2,1,0:T(8,128)(2,1)} %bitcast.11), calls=%async_computation.2 | async-start | bytes 8388608 | tf_op jit(solution)/shard_map/all_to_all | solution.py:99
  177.0 5.2 %copy-start.5 = (bf16[512,512]{1,0:T(8,128)(2,1)S(1)}, bf16[512,512]{1,0:T(8,128)(2,1)}, u32[]{:S(2)}) copy-start(bf16[512,512]{1,0:T(8,128)(2,1)} %all-reduce.4.cloned.1.call-done) | copy-start | bytes 1572868
  271.9 4.8 %copy-start.2 = (f32[512,1024]{1,0:T(8,128)S(1)}, f32[512,1024]{1,0:T(8,128)}, u32[]{:S(2)}) copy-start(f32[512,1024]{1,0:T(8,128)} %convolution_add_fusion.1) | copy-start | bytes 6291460
  287.3 2.4 copy-start.3
Sparse Core Ops, SparseCore 0:
  58.6 45.5 all-reduce.3

commit v4 on v3

--- a/solution.py
+++ b/solution.py
@@ -54,6 +54,13 @@
     requests = jnp.sum(jnp.where(slot_at, wanted_rows[:, None], 0), axis=0).reshape(group_size, capacity)
     indices = lax.all_to_all(requests, DP, 0, 0, tiled=True).reshape(-1)
 
+    tool_ids = jnp.arange(tool_count, dtype=jnp.int32)
+    pick_tool = (indices[:, None] == tool_ids[None, :]).astype(jnp.bfloat16)
+    answers = jnp.dot(pick_tool, tool_hidden, preferred_element_type=jnp.float32).astype(jnp.bfloat16)
+    back_hidden = lax.all_to_all(
+        answers.reshape(group_size, capacity, features), DP, 0, 0, tiled=True
+    ).reshape(places, features)
+
     query_scaled = query_hidden.astype(jnp.float32) * norm_gain
     tool_scaled = tool_hidden.astype(jnp.float32) * norm_gain
     query_squares, tool_squares = lax.psum(
@@ -67,25 +74,27 @@
     query_unit = query_unit32.astype(jnp.bfloat16)
     tool_unit = tool_unit32.astype(jnp.bfloat16)
 
-    tool_ids = jnp.arange(tool_count, dtype=jnp.int32)
-    pick_tool = (indices[:, None] == tool_ids[None, :]).astype(jnp.bfloat16)
-    answers = jnp.dot(pick_tool, tool_unit, preferred_element_type=jnp.float32).astype(jnp.bfloat16)
-    back_unit = lax.all_to_all(
-        answers.reshape(group_size, capacity, features), DP, 0, 0, tiled=True
-    ).reshape(places, features)
-
     local_part = lax.dot_general(
         query_unit, tool_unit, (((1,), (1,)), ((), ())), preferred_element_type=jnp.float32
     )
+    shard_scores = lax.psum(local_part.astype(jnp.bfloat16), "section").astype(jnp.float32)
+    back_hidden, query_unit, shard_scores = lax.optimization_barrier((back_hidden, query_unit, shard_scores))
+
+    back_scaled = back_hidden.astype(jnp.float32) * norm_gain
     slot_grid = slot_at.reshape(query_count, per_query, places)
     every_place = lax.dot_general(
-        query_unit, back_unit, (((1,), (1,)), ((), ())), preferred_element_type=jnp.float32
+        query_unit, back_scaled.astype(jnp.bfloat16), (((1,), (1,)), ((), ())),
+        preferred_element_type=jnp.float32,
     )
-    hard_part = jnp.sum(jnp.where(slot_grid, every_place[:, None, :], 0.0), axis=2)
-    shard_scores, negative_scores = (
-        lax.psum(local_part.astype(jnp.bfloat16), "section").astype(jnp.float32),
-        lax.psum(hard_part.astype(jnp.bfloat16), "section").astype(jnp.float32),
+    hard_dot = jnp.sum(jnp.where(slot_grid, every_place[:, None, :], 0.0), axis=2)
+    summed = lax.psum(
+        jnp.concatenate([jnp.sum(back_scaled * back_scaled, axis=1), hard_dot.reshape(-1)]), "section"
     )
+    back_squares, hard_dot = summed[:places], summed[places:].reshape(query_count, per_query)
+    back_norm = jnp.sqrt(back_squares + EPSILON)
+    back_unit = (back_scaled / back_norm[:, None]).astype(jnp.bfloat16)
+    slot_norm = jnp.sum(jnp.where(slot_grid, back_norm[None, None, :], 0.0), axis=2)
+    negative_scores = hard_dot / jnp.where(hard_valid > 0, slot_norm, 1.0)
     shard_gradients, negative_gradients = softmax_grads(
         shard_scores, negative_scores, positive_tool, hard_valid
     )
@@ -120,7 +129,11 @@
     gain_terms = jnp.sum(query_back * query_hidden.astype(jnp.float32), axis=0) + jnp.sum(
         tool_back * tool_hidden.astype(jnp.float32), axis=0
     )
-    gain_grad = lax.psum(lax.psum(lax.psum(gain_terms, "dc"), "dy"), "dz")
+    chunks = gain_terms.reshape(group_size, -1)
+    owned = jnp.sum(lax.all_to_all(chunks, DP, 0, 0, tiled=True), axis=0)
+    gain_grad = lax.all_to_all(
+        jnp.broadcast_to(owned[None, :], chunks.shape), DP, 0, 0, tiled=True
+    ).reshape(-1)
     return (query_grad, tool_grad, gain_grad)
 
 

time: 330 us -> 338 us (1.024); the launches traced: 326 us -> 338 us
  blocking collectives: 48.6 us -> 68.6 us
  starting transfers between devices: 34.4 us -> 21.1 us
  other arithmetic: 15.8 us -> 20 us
    all_to_all x0 -> x2, blocking collectives: none -> 40 us  [the longest x1 22.3 us: body(): indices = lax.all_to_all(requests, DP, 0, 0, tiled=True).reshape(-1)]
    psum x4 -> x1, blocking collectives: 32.1 us -> 13.4 us  [body(): lax.psum(jnp.concatenate([jnp.sum(back_scaled * back_scaled, axis=1), har...]
    all_to_all x1, waiting for transfers between devices: 43.9 us -> 33.8 us  [body(): lax.all_to_all(answers.reshape(group_size, capacity, features), DP, 0, 0,...]
    all_to_all x1, starting transfers between devices: 13.1 us -> 4.72 us  [body(): lax.all_to_all(jnp.broadcast_to(owned[None, :], chunks.shape), DP, 0, 0,...]
    all_to_all x1, waiting for transfers between devices: 0.01 us -> 8.29 us  [body(): lax.all_to_all(jnp.broadcast_to(owned[None, :], chunks.shape), DP, 0, 0,...]
    all_to_all x1, starting transfers between devices: 12.3 us -> 5.83 us  [body(): lax.all_to_all(answers.reshape(group_size, capacity, features), DP, 0, 0,...]
  transfers between devices with their start and end apart: 4 -> 4, of which waited for: 3 -> 4; matrix products, arithmetic and copies ran while one was open for 4% -> 4% of each run, Pallas kernels for 0% -> 0%
where the time goes in v4:
time: 338 us
  waiting for transfers between devices  176 us (52%)
  blocking collectives  68.6 us (20%)
  matrix products  31 us (9%)
  starting transfers between devices  21.1 us (6%)
  other arithmetic  20 us (6%)
  between operations  14.3 us (4%)
  local copies, waits for them, and re-layouts  6.85 us (2%)
    all_to_all x1, waiting for transfers between devices, body(): lax.all_to_all(sent_terms.reshape(group_size, capacity, features), DP, 0,...  87.2 us
    psum x1, waiting for transfers between devices, body(): lax.psum(local_part.astype(jnp.bfloat16), 'section').astype(jnp.float32)  46.7 us
    all_to_all x1, waiting for transfers between devices, body(): lax.all_to_all(answers.reshape(group_size, capacity, features), DP, 0, 0,...  33.8 us
    all_to_all x1, blocking collectives, body(): indices = lax.all_to_all(requests, DP, 0, 0, tiled=True).reshape(-1)  22.3 us
    all_to_all x1, blocking collectives, body(): owned = jnp.sum(lax.all_to_all(chunks, DP, 0, 0, tiled=True), axis=0)  17.7 us
    psum x1, blocking collectives, body(): lax.psum(jnp.concatenate([jnp.sum(back_scaled * back_scaled, axis=1), har...  13.4 us
    all_to_all x1, starting transfers between devices, body(): lax.all_to_all(sent_terms.reshape(group_size, capacity, features), DP, 0,...  10.5 us
    psum x1, blocking collectives, body(): lax.psum((jnp.sum(query_scaled * query_scaled, axis=1), jnp.sum(tool_scal...  9.27 us
  transfers between devices with their start and end apart: 4, of which 4 were waited for; matrix products, arithmetic and copies ran while one was open for 4% of the time, Pallas kernels for 0%

profile of v4, /device:TPU:1, one launch (start us, length us, event | category | flops | bytes accessed | tf_op | source)
XLA Modules:
  0.0 337.8 jit_solution(10886067817928339671)
XLA Ops:
  7.2 0.8 copy.26
  9.2 0.8 copy.25
  10.9 1.1 select_reduce_fusion.3
  12.1 22.3 %all_to_all.31 = s32[64,1,32]{2,1,0:T(1,128)S(1)} all-to-all(s32[64,1,32]{2,1,0:T(1,128)S(1)} %bitcast.16), channel_id=1, replica_groups=mesh['dz'=8,'dy'=4,'dc'=2,'section'=4] {'dz','dy','dc'}, dimensions={0} | all-to-all | bytes 16384 | tf_op jit(solution)/shard_map/all_to_all | solution.py:55
  35.7 5.2 %fusion.8 = bf16[2048,1024]{1,0:T(8,128)(2,1)} fusion(bf16[512,1024]{1,0:T(8,128)(2,1)} %param.8, s32[2048]{0:T(1024)S(1)} %eq.62), kind=kOutput, calls=%fused_computation.19 | convolution fusion | flops 2150629376 | bytes 5251072 | tf_op jit(solution)/shard_map/dot_general | solution.py:59
  40.9 5.8 %all-to-all-start.1 = ((bf16[64,32,1024]{2,1,0:T(8,128)(2,1)}), bf16[64,32,1024]{2,1,0:T(8,128)(2,1)}, u32[]{:S(2)}, u32[]{:S(2)}) async-start(bf16[64,32,1024]{2,1,0:T(8,128)(2,1)} %bitcast.14), calls=%async_computation.1 | async-start | bytes 8388608 | tf_op jit(solution)/shard_map/all_to_all | solution.py:60
  47.5 9.3 %all-reduce.1 = (f32[512]{0:T(512)S(1)}, f32[512]{0:T(512)S(1)}) all-reduce(f32[512]{0:T(512)S(1)} %get-tuple-element.14, f32[512]{0:T(512)S(1)} %get-tuple-element.13), channel_id=1, replica_groups=mesh['dz'=8,'dy'=4,'dc'=2,'section'=4] {'section'}, use_global_device_ids=true, to_apply=%region_3.4 | all-reduce | flops 1024 | bytes 8192 | tf_op jit(solution)/shard_map/psum | solution.py:66
  57.1 1.0 copy-done.5
  58.1 1.6 convolution_convert_fusion.1
  60.1 46.7 %all-reduce.4.cloned.1.call-done = bf16[512,512]{1,0:T(8,128)(2,1)} async-done(((bf16[512,512]{1,0:T(8,128)(2,1)}), bf16[512,512]{1,0:T(8,128)(2,1)}) %all-reduce.4.cloned.1.call-update) | async-done | bytes 524304 | tf_op jit(solution)/shard_map/psum | solution.py:80
  106.7 1.2 convert_element_type.64
  107.9 33.8 %all-to-all-done.1 = bf16[64,32,1024]{2,1,0:T(8,128)(2,1)} async-done(((bf16[64,32,1024]{2,1,0:T(8,128)(2,1)}), bf16[64,32,1024]{2,1,0:T(8,128)(2,1)}, u32[]{:S(2)}, u32[]{:S(2)}) %all-to-all-start.1) | async-done | bytes 4194336 | tf_op jit(solution)/shard_map/all_to_all | solution.py:60
  141.7 3.4 %multiply_reduce_fusion = f32[2048]{0:T(1024)S(1)} fusion(bf16[2048,1024]{1,0:T(8,128)(2,1)} %bitcast.2, f32[1024]{0:T(1024)S(1)} %copy-done.9), kind=kLoop, calls=%fused_computation.5 | loop fusion | flops 8386560 | bytes 4206592 | tf_op jit(solution)/shard_map/reduce_sum | solution.py:91
  145.1 4.6 %fusion.1 = f32[512,2048]{1,0:T(8,128)S(1)} fusion(bf16[512,1024]{1,0:T(8,128)(2,1)S(1)} %copy-done.6, bf16[2048,1024]{1,0:T(8,128)(2,1)} %bitcast.2, f32[1024]{0:T(1024)S(1)} %copy-done.9), kind=kOutput, calls=%fused_computation.10 | convolution fusion | flops 2153775104 | bytes 9441280 | tf_op jit(solution)/shard_map/dot_general | solution.py:85
  149.7 1.4 select_reduce_fusion.2
  151.4 13.4 %psum.45 = f32[3072]{0:T(1024)S(1)} all-reduce(f32[3072]{0:T(1024)S(1)} %pad_maximum_fusion), channel_id=1, replica_groups=mesh['dz'=8,'dy'=4,'dc'=2,'section'=4] {'section'}, use_global_device_ids=true, to_apply=%region_11.12 | all-reduce | flops 3072 | bytes 24576 | tf_op jit(solution)/shard_map/psum | solution.py:90
  165.1 1.2 select_reduce_fusion.1
  166.8 1.9 select_reduce_fusion
  168.8 4.4 %convolution_convert_fusion = bf16[2048,1024]{1,0:T(8,128)(2,1)} fusion(bf16[512,1024]{1,0:T(8,128)(2,1)S(1)} %copy-done.7, bf16[512,2048]{1,0:T(8,128)(2,1)S(1)} %select_reduce_fusion), kind=kOutput, calls=%fused_computation.20 | convolution fusion | flops 2149580800 | bytes 7340032 | tf_op jit(solution)/shard_map/dot_general | solution.py:105
  173.1 10.5 %all-to-all-start.2 = ((bf16[64,32,1024]{2,1,0:T(8,128)(2,1)}), bf16[64,32,1024]{2,1,0:T(8,128)(2,1)}, u32[]{:S(2)}, u32[]{:S(2)}) async-start(bf16[64,32,1024]{2,1,0:T(8,128)(2,1)} %bitcast.15), calls=%async_computation.2 | async-start | bytes 8388608 | tf_op jit(solution)/shard_map/all_to_all | solution.py:108
  183.6 5.3 %fusion.6 = f32[512,1024]{1,0:T(8,128)S(1)} fusion(bf16[2048,1024]{1,0:T(8,128)(2,1)} %bitcast.2, f32[2048]{0:T(1024)S(1)} %fusion.24, f32[1024]{0:T(1024)S(1)} %copy-done.9, bf16[512,2048]{1,0:T(8,128)(2,1)} %copy-done.4), kind=kOutput, calls=%fused_computation.17 | convolution fusion | flops 2155872256 | bytes 8400896 | tf_op jit(solution)/shard_map/dot_general | solution.py:113
  188.9 2.4 convolution_add_fusion.1
  191.3 87.2 %all-to-all-done.2 = bf16[64,32,1024]{2,1,0:T(8,128)(2,1)} async-done(((bf16[64,32,1024]{2,1,0:T(8,128)(2,1)}), bf16[64,32,1024]{2,1,0:T(8,128)(2,1)}, u32[]{:S(2)}, u32[]{:S(2)}) %all-to-all-start.2) | async-done | bytes 4194336 | tf_op jit(solution)/shard_map/all_to_all | solution.py:108
  278.5 4.8 %fusion.4 = f32[512,1024]{1,0:T(8,128)S(1)} fusion(bf16[2048,1024]{1,0:T(8,128)(2,1)} %bitcast.4, s32[2048]{0:T(1024)S(1)} %eq.62), kind=kOutput, calls=%fused_computation.13 | convolution fusion | flops 2148532224 | bytes 6299648 | tf_op jit(solution)/shard_map/dot_general | solution.py:117
  283.3 2.8 multiply_reduce_fusion.1
  286.1 6.0 %all-reduce = (f32[512]{0:T(512)S(1)}, f32[512]{0:T(512)S(1)}) all-reduce(f32[512]{0:T(512)S(1)} %get-tuple-element.12, f32[512]{0:T(512)S(1)} %get-tuple-element.11), channel_id=1, replica_groups=mesh['dz'=8,'dy'=4,'dc'=2,'section'=4] {'section'}, use_global_device_ids=true, to_apply=%region_16.17 | all-reduce | flops 1024 | bytes 8192 | tf_op jit(solution)/shard_map/psum | solution.py:121
  292.1 2.4 fusion.16
  294.5 1.9 fusion.15
  296.4 17.7 %all_to_all.32 = f32[64,1,16]{2,1,0:T(1,128)S(1)} all-to-all(f32[64,1,16]{2,1,0:T(1,128)S(1)} %bitcast.17), channel_id=1, replica_groups=mesh['dz'=8,'dy'=4,'dc'=2,'section'=4] {'dz','dy','dc'}, dimensions={0} | all-to-all | bytes 8192 | tf_op jit(solution)/shard_map/all_to_all | solution.py:133
  314.8 4.7 %all-to-all-start.4 = ((f32[64,1,16]{2,1,0:T(1,128)}), f32[64,1,16]{2,1,0:T(1,128)S(1)}, u32[]{:S(2)}, u32[]{:S(2)}) async-start(f32[64,1,16]{2,1,0:T(1,128)} %broadcast_in_dim.117), calls=%async_computation.4 | async-start | bytes 65536 | tf_op jit(solution)/shard_map/all_to_all | solution.py:134
  319.5 1.2 multiply_convert_fusion.1
  320.8 8.3 %all-to-all-done.4 = f32[64,1,16]{2,1,0:T(1,128)S(1)} async-done(((f32[64,1,16]{2,1,0:T(1,128)}), f32[64,1,16]{2,1,0:T(1,128)S(1)}, u32[]{:S(2)}, u32[]{:S(2)}) %all-to-all-start.4) | async-done | bytes 4128 | tf_op jit(solution)/shard_map/all_to_all | solution.py:134
  (63 shorter events, 8.6 us)
Async XLA Ops:
  40.9 5.9 %copy-start = (bf16[512,1024]{1,0:T(8,128)(2,1)S(1)}, bf16[512,1024]{1,0:T(8,128)(2,1)}, u32[]{:S(2)}) copy-start(bf16[512,1024]{1,0:T(8,128)(2,1)} %param.7) | copy-start | bytes 3145732
  40.9 5.9 %copy-start.1 = (bf16[512,1024]{1,0:T(8,128)(2,1)S(1)}, bf16[512,1024]{1,0:T(8,128)(2,1)}, u32[]{:S(2)}) copy-start(bf16[512,1024]{1,0:T(8,128)(2,1)} %param.8) | copy-start | bytes 3145732
  40.9 5.9 %copy-start.9 = (f32[1024]{0:T(1024)S(1)}, f32[1024]{0:T(1024)}, u32[]{:S(2)}) copy-start(f32[1024]{0:T(1024)} %param.9) | copy-start | bytes 12292
  40.9 100.7 %all-to-all-start.1 = ((bf16[64,32,1024]{2,1,0:T(8,128)(2,1)}), bf16[64,32,1024]{2,1,0:T(8,128)(2,1)}, u32[]{:S(2)}, u32[]{:S(2)}) async-start(bf16[64,32,1024]{2,1,0:T(8,128)(2,1)} %bitcast.14), calls=%async_computation.1 | async-start | bytes 8388608 | tf_op jit(solution)/shard_map/all_to_all | solution.py:60
  46.8 60.0 %all-reduce.4.cloned.1.call-start = ((), (), s32[]{:S(2)}) async-start(), calls=%async_computation.5 | async-start | bytes 1048576 | tf_op jit(solution)/shard_map/psum | solution.py:80
  57.1 1.0 copy-start.5
  58.1 2.0 copy-start.10
  58.1 2.0 copy-start.11
  141.7 3.4 %copy-start.6 = (bf16[512,1024]{1,0:T(8,128)(2,1)S(1)}, bf16[512,1024]{1,0:T(8,128)(2,1)}, u32[]{:S(2)}) copy-start(bf16[512,1024]{1,0:T(8,128)(2,1)} %copy-done.5) | copy-start | bytes 3145732
  149.7 16.7 %copy-start.12 = (s32[512]{0:T(512)S(1)}, s32[512]{0:T(512)}, u32[]{:S(2)}) copy-start(s32[512]{0:T(512)} %param.10) | copy-start | bytes 6148
  165.1 3.6 %copy-start.7 = (bf16[512,1024]{1,0:T(8,128)(2,1)S(1)}, bf16[512,1024]{1,0:T(8,128)(2,1)}, u32[]{:S(2)}) copy-start(bf16[512,1024]{1,0:T(8,128)(2,1)} %copy-done.5) | copy-start | bytes 3145732
  168.7 4.4 %copy-start.4 = (bf16[512,2048]{1,0:T(8,128)(2,1)}, bf16[512,2048]{1,0:T(8,128)(2,1)S(1)}, u32[]{:S(2)}) copy-start(bf16[512,2048]{1,0:T(8,128)(2,1)S(1)} %select_reduce_fusion) | copy-start | bytes 6291460
  173.1 105.4 %all-to-all-start.2 = ((bf16[64,32,1024]{2,1,0:T(8,128)(2,1)}), bf16[64,32,1024]{2,1,0:T(8,128)(2,1)}, u32[]{:S(2)}, u32[]{:S(2)}) async-start(bf16[64,32,1024]{2,1,0:T(8,128)(2,1)} %bitcast.15), calls=%async_computation.2 | async-start | bytes 8388608 | tf_op jit(solution)/shard_map/all_to_all | solution.py:108
  278.5 4.8 %copy-start.2 = (f32[512,1024]{1,0:T(8,128)S(1)}, f32[512,1024]{1,0:T(8,128)}, u32[]{:S(2)}) copy-start(f32[512,1024]{1,0:T(8,128)} %convolution_add_fusion.1) | copy-start | bytes 6291460
  278.5 4.8 %copy-start.8 = (bf16[512,1024]{1,0:T(8,128)(2,1)S(1)}, bf16[512,1024]{1,0:T(8,128)(2,1)}, u32[]{:S(2)}) copy-start(bf16[512,1024]{1,0:T(8,128)(2,1)} %copy-done.5) | copy-start | bytes 3145732
  292.1 2.4 copy-start.3
  314.8 14.2 %all-to-all-start.4 = ((f32[64,1,16]{2,1,0:T(1,128)}), f32[64,1,16]{2,1,0:T(1,128)S(1)}, u32[]{:S(2)}, u32[]{:S(2)}) async-start(f32[64,1,16]{2,1,0:T(1,128)} %broadcast_in_dim.117), calls=%async_computation.4 | async-start | bytes 65536 | tf_op jit(solution)/shard_map/all_to_all | solution.py:134
Sparse Core Ops, SparseCore 0:
  59.9 46.8 all-reduce.3

commit v5 on v3

--- a/solution.py
+++ b/solution.py
@@ -120,7 +120,8 @@
     gain_terms = jnp.sum(query_back * query_hidden.astype(jnp.float32), axis=0) + jnp.sum(
         tool_back * tool_hidden.astype(jnp.float32), axis=0
     )
-    gain_grad = lax.psum(lax.psum(lax.psum(gain_terms, "dc"), "dy"), "dz")
+    everyone = jnp.broadcast_to(gain_terms[None, :], (group_size, gain_terms.shape[0]))
+    gain_grad = jnp.sum(lax.all_to_all(everyone, DP, 0, 0, tiled=True), axis=0)
     return (query_grad, tool_grad, gain_grad)
 
 

time: 330 us -> 323 us (0.979); the launches traced: 326 us -> 322 us
  blocking collectives: 48.6 us -> 22.9 us
  waiting for transfers between devices: 178 us -> 190 us
  starting transfers between devices: 34.4 us -> 43.1 us
    psum x3 -> x0, blocking collectives: 25.9 us -> none  [body(): gain_grad = lax.psum(lax.psum(lax.psum(gain_terms, 'dc'), 'dy'), 'dz')]
    all_to_all x0 -> x1, waiting for transfers between devices: none -> 11.8 us  [body(): gain_grad = jnp.sum(lax.all_to_all(everyone, DP, 0, 0, tiled=True), axis=0)]
    all_to_all x0 -> x1, starting transfers between devices: none -> 8.74 us  [body(): gain_grad = jnp.sum(lax.all_to_all(everyone, DP, 0, 0, tiled=True), axis=0)]
  transfers between devices with their start and end apart: 4 -> 5, of which waited for: 3 -> 4; matrix products, arithmetic and copies ran while one was open for 4% -> 5% of each run, Pallas kernels for 0% -> 0%
where the time goes in v5:
time: 323 us; the launch traced here: 322 us
  waiting for transfers between devices  190 us (59%)
  starting transfers between devices  43.1 us (13%)
  matrix products  30.2 us (9%)
  blocking collectives  22.9 us (7%)
  other arithmetic  16.5 us (5%)
  between operations  14.3 us (4%)
  local copies, waits for them, and re-layouts  4.84 us (1%)
    all_to_all x1, waiting for transfers between devices, body(): lax.all_to_all(sent_terms.reshape(group_size, capacity, features), DP, 0,...  87.2 us
    psum x1, waiting for transfers between devices, body(): lax.psum(local_part.astype(jnp.bfloat16), 'section').astype(jnp.float32)  47.2 us
    all_to_all x1, waiting for transfers between devices, body(): lax.all_to_all(answers.reshape(group_size, capacity, features), DP, 0, 0,...  43.9 us
    all_to_all x1, starting transfers between devices, body(): indices = lax.all_to_all(requests, DP, 0, 0, tiled=True).reshape(-1)  13.1 us
    all_to_all x1, starting transfers between devices, body(): lax.all_to_all(answers.reshape(group_size, capacity, features), DP, 0, 0,...  12.3 us
    all_to_all x1, waiting for transfers between devices, body(): gain_grad = jnp.sum(lax.all_to_all(everyone, DP, 0, 0, tiled=True), axis=0)  11.8 us
    all_to_all x1, starting transfers between devices, body(): lax.all_to_all(sent_terms.reshape(group_size, capacity, features), DP, 0,...  8.84 us
    psum x1, blocking collectives, body(): lax.psum((jnp.sum(query_scaled * query_scaled, axis=1), jnp.sum(tool_scal...  8.77 us
  transfers between devices with their start and end apart: 5, of which 4 were waited for; matrix products, arithmetic and copies ran while one was open for 5% of the time, Pallas kernels for 0%

profile of v5, /device:TPU:1, one launch (start us, length us, event | category | flops | bytes accessed | tf_op | source)
XLA Modules:
  0.0 322.1 jit_solution(10352026346735568732)
XLA Ops:
  7.2 0.8 broadcast_compare_fusion
  8.4 0.8 copy.31
  9.4 0.8 copy.28
  11.0 1.1 select_reduce_fusion.2
  12.8 13.1 %all-to-all-start = ((s32[64,1,32]{2,1,0:T(1,128)}), s32[64,1,32]{2,1,0:T(1,128)S(1)}, u32[]{:S(2)}, u32[]{:S(2)}) async-start(s32[64,1,32]{2,1,0:T(1,128)} %bitcast), calls=%async_computation | async-start | bytes 65536 | tf_op jit(solution)/shard_map/all_to_all | solution.py:55
  26.0 2.2 fusion.9
  28.1 8.8 %all-reduce.1 = (f32[512]{0:T(512)S(1)}, f32[512]{0:T(512)S(1)}) all-reduce(f32[512]{0:T(512)S(1)} %get-tuple-element.8, f32[512]{0:T(512)S(1)} %get-tuple-element.7), channel_id=1, replica_groups=mesh['dz'=8,'dy'=4,'dc'=2,'section'=4] {'section'}, use_global_device_ids=true, to_apply=%region_3.4 | all-reduce | flops 1024 | bytes 8192 | tf_op jit(solution)/shard_map/psum | solution.py:59
  38.2 4.2 %fusion.3 = bf16[2048,1024]{1,0:T(8,128)(2,1)} fusion(s32[2048]{0:T(1024)S(1)} %eq.70, bf16[512,1024]{1,0:T(8,128)(2,1)S(1)} %copy-done.1, f32[512]{0:T(512)S(1)} %add_sqrt_fusion, f32[1024]{0:T(1024)S(1)} %copy-done.7), kind=kOutput, calls=%fused_computation.11 | convolution fusion | flops 2152726528 | bytes 5257216 | tf_op jit(solution)/shard_map/dot_general | solution.py:72
  42.5 12.3 %all-to-all-start.1 = ((bf16[64,32,1024]{2,1,0:T(8,128)(2,1)}), bf16[64,32,1024]{2,1,0:T(8,128)(2,1)}, u32[]{:S(2)}, u32[]{:S(2)}) async-start(bf16[64,32,1024]{2,1,0:T(8,128)(2,1)} %bitcast.10), calls=%async_computation.1 | async-start | bytes 8388608 | tf_op jit(solution)/shard_map/all_to_all | solution.py:73
  54.9 1.6 convolution_convert_fusion.1
  56.9 47.2 %all-reduce.4.cloned.1.call-done = bf16[512,512]{1,0:T(8,128)(2,1)} async-done(((bf16[512,512]{1,0:T(8,128)(2,1)}), bf16[512,512]{1,0:T(8,128)(2,1)}) %all-reduce.4.cloned.1.call-update) | async-done | bytes 524304 | tf_op jit(solution)/shard_map/psum | solution.py:86
  104.1 1.5 fusion.16
  105.6 43.9 %all-to-all-done.1 = bf16[64,32,1024]{2,1,0:T(8,128)(2,1)} async-done(((bf16[64,32,1024]{2,1,0:T(8,128)(2,1)}), bf16[64,32,1024]{2,1,0:T(8,128)(2,1)}, u32[]{:S(2)}, u32[]{:S(2)}) %all-to-all-start.1) | async-done | bytes 4194336 | tf_op jit(solution)/shard_map/all_to_all | solution.py:73
  149.5 4.6 %fusion.37 = f32[512,2048]{1,0:T(8,128)S(1)} fusion(bf16[2048,1024]{1,0:T(8,128)(2,1)} %bitcast.2, f32[512]{0:T(512)S(1)} %add_sqrt_fusion.1, f32[1024]{0:T(1024)S(1)} %copy-done.7, bf16[512,1024]{1,0:T(8,128)(2,1)S(1)} %copy-done), kind=kOutput, calls=%fused_computation.65 | convolution fusion | flops 2149580800 | bytes 9443328 | tf_op jit(solution)/shard_map/dot_general | solution.py:81
  154.1 1.4 select_reduce_fusion.1
  155.5 6.2 %psum.45 = bf16[512,2]{0,1:T(2,128)(2,1)S(1)} all-reduce(bf16[512,2]{0,1:T(2,128)(2,1)S(1)} %select_reduce_fusion.1), channel_id=1, replica_groups=mesh['dz'=8,'dy'=4,'dc'=2,'section'=4] {'section'}, use_global_device_ids=true, to_apply=%region_10.11 | all-reduce | flops 1024 | bytes 4096 | tf_op jit(solution)/shard_map/psum | solution.py:87
  161.8 1.9 select_reduce_fusion
  163.7 4.5 %convolution_convert_fusion = bf16[2048,1024]{1,0:T(8,128)(2,1)} fusion(bf16[512,2048]{1,0:T(8,128)(2,1)S(1)} %select_reduce_fusion, f32[512]{0:T(512)S(1)} %add_sqrt_fusion.1, f32[1024]{0:T(1024)S(1)} %copy-done.7, bf16[512,1024]{1,0:T(8,128)(2,1)S(1)} %copy-done), kind=kOutput, calls=%fused_computation.12 | convolution fusion | flops 2151677952 | bytes 7346176 | tf_op jit(solution)/shard_map/dot_general | solution.py:96
  168.2 8.8 %all-to-all-start.2 = ((bf16[64,32,1024]{2,1,0:T(8,128)(2,1)}), bf16[64,32,1024]{2,1,0:T(8,128)(2,1)}, u32[]{:S(2)}, u32[]{:S(2)}) async-start(bf16[64,32,1024]{2,1,0:T(8,128)(2,1)} %bitcast.11), calls=%async_computation.2 | async-start | bytes 8388608 | tf_op jit(solution)/shard_map/all_to_all | solution.py:99
  177.0 5.2 %fusion.40 = f32[512,1024]{1,0:T(8,128)S(1)} fusion(bf16[512,2048]{1,0:T(8,128)(2,1)} %copy-done.4, bf16[2048,1024]{1,0:T(8,128)(2,1)} %bitcast.2), kind=kOutput, calls=%fused_computation.66 | convolution fusion | flops 2147483648 | bytes 8388608 | tf_op jit(solution)/shard_map/dot_general | solution.py:104
  182.2 2.4 convolution_add_fusion.1
  184.7 87.2 %all-to-all-done.2 = bf16[64,32,1024]{2,1,0:T(8,128)(2,1)} async-done(((bf16[64,32,1024]{2,1,0:T(8,128)(2,1)}), bf16[64,32,1024]{2,1,0:T(8,128)(2,1)}, u32[]{:S(2)}, u32[]{:S(2)}) %all-to-all-start.2) | async-done | bytes 4194336 | tf_op jit(solution)/shard_map/all_to_all | solution.py:99
  271.9 4.8 %fusion = f32[512,1024]{1,0:T(8,128)S(1)} fusion(bf16[2048,1024]{1,0:T(8,128)(2,1)} %bitcast.4, s32[2048]{0:T(1024)S(1)} %eq.70), kind=kOutput, calls=%fused_computation.6 | convolution fusion | flops 2148532224 | bytes 6299648 | tf_op jit(solution)/shard_map/dot_general | solution.py:108
  276.7 2.9 multiply_reduce_fusion
  279.6 7.9 %all-reduce = (f32[512]{0:T(512)S(1)}, f32[512]{0:T(512)S(1)}) all-reduce(f32[512]{0:T(512)S(1)} %get-tuple-element.6, f32[512]{0:T(512)S(1)} %get-tuple-element.5), channel_id=1, replica_groups=mesh['dz'=8,'dy'=4,'dc'=2,'section'=4] {'section'}, use_global_device_ids=true, to_apply=%region_14.15 | all-reduce | flops 1024 | bytes 8192 | tf_op jit(solution)/shard_map/psum | solution.py:112
  287.5 2.4 fusion.11
  289.9 1.9 fusion.10
  291.8 0.8 broadcast_in_dim.99
  292.6 8.7 %all-to-all-start.3 = ((f32[64,1,1024]{2,1,0:T(1,128)}), f32[64,1,1024]{2,1,0:T(1,128)S(1)}, u32[]{:S(2)}, u32[]{:S(2)}) async-start(f32[64,1,1024]{2,1,0:T(1,128)} %broadcast_in_dim.99), calls=%async_computation.3 | async-start | bytes 524288 | tf_op jit(solution)/shard_map/all_to_all | solution.py:124
  301.4 1.2 multiply_convert_fusion.1
  302.6 11.8 %all-to-all-done.3 = f32[64,1,1024]{2,1,0:T(1,128)S(1)} async-done(((f32[64,1,1024]{2,1,0:T(1,128)}), f32[64,1,1024]{2,1,0:T(1,128)S(1)}, u32[]{:S(2)}, u32[]{:S(2)}) %all-to-all-start.3) | async-done | bytes 262176 | tf_op jit(solution)/shard_map/all_to_all | solution.py:124
  314.4 0.8 reduce_sum.142
  (42 shorter events, 3.9 us)
Async XLA Ops:
  7.2 31.1 %copy-start.7 = (f32[1024]{0:T(1024)S(1)}, f32[1024]{0:T(1024)}, u32[]{:S(2)}) copy-start(f32[1024]{0:T(1024)} %param.9) | copy-start | bytes 12292
  7.2 31.1 %copy-start.1 = (bf16[512,1024]{1,0:T(8,128)(2,1)S(1)}, bf16[512,1024]{1,0:T(8,128)(2,1)}, u32[]{:S(2)}) copy-start(bf16[512,1024]{1,0:T(8,128)(2,1)} %param.8) | copy-start | bytes 3145732
  12.8 24.1 %all-to-all-start = ((s32[64,1,32]{2,1,0:T(1,128)}), s32[64,1,32]{2,1,0:T(1,128)S(1)}, u32[]{:S(2)}, u32[]{:S(2)}) async-start(s32[64,1,32]{2,1,0:T(1,128)} %bitcast), calls=%async_computation | async-start | bytes 65536 | tf_op jit(solution)/shard_map/all_to_all | solution.py:55
  42.5 12.4 %copy-start = (bf16[512,1024]{1,0:T(8,128)(2,1)S(1)}, bf16[512,1024]{1,0:T(8,128)(2,1)}, u32[]{:S(2)}) copy-start(bf16[512,1024]{1,0:T(8,128)(2,1)} %param.7) | copy-start | bytes 3145732
  42.5 107.1 %all-to-all-start.1 = ((bf16[64,32,1024]{2,1,0:T(8,128)(2,1)}), bf16[64,32,1024]{2,1,0:T(8,128)(2,1)}, u32[]{:S(2)}, u32[]{:S(2)}) async-start(bf16[64,32,1024]{2,1,0:T(8,128)(2,1)} %bitcast.10), calls=%async_computation.1 | async-start | bytes 8388608 | tf_op jit(solution)/shard_map/all_to_all | solution.py:73
  54.8 49.3 %all-reduce.4.cloned.1.call-start = ((), (), s32[]{:S(2)}) async-start(), calls=%async_computation.4 | async-start | bytes 1048576 | tf_op jit(solution)/shard_map/psum | solution.py:86
  54.9 2.0 copy-start.6
  54.9 2.0 copy-start.8
  54.9 49.2 %copy-start.9 = (s32[512]{0:T(512)S(1)}, s32[512]{0:T(512)}, u32[]{:S(2)}) copy-start(s32[512]{0:T(512)} %param.10) | copy-start | bytes 6148
  163.7 4.5 %copy-start.4 = (bf16[512,2048]{1,0:T(8,128)(2,1)}, bf16[512,2048]{1,0:T(8,128)(2,1)S(1)}, u32[]{:S(2)}) copy-start(bf16[512,2048]{1,0:T(8,128)(2,1)S(1)} %select_reduce_fusion) | copy-start | bytes 6291460
  168.2 103.8 %all-to-all-start.2 = ((bf16[64,32,1024]{2,1,0:T(8,128)(2,1)}), bf16[64,32,1024]{2,1,0:T(8,128)(2,1)}, u32[]{:S(2)}, u32[]{:S(2)}) async-start(bf16[64,32,1024]{2,1,0:T(8,128)(2,1)} %bitcast.11), calls=%async_computation.2 | async-start | bytes 8388608 | tf_op jit(solution)/shard_map/all_to_all | solution.py:99
  177.0 5.2 %copy-start.5 = (bf16[512,512]{1,0:T(8,128)(2,1)S(1)}, bf16[512,512]{1,0:T(8,128)(2,1)}, u32[]{:S(2)}) copy-start(bf16[512,512]{1,0:T(8,128)(2,1)} %all-reduce.4.cloned.1.call-done) | copy-start | bytes 1572868
  271.9 4.8 %copy-start.2 = (f32[512,1024]{1,0:T(8,128)S(1)}, f32[512,1024]{1,0:T(8,128)}, u32[]{:S(2)}) copy-start(f32[512,1024]{1,0:T(8,128)} %convolution_add_fusion.1) | copy-start | bytes 6291460
  287.5 2.4 copy-start.3
  292.6 21.8 %all-to-all-start.3 = ((f32[64,1,1024]{2,1,0:T(1,128)}), f32[64,1,1024]{2,1,0:T(1,128)S(1)}, u32[]{:S(2)}, u32[]{:S(2)}) async-start(f32[64,1,1024]{2,1,0:T(1,128)} %broadcast_in_dim.99), calls=%async_computation.3 | async-start | bytes 524288 | tf_op jit(solution)/shard_map/all_to_all | solution.py:124
Sparse Core Ops, SparseCore 0:
  58.6 45.5 all-reduce.3

commit v6 on v5

--- a/solution.py
+++ b/solution.py
@@ -31,6 +31,13 @@
     return (shard_gradients, negative_gradients)
 
 
+def section_sum(value):
+    parts = lax.axis_size("section")
+    flat = value.reshape(-1)
+    gathered = lax.all_to_all(jnp.broadcast_to(flat[None, :], (parts, flat.shape[0])), "section", 0, 0, tiled=True)
+    return jnp.sum(gathered.astype(jnp.float32), axis=0).reshape(value.shape)
+
+
 def body(query_hidden, tool_hidden, norm_gain, positive_tool, hard_owner, hard_row, hard_valid):
     query_count, features = query_hidden.shape
     tool_count = tool_hidden.shape[0]
@@ -56,10 +63,10 @@
 
     query_scaled = query_hidden.astype(jnp.float32) * norm_gain
     tool_scaled = tool_hidden.astype(jnp.float32) * norm_gain
-    query_squares, tool_squares = lax.psum(
-        (jnp.sum(query_scaled * query_scaled, axis=1), jnp.sum(tool_scaled * tool_scaled, axis=1)),
-        "section",
+    squares = section_sum(
+        jnp.stack([jnp.sum(query_scaled * query_scaled, axis=1), jnp.sum(tool_scaled * tool_scaled, axis=1)])
     )
+    query_squares, tool_squares = squares[0], squares[1]
     query_norm = jnp.sqrt(query_squares + EPSILON)
     tool_norm = jnp.sqrt(tool_squares + EPSILON)
     query_unit32 = query_scaled / query_norm[:, None]
@@ -84,7 +91,7 @@
     hard_part = jnp.sum(jnp.where(slot_grid, every_place[:, None, :], 0.0), axis=2)
     shard_scores, negative_scores = (
         lax.psum(local_part.astype(jnp.bfloat16), "section").astype(jnp.float32),
-        lax.psum(hard_part.astype(jnp.bfloat16), "section").astype(jnp.float32),
+        section_sum(hard_part.astype(jnp.bfloat16)),
     )
     shard_gradients, negative_gradients = softmax_grads(
         shard_scores, negative_scores, positive_tool, hard_valid
@@ -109,10 +116,10 @@
         pick_tool, arrived_terms, (((0,), (0,)), ((), ())), preferred_element_type=jnp.float32
     )
 
-    query_inner, tool_inner = lax.psum(
-        (jnp.sum(query_unit32 * query_pull, axis=1), jnp.sum(tool_unit32 * tool_pull, axis=1)),
-        "section",
+    inner = section_sum(
+        jnp.stack([jnp.sum(query_unit32 * query_pull, axis=1), jnp.sum(tool_unit32 * tool_pull, axis=1)])
     )
+    query_inner, tool_inner = inner[0], inner[1]
     query_back = (query_pull - query_unit32 * query_inner[:, None]) / query_norm[:, None]
     tool_back = (tool_pull - tool_unit32 * tool_inner[:, None]) / tool_norm[:, None]
     query_grad = (query_back * norm_gain).astype(jnp.bfloat16)

time: 323 us -> 324 us (level)
  blocking collectives: 22.9 us -> 6.56 us
  waiting for transfers between devices: 190 us -> 206 us
    all_to_all x1, waiting for transfers between devices: 43.9 us -> 92.9 us  [body(): lax.all_to_all(answers.reshape(group_size, capacity, features), DP, 0, 0,...]
    psum x1, waiting for transfers between devices: 47.2 us -> 0.02 us  [body(): lax.psum(local_part.astype(jnp.bfloat16), 'section').astype(jnp.float32)]
    psum x3 -> x0, blocking collectives: 22.9 us -> none  [the longest x1 8.77 us: body(): lax.psum((jnp.sum(query_scaled * query_scaled, axis=1), jnp.sum(tool_scal...]
    all_to_all x1, waiting for transfers between devices: 0.01 us -> 9.28 us  [body(): indices = lax.all_to_all(requests, DP, 0, 0, tiled=True).reshape(-1)]
    all_to_all x0 -> x2, starting transfers between devices: none -> 8.26 us  [section_sum(): lax.all_to_all(jnp.broadcast_to(flat[None, :], (parts, flat.shape[0])), '...]
    all_to_all x0 -> x1, blocking collectives: none -> 6.56 us  [section_sum(): lax.all_to_all(jnp.broadcast_to(flat[None, :], (parts, flat.shape[0])), '...]
    all_to_all x1, starting transfers between devices: 12.3 us -> 5.83 us  [body(): lax.all_to_all(answers.reshape(group_size, capacity, features), DP, 0, 0,...]
  transfers between devices with their start and end apart: 5 -> 7, of which waited for: 4 -> 6; matrix products, arithmetic and copies ran while one was open for 5% -> 7% of each run, Pallas kernels for 0% -> 0%
where the time goes in v6:
time: 324 us
  waiting for transfers between devices  206 us (64%)
  starting transfers between devices  43.9 us (14%)
  matrix products  30 us (9%)
  other arithmetic  16.6 us (5%)
  between operations  14.4 us (4%)
  blocking collectives  6.56 us (2%)
  local copies, waits for them, and re-layouts  6.46 us (2%)
    all_to_all x1, waiting for transfers between devices, body(): lax.all_to_all(answers.reshape(group_size, capacity, features), DP, 0, 0,...  92.9 us
    all_to_all x1, waiting for transfers between devices, body(): lax.all_to_all(sent_terms.reshape(group_size, capacity, features), DP, 0,...  88.4 us
    all_to_all x1, starting transfers between devices, body(): indices = lax.all_to_all(requests, DP, 0, 0, tiled=True).reshape(-1)  13.8 us
    all_to_all x1, waiting for transfers between devices, body(): gain_grad = jnp.sum(lax.all_to_all(everyone, DP, 0, 0, tiled=True), axis=0)  11.8 us
    all_to_all x1, waiting for transfers between devices, body(): indices = lax.all_to_all(requests, DP, 0, 0, tiled=True).reshape(-1)  9.28 us
    all_to_all x2, starting transfers between devices, section_sum(): lax.all_to_all(jnp.broadcast_to(flat[None, :], (parts, flat.shape[0])), '...  8.26 us
    all_to_all x1, starting transfers between devices, body(): lax.all_to_all(sent_terms.reshape(group_size, capacity, features), DP, 0,...  8.18 us
    all_to_all x1, starting transfers between devices, body(): gain_grad = jnp.sum(lax.all_to_all(everyone, DP, 0, 0, tiled=True), axis=0)  7.88 us
  transfers between devices with their start and end apart: 7, of which 6 were waited for; matrix products, arithmetic and copies ran while one was open for 7% of the time, Pallas kernels for 0%

profile of v6, /device:TPU:1, one launch (start us, length us, event | category | flops | bytes accessed | tf_op | source)
XLA Modules:
  0.0 323.6 jit_solution(442092413464434784)
XLA Ops:
  7.2 2.3 fusion.9
  10.1 4.8 %all-to-all-start = ((f32[4,1,1024]{2,1,0:T(1,128)}), f32[4,1,1024]{2,1,0:T(1,128)S(1)}, u32[]{:S(2)}, u32[]{:S(2)}) async-start(f32[4,1,1024]{2,1,0:T(1,128)} %broadcast_in_dim.106), calls=%async_computation | async-start | bytes 32768 | tf_op jit(solution)/shard_map/all_to_all | solution.py:37
  16.6 1.1 select_reduce_fusion.2
  18.4 0.7 all-to-all-done
  19.2 13.8 %all-to-all-start.1 = ((s32[64,1,32]{2,1,0:T(1,128)}), s32[64,1,32]{2,1,0:T(1,128)S(1)}, u32[]{:S(2)}, u32[]{:S(2)}) async-start(s32[64,1,32]{2,1,0:T(1,128)} %bitcast.2), calls=%async_computation.1 | async-start | bytes 65536 | tf_op jit(solution)/shard_map/all_to_all | solution.py:62
  33.0 9.3 %all-to-all-done.1 = s32[64,1,32]{2,1,0:T(1,128)S(1)} async-done(((s32[64,1,32]{2,1,0:T(1,128)}), s32[64,1,32]{2,1,0:T(1,128)S(1)}, u32[]{:S(2)}, u32[]{:S(2)}) %all-to-all-start.1) | async-done | bytes 8224 | tf_op jit(solution)/shard_map/all_to_all | solution.py:62
  42.8 0.7 reduce.7
  43.6 4.2 %fusion.3 = bf16[2048,1024]{1,0:T(8,128)(2,1)} fusion(s32[2048]{0:T(1024)S(1)} %eq.70, bf16[512,1024]{1,0:T(8,128)(2,1)S(1)} %copy-done.1, f32[512]{0:T(512)S(1)} %get-tuple-element.19, f32[1024]{0:T(1024)S(1)} %copy-done.7), kind=kOutput, calls=%fused_computation.11 | convolution fusion | flops 2152726528 | bytes 5257216 | tf_op jit(solution)/shard_map/dot_general | solution.py:79
  47.8 5.8 %all-to-all-start.2 = ((bf16[64,32,1024]{2,1,0:T(8,128)(2,1)}), bf16[64,32,1024]{2,1,0:T(8,128)(2,1)}, u32[]{:S(2)}, u32[]{:S(2)}) async-start(bf16[64,32,1024]{2,1,0:T(8,128)(2,1)} %bitcast.20), calls=%async_computation.2 | async-start | bytes 8388608 | tf_op jit(solution)/shard_map/all_to_all | solution.py:80
  54.0 1.6 convolution_convert_fusion.1
  55.7 92.9 %all-to-all-done.2 = bf16[64,32,1024]{2,1,0:T(8,128)(2,1)} async-done(((bf16[64,32,1024]{2,1,0:T(8,128)(2,1)}), bf16[64,32,1024]{2,1,0:T(8,128)(2,1)}, u32[]{:S(2)}, u32[]{:S(2)}) %all-to-all-start.2) | async-done | bytes 4194336 | tf_op jit(solution)/shard_map/all_to_all | solution.py:80
  148.6 4.6 %fusion.37 = f32[512,2048]{1,0:T(8,128)S(1)} fusion(bf16[2048,1024]{1,0:T(8,128)(2,1)} %bitcast.4, f32[512]{0:T(512)S(1)} %get-tuple-element.18, f32[1024]{0:T(1024)S(1)} %copy-done.7, bf16[512,1024]{1,0:T(8,128)(2,1)S(1)} %copy-done), kind=kOutput, calls=%fused_computation.69 | convolution fusion | flops 2149580800 | bytes 9443328 | tf_op jit(solution)/shard_map/dot_general | solution.py:88
  153.1 1.4 select_reduce_fusion.1
  156.8 3.4 %all-to-all-start.3 = ((bf16[4,2,512]{2,1,0:T(2,128)(2,1)}), bf16[4,2,512]{2,1,0:T(2,128)(2,1)S(1)}, u32[]{:S(2)}, u32[]{:S(2)}) async-start(bf16[4,2,512]{2,1,0:T(2,128)(2,1)} %reshape.157), calls=%async_computation.3 | async-start | bytes 16384 | tf_op jit(solution)/shard_map/all_to_all | solution.py:37
  160.2 1.5 fusion.16
  161.7 2.4 all-to-all-done.3
  164.6 1.9 select_reduce_fusion
  166.5 4.5 %convolution_convert_fusion = bf16[2048,1024]{1,0:T(8,128)(2,1)} fusion(bf16[512,2048]{1,0:T(8,128)(2,1)S(1)} %select_reduce_fusion, f32[512]{0:T(512)S(1)} %get-tuple-element.18, f32[1024]{0:T(1024)S(1)} %copy-done.7, bf16[512,1024]{1,0:T(8,128)(2,1)S(1)} %copy-done), kind=kOutput, calls=%fused_computation.12 | convolution fusion | flops 2151677952 | bytes 7346176 | tf_op jit(solution)/shard_map/dot_general | solution.py:103
  171.0 8.2 %all-to-all-start.4 = ((bf16[64,32,1024]{2,1,0:T(8,128)(2,1)}), bf16[64,32,1024]{2,1,0:T(8,128)(2,1)}, u32[]{:S(2)}, u32[]{:S(2)}) async-start(bf16[64,32,1024]{2,1,0:T(8,128)(2,1)} %bitcast.21), calls=%async_computation.4 | async-start | bytes 8388608 | tf_op jit(solution)/shard_map/all_to_all | solution.py:106
  179.1 6.5 %fusion.41 = f32[512,1024]{1,0:T(8,128)} fusion(bf16[512,2048]{1,0:T(8,128)(2,1)} %copy-done.4, bf16[2048,1024]{1,0:T(8,128)(2,1)} %bitcast.4), kind=kOutput, calls=%fused_computation.71 | convolution fusion | flops 2147483648 | bytes 8388608 | tf_op jit(solution)/shard_map/dot_general | solution.py:111
  185.7 88.4 %all-to-all-done.4 = bf16[64,32,1024]{2,1,0:T(8,128)(2,1)} async-done(((bf16[64,32,1024]{2,1,0:T(8,128)(2,1)}), bf16[64,32,1024]{2,1,0:T(8,128)(2,1)}, u32[]{:S(2)}, u32[]{:S(2)}) %all-to-all-start.4) | async-done | bytes 4194336 | tf_op jit(solution)/shard_map/all_to_all | solution.py:106
  274.1 4.7 %fusion = f32[512,1024]{1,0:T(8,128)S(1)} fusion(bf16[2048,1024]{1,0:T(8,128)(2,1)} %bitcast.7, s32[2048]{0:T(1024)S(1)} %eq.70), kind=kOutput, calls=%fused_computation.6 | convolution fusion | flops 2148532224 | bytes 6299648 | tf_op jit(solution)/shard_map/dot_general | solution.py:115
  278.8 1.1 convolution_add_fusion
  280.4 2.9 multiply_reduce_fusion.1
  283.3 6.6 %all_to_all.43 = f32[4,1,1024]{2,1,0:T(1,128)S(1)} all-to-all(f32[4,1,1024]{2,1,0:T(1,128)S(1)} %broadcast_in_dim.120), channel_id=1, replica_groups=mesh['dz'=8,'dy'=4,'dc'=2,'section'=4] {'section'}, dimensions={0} | all-to-all | bytes 32768 | tf_op jit(solution)/shard_map/all_to_all | solution.py:37
  289.9 2.4 fusion.11
  292.3 1.9 fusion.10
  294.1 0.8 broadcast_in_dim.121
  295.0 7.9 %all-to-all-start.6 = ((f32[64,1,1024]{2,1,0:T(1,128)}), f32[64,1,1024]{2,1,0:T(1,128)S(1)}, u32[]{:S(2)}, u32[]{:S(2)}) async-start(f32[64,1,1024]{2,1,0:T(1,128)} %broadcast_in_dim.121), calls=%async_computation.6 | async-start | bytes 524288 | tf_op jit(solution)/shard_map/all_to_all | solution.py:131
  302.9 1.2 multiply_convert_fusion.1
  304.1 11.8 %all-to-all-done.6 = f32[64,1,1024]{2,1,0:T(1,128)S(1)} async-done(((f32[64,1,1024]{2,1,0:T(1,128)}), f32[64,1,1024]{2,1,0:T(1,128)S(1)}, u32[]{:S(2)}, u32[]{:S(2)}) %all-to-all-start.6) | async-done | bytes 262176 | tf_op jit(solution)/shard_map/all_to_all | solution.py:131
  315.9 0.8 reduce_sum.172
  (67 shorter events, 7.2 us)
Async XLA Ops:
  7.2 36.4 %copy-start.7 = (f32[1024]{0:T(1024)S(1)}, f32[1024]{0:T(1024)}, u32[]{:S(2)}) copy-start(f32[1024]{0:T(1024)} %param.9) | copy-start | bytes 12292
  7.2 36.4 %copy-start.1 = (bf16[512,1024]{1,0:T(8,128)(2,1)S(1)}, bf16[512,1024]{1,0:T(8,128)(2,1)}, u32[]{:S(2)}) copy-start(bf16[512,1024]{1,0:T(8,128)(2,1)} %param.8) | copy-start | bytes 3145732
  7.2 7.8 %copy-start.6 = (s32[512,2]{0,1:T(2,128)S(1)}, s32[512,2]{0,1:T(2,128)}, u32[]{:S(2)}) copy-start(s32[512,2]{0,1:T(2,128)} %param.13) | copy-start | bytes 12292
  7.2 8.1 %copy-start.9 = (s32[512,2]{0,1:T(2,128)S(1)}, s32[512,2]{0,1:T(2,128)}, u32[]{:S(2)}) copy-start(s32[512,2]{0,1:T(2,128)} %param.12) | copy-start | bytes 12292
  7.2 8.5 %copy-start.8 = (s32[512,2]{0,1:T(2,128)S(1)}, s32[512,2]{0,1:T(2,128)}, u32[]{:S(2)}) copy-start(s32[512,2]{0,1:T(2,128)} %param.11) | copy-start | bytes 12292
  10.1 9.0 %all-to-all-start = ((f32[4,1,1024]{2,1,0:T(1,128)}), f32[4,1,1024]{2,1,0:T(1,128)S(1)}, u32[]{:S(2)}, u32[]{:S(2)}) async-start(f32[4,1,1024]{2,1,0:T(1,128)} %broadcast_in_dim.106), calls=%async_computation | async-start | bytes 32768 | tf_op jit(solution)/shard_map/all_to_all | solution.py:37
  19.2 23.1 %all-to-all-start.1 = ((s32[64,1,32]{2,1,0:T(1,128)}), s32[64,1,32]{2,1,0:T(1,128)S(1)}, u32[]{:S(2)}, u32[]{:S(2)}) async-start(s32[64,1,32]{2,1,0:T(1,128)} %bitcast.2), calls=%async_computation.1 | async-start | bytes 65536 | tf_op jit(solution)/shard_map/all_to_all | solution.py:62
  47.8 6.2 %copy-start = (bf16[512,1024]{1,0:T(8,128)(2,1)S(1)}, bf16[512,1024]{1,0:T(8,128)(2,1)}, u32[]{:S(2)}) copy-start(bf16[512,1024]{1,0:T(8,128)(2,1)} %param.7) | copy-start | bytes 3145732
  47.8 100.7 %all-to-all-start.2 = ((bf16[64,32,1024]{2,1,0:T(8,128)(2,1)}), bf16[64,32,1024]{2,1,0:T(8,128)(2,1)}, u32[]{:S(2)}, u32[]{:S(2)}) async-start(bf16[64,32,1024]{2,1,0:T(8,128)(2,1)} %bitcast.20), calls=%async_computation.2 | async-start | bytes 8388608 | tf_op jit(solution)/shard_map/all_to_all | solution.py:80
  53.6 106.6 %all-reduce.2.cloned.1.call-start = ((), (), s32[]{:S(2)}) async-start(), calls=%async_computation.7 | async-start | bytes 1048576 | tf_op jit(solution)/shard_map/psum | solution.py:93
  153.1 7.1 %copy-start.10 = (s32[512]{0:T(512)S(1)}, s32[512]{0:T(512)}, u32[]{:S(2)}) copy-start(s32[512]{0:T(512)} %param.10) | copy-start | bytes 6148
  156.8 7.4 %all-to-all-start.3 = ((bf16[4,2,512]{2,1,0:T(2,128)(2,1)}), bf16[4,2,512]{2,1,0:T(2,128)(2,1)S(1)}, u32[]{:S(2)}, u32[]{:S(2)}) async-start(bf16[4,2,512]{2,1,0:T(2,128)(2,1)} %reshape.157), calls=%async_computation.3 | async-start | bytes 16384 | tf_op jit(solution)/shard_map/all_to_all | solution.py:37
  166.5 4.5 %copy-start.4 = (bf16[512,2048]{1,0:T(8,128)(2,1)}, bf16[512,2048]{1,0:T(8,128)(2,1)S(1)}, u32[]{:S(2)}) copy-start(bf16[512,2048]{1,0:T(8,128)(2,1)S(1)} %select_reduce_fusion) | copy-start | bytes 6291460
  171.0 103.1 %all-to-all-start.4 = ((bf16[64,32,1024]{2,1,0:T(8,128)(2,1)}), bf16[64,32,1024]{2,1,0:T(8,128)(2,1)}, u32[]{:S(2)}, u32[]{:S(2)}) async-start(bf16[64,32,1024]{2,1,0:T(8,128)(2,1)} %bitcast.21), calls=%async_computation.4 | async-start | bytes 8388608 | tf_op jit(solution)/shard_map/all_to_all | solution.py:106
  274.1 4.7 %copy-start.5 = (bf16[512,512]{1,0:T(8,128)(2,1)S(1)}, bf16[512,512]{1,0:T(8,128)(2,1)}, u32[]{:S(2)}) copy-start(bf16[512,512]{1,0:T(8,128)(2,1)} %all-reduce.2.cloned.1.call-done) | copy-start | bytes 1572868
  278.8 1.6 copy-start.11
  280.4 2.9 copy-start.3
  289.9 2.4 copy-start.2
  295.0 21.0 %all-to-all-start.6 = ((f32[64,1,1024]{2,1,0:T(1,128)}), f32[64,1,1024]{2,1,0:T(1,128)S(1)}, u32[]{:S(2)}, u32[]{:S(2)}) async-start(f32[64,1,1024]{2,1,0:T(1,128)} %broadcast_in_dim.121), calls=%async_computation.6 | async-start | bytes 524288 | tf_op jit(solution)/shard_map/all_to_all | solution.py:131
Sparse Core Ops, SparseCore 0:
  57.4 46.4 all-reduce.1

commit v7 on v6

--- a/solution.py
+++ b/solution.py
@@ -63,10 +63,10 @@
 
     query_scaled = query_hidden.astype(jnp.float32) * norm_gain
     tool_scaled = tool_hidden.astype(jnp.float32) * norm_gain
-    squares = section_sum(
-        jnp.stack([jnp.sum(query_scaled * query_scaled, axis=1), jnp.sum(tool_scaled * tool_scaled, axis=1)])
+    query_squares, tool_squares = lax.psum(
+        (jnp.sum(query_scaled * query_scaled, axis=1), jnp.sum(tool_scaled * tool_scaled, axis=1)),
+        "section",
     )
-    query_squares, tool_squares = squares[0], squares[1]
     query_norm = jnp.sqrt(query_squares + EPSILON)
     tool_norm = jnp.sqrt(tool_squares + EPSILON)
     query_unit32 = query_scaled / query_norm[:, None]
@@ -81,6 +81,12 @@
         answers.reshape(group_size, capacity, features), DP, 0, 0, tiled=True
     ).reshape(places, features)
 
+    slot_of_query = slot_at.reshape(query_count, per_query, places).any(axis=1)
+    placed_queries = lax.dot_general(
+        slot_of_query.astype(jnp.bfloat16), query_unit, (((0,), (0,)), ((), ())),
+        preferred_element_type=jnp.float32,
+    ).astype(jnp.bfloat16)
+    back_unit, placed_queries = lax.optimization_barrier((back_unit, placed_queries))
     local_part = lax.dot_general(
         query_unit, tool_unit, (((1,), (1,)), ((), ())), preferred_element_type=jnp.float32
     )
@@ -100,9 +106,8 @@
         jnp.where(slot_grid, negative_gradients.astype(jnp.float32)[:, :, None], 0.0), axis=1
     ).astype(jnp.bfloat16)
 
-    sent_terms = lax.dot_general(
-        spread_grads, query_unit, (((0,), (0,)), ((), ())), preferred_element_type=jnp.float32
-    ).astype(jnp.bfloat16)
+    place_grads = jnp.sum(spread_grads.astype(jnp.float32), axis=0)
+    sent_terms = (place_grads[:, None] * placed_queries.astype(jnp.float32)).astype(jnp.bfloat16)
     arrived_terms = lax.all_to_all(
         sent_terms.reshape(group_size, capacity, features), DP, 0, 0, tiled=True
     ).reshape(places, features)

time: 324 us -> 324 us (level)
  waiting for transfers between devices: 206 us -> 190 us
  blocking collectives: 6.56 us -> 15.3 us
  other arithmetic: 16.6 us -> 21.4 us
    all_to_all x1, waiting for transfers between devices: 9.28 us -> 0.01 us  [body(): indices = lax.all_to_all(requests, DP, 0, 0, tiled=True).reshape(-1)]
    psum x0 -> x1, blocking collectives: none -> 8.77 us  [body(): lax.psum((jnp.sum(query_scaled * query_scaled, axis=1), jnp.sum(tool_scal...]
    all_to_all x1, starting transfers between devices: 5.83 us -> 12.3 us  [body(): lax.all_to_all(answers.reshape(group_size, capacity, features), DP, 0, 0,...]
    all_to_all x1, waiting for transfers between devices: 92.9 us -> 86.8 us  [body(): lax.all_to_all(answers.reshape(group_size, capacity, features), DP, 0, 0,...]
    all_to_all x2 -> x1, starting transfers between devices: 8.26 us -> 3.25 us  [section_sum(): lax.all_to_all(jnp.broadcast_to(flat[None, :], (parts, flat.shape[0])), '...]
  transfers between devices with their start and end apart: 7 -> 6, of which waited for: 6 -> 4; matrix products, arithmetic and copies ran while one was open for 7% -> 8% of each run, Pallas kernels for 0% -> 0%
where the time goes in v7:
time: 324 us
  waiting for transfers between devices  190 us (59%)
  starting transfers between devices  45.1 us (14%)
  matrix products  29.4 us (9%)
  other arithmetic  21.4 us (7%)
  blocking collectives  15.3 us (5%)
  between operations  14.4 us (4%)
  local copies, waits for them, and re-layouts  7.62 us (2%)
    all_to_all x1, waiting for transfers between devices, body(): lax.all_to_all(sent_terms.reshape(group_size, capacity, features), DP, 0,...  89 us
    all_to_all x1, waiting for transfers between devices, body(): lax.all_to_all(answers.reshape(group_size, capacity, features), DP, 0, 0,...  86.8 us
    all_to_all x1, starting transfers between devices, body(): indices = lax.all_to_all(requests, DP, 0, 0, tiled=True).reshape(-1)  13.1 us
    all_to_all x1, starting transfers between devices, body(): lax.all_to_all(answers.reshape(group_size, capacity, features), DP, 0, 0,...  12.3 us
    all_to_all x1, waiting for transfers between devices, body(): gain_grad = jnp.sum(lax.all_to_all(everyone, DP, 0, 0, tiled=True), axis=0)  11.8 us
    psum x1, blocking collectives, body(): lax.psum((jnp.sum(query_scaled * query_scaled, axis=1), jnp.sum(tool_scal...  8.77 us
    all_to_all x1, starting transfers between devices, body(): lax.all_to_all(sent_terms.reshape(group_size, capacity, features), DP, 0,...  8.26 us
    all_to_all x1, starting transfers between devices, body(): gain_grad = jnp.sum(lax.all_to_all(everyone, DP, 0, 0, tiled=True), axis=0)  7.88 us
  transfers between devices with their start and end apart: 6, of which 4 were waited for; matrix products, arithmetic and copies ran while one was open for 8% of the time, Pallas kernels for 0%

profile of v7, /device:TPU:1, one launch (start us, length us, event | category | flops | bytes accessed | tf_op | source)
XLA Modules:
  0.0 323.6 jit_solution(14656758460625550027)
XLA Ops:
  7.2 0.9 copy.44
  10.0 0.8 copy.47
  11.0 1.1 select_reduce_fusion.2
  12.8 13.1 %all-to-all-start = ((s32[64,1,32]{2,1,0:T(1,128)}), s32[64,1,32]{2,1,0:T(1,128)S(1)}, u32[]{:S(2)}, u32[]{:S(2)}) async-start(s32[64,1,32]{2,1,0:T(1,128)} %bitcast), calls=%async_computation | async-start | bytes 65536 | tf_op jit(solution)/shard_map/all_to_all | solution.py:62
  26.0 2.2 fusion.10
  28.1 8.8 %all-reduce = (f32[512]{0:T(512)S(1)}, f32[512]{0:T(512)S(1)}) all-reduce(f32[512]{0:T(512)S(1)} %get-tuple-element.12, f32[512]{0:T(512)S(1)} %get-tuple-element.11), channel_id=1, replica_groups=mesh['dz'=8,'dy'=4,'dc'=2,'section'=4] {'section'}, use_global_device_ids=true, to_apply=%region_3.4 | all-reduce | flops 1024 | bytes 8192 | tf_op jit(solution)/shard_map/psum | solution.py:66
  38.2 4.2 %fusion.4 = bf16[2048,1024]{1,0:T(8,128)(2,1)} fusion(s32[2048]{0:T(1024)S(1)} %eq.70, bf16[512,1024]{1,0:T(8,128)(2,1)S(1)} %copy-done.2, f32[512]{0:T(512)S(1)} %add_sqrt_fusion, f32[1024]{0:T(1024)S(1)} %copy-done.8), kind=kOutput, calls=%fused_computation.14 | convolution fusion | flops 2152726528 | bytes 5257216 | tf_op jit(solution)/shard_map/dot_general | solution.py:79
  42.5 12.3 %all-to-all-start.1 = ((bf16[64,32,1024]{2,1,0:T(8,128)(2,1)}), bf16[64,32,1024]{2,1,0:T(8,128)(2,1)}, u32[]{:S(2)}, u32[]{:S(2)}) async-start(bf16[64,32,1024]{2,1,0:T(8,128)(2,1)} %bitcast.16), calls=%async_computation.1 | async-start | bytes 8388608 | tf_op jit(solution)/shard_map/all_to_all | solution.py:80
  55.1 1.7 convolution_convert_fusion.1
  57.1 1.1 fusion
  58.3 4.5 %convolution_convert_fusion = bf16[2048,1024]{1,0:T(8,128)(2,1)} fusion(pred[512,2048]{1,0:T(8,128)(4,1)S(1)} %fusion, f32[512]{0:T(512)S(1)} %add_sqrt_fusion.1, f32[1024]{0:T(1024)S(1)} %copy-done.8, bf16[512,1024]{1,0:T(8,128)(2,1)S(1)} %copy-done.1), kind=kOutput, calls=%fused_computation.15 | convolution fusion | flops 2151677952 | bytes 6297600 | tf_op jit(solution)/shard_map/dot_general | solution.py:85
  62.7 86.8 %all-to-all-done.1 = bf16[64,32,1024]{2,1,0:T(8,128)(2,1)} async-done(((bf16[64,32,1024]{2,1,0:T(8,128)(2,1)}), bf16[64,32,1024]{2,1,0:T(8,128)(2,1)}, u32[]{:S(2)}, u32[]{:S(2)}) %all-to-all-start.1) | async-done | bytes 4194336 | tf_op jit(solution)/shard_map/all_to_all | solution.py:80
  149.5 4.6 %fusion.36 = f32[512,2048]{1,0:T(8,128)S(1)} fusion(bf16[2048,1024]{1,0:T(8,128)(2,1)} %bitcast.2, f32[512]{0:T(512)S(1)} %add_sqrt_fusion.1, f32[1024]{0:T(1024)S(1)} %copy-done.8, bf16[512,1024]{1,0:T(8,128)(2,1)S(1)} %copy-done.1), kind=kOutput, calls=%fused_computation.70 | convolution fusion | flops 2149580800 | bytes 9443328 | tf_op jit(solution)/shard_map/dot_general | solution.py:94
  154.1 1.4 select_reduce_fusion.1
  157.8 3.2 %all-to-all-start.2 = ((bf16[4,2,512]{2,1,0:T(2,128)(2,1)}), bf16[4,2,512]{2,1,0:T(2,128)(2,1)S(1)}, u32[]{:S(2)}, u32[]{:S(2)}) async-start(bf16[4,2,512]{2,1,0:T(2,128)(2,1)} %reshape.140), calls=%async_computation.2 | async-start | bytes 16384 | tf_op jit(solution)/shard_map/all_to_all | solution.py:37
  161.1 1.5 fusion.17
  162.6 2.6 all-to-all-done.2
  165.6 1.9 select_reduce_fusion
  167.9 2.7 multiply_convert_fusion
  170.6 8.3 %all-to-all-start.3 = ((bf16[64,32,1024]{2,1,0:T(8,128)(2,1)}), bf16[64,32,1024]{2,1,0:T(8,128)(2,1)}, u32[]{:S(2)}, u32[]{:S(2)}) async-start(bf16[64,32,1024]{2,1,0:T(8,128)(2,1)} %bitcast.15), calls=%async_computation.3 | async-start | bytes 8388608 | tf_op jit(solution)/shard_map/all_to_all | solution.py:111
  178.8 5.9 %fusion.41 = f32[512,1024]{1,0:T(8,128)} fusion(bf16[512,2048]{1,0:T(8,128)(2,1)S(1)} %select_reduce_fusion, bf16[2048,1024]{1,0:T(8,128)(2,1)} %bitcast.2), kind=kOutput, calls=%fused_computation.72 | convolution fusion | flops 2147483648 | bytes 8388608 | tf_op jit(solution)/shard_map/dot_general | solution.py:116
  184.7 89.0 %all-to-all-done.3 = bf16[64,32,1024]{2,1,0:T(8,128)(2,1)} async-done(((bf16[64,32,1024]{2,1,0:T(8,128)(2,1)}), bf16[64,32,1024]{2,1,0:T(8,128)(2,1)}, u32[]{:S(2)}, u32[]{:S(2)}) %all-to-all-start.3) | async-done | bytes 4194336 | tf_op jit(solution)/shard_map/all_to_all | solution.py:111
  273.7 4.7 %fusion.1 = f32[512,1024]{1,0:T(8,128)S(1)} fusion(bf16[2048,1024]{1,0:T(8,128)(2,1)} %bitcast.5, s32[2048]{0:T(1024)S(1)} %eq.70), kind=kOutput, calls=%fused_computation.9 | convolution fusion | flops 2148532224 | bytes 6299648 | tf_op jit(solution)/shard_map/dot_general | solution.py:120
  278.5 1.1 convolution_add_fusion
  280.4 2.9 multiply_reduce_fusion.1
  283.3 6.6 %all_to_all.37 = f32[4,1,1024]{2,1,0:T(1,128)S(1)} all-to-all(f32[4,1,1024]{2,1,0:T(1,128)S(1)} %broadcast_in_dim.112), channel_id=1, replica_groups=mesh['dz'=8,'dy'=4,'dc'=2,'section'=4] {'section'}, dimensions={0} | all-to-all | bytes 32768 | tf_op jit(solution)/shard_map/all_to_all | solution.py:37
  289.9 2.4 fusion.12
  292.3 1.9 fusion.11
  294.2 0.8 broadcast_in_dim.113
  295.0 7.9 %all-to-all-start.5 = ((f32[64,1,1024]{2,1,0:T(1,128)}), f32[64,1,1024]{2,1,0:T(1,128)S(1)}, u32[]{:S(2)}, u32[]{:S(2)}) async-start(f32[64,1,1024]{2,1,0:T(1,128)} %broadcast_in_dim.113), calls=%async_computation.5 | async-start | bytes 524288 | tf_op jit(solution)/shard_map/all_to_all | solution.py:136
  302.9 1.2 multiply_convert_fusion.2
  304.1 11.8 %all-to-all-done.5 = f32[64,1,1024]{2,1,0:T(1,128)S(1)} async-done(((f32[64,1,1024]{2,1,0:T(1,128)}), f32[64,1,1024]{2,1,0:T(1,128)S(1)}, u32[]{:S(2)}, u32[]{:S(2)}) %all-to-all-start.5) | async-done | bytes 262176 | tf_op jit(solution)/shard_map/all_to_all | solution.py:136
  (66 shorter events, 9.3 us)
Async XLA Ops:
  7.2 31.1 %copy-start.2 = (bf16[512,1024]{1,0:T(8,128)(2,1)S(1)}, bf16[512,1024]{1,0:T(8,128)(2,1)}, u32[]{:S(2)}) copy-start(bf16[512,1024]{1,0:T(8,128)(2,1)} %param.8) | copy-start | bytes 3145732
  7.2 31.1 %copy-start.8 = (f32[1024]{0:T(1024)S(1)}, f32[1024]{0:T(1024)}, u32[]{:S(2)}) copy-start(f32[1024]{0:T(1024)} %param.9) | copy-start | bytes 12292
  12.8 24.1 %all-to-all-start = ((s32[64,1,32]{2,1,0:T(1,128)}), s32[64,1,32]{2,1,0:T(1,128)S(1)}, u32[]{:S(2)}, u32[]{:S(2)}) async-start(s32[64,1,32]{2,1,0:T(1,128)} %bitcast), calls=%async_computation | async-start | bytes 65536 | tf_op jit(solution)/shard_map/all_to_all | solution.py:62
  42.5 12.6 %copy-start.1 = (bf16[512,1024]{1,0:T(8,128)(2,1)S(1)}, bf16[512,1024]{1,0:T(8,128)(2,1)}, u32[]{:S(2)}) copy-start(bf16[512,1024]{1,0:T(8,128)(2,1)} %param.7) | copy-start | bytes 3145732
  42.5 107.1 %all-to-all-start.1 = ((bf16[64,32,1024]{2,1,0:T(8,128)(2,1)}), bf16[64,32,1024]{2,1,0:T(8,128)(2,1)}, u32[]{:S(2)}, u32[]{:S(2)}) async-start(bf16[64,32,1024]{2,1,0:T(8,128)(2,1)} %bitcast.16), calls=%async_computation.1 | async-start | bytes 8388608 | tf_op jit(solution)/shard_map/all_to_all | solution.py:80
  54.8 106.2 %all-reduce.3.cloned.1.call-start = ((), (), s32[]{:S(2)}) async-start(), calls=%async_computation.6 | async-start | bytes 1048576 | tf_op jit(solution)/shard_map/psum | solution.py:99
  55.1 2.0 copy-start.7
  55.1 2.0 copy-start.9
  154.1 6.9 %copy-start.10 = (s32[512]{0:T(512)S(1)}, s32[512]{0:T(512)}, u32[]{:S(2)}) copy-start(s32[512]{0:T(512)} %param.10) | copy-start | bytes 6148
  157.8 7.4 %all-to-all-start.2 = ((bf16[4,2,512]{2,1,0:T(2,128)(2,1)}), bf16[4,2,512]{2,1,0:T(2,128)(2,1)S(1)}, u32[]{:S(2)}, u32[]{:S(2)}) async-start(bf16[4,2,512]{2,1,0:T(2,128)(2,1)} %reshape.140), calls=%async_computation.2 | async-start | bytes 16384 | tf_op jit(solution)/shard_map/all_to_all | solution.py:37
  165.6 2.3 copy-start
  170.6 103.2 %all-to-all-start.3 = ((bf16[64,32,1024]{2,1,0:T(8,128)(2,1)}), bf16[64,32,1024]{2,1,0:T(8,128)(2,1)}, u32[]{:S(2)}, u32[]{:S(2)}) async-start(bf16[64,32,1024]{2,1,0:T(8,128)(2,1)} %bitcast.15), calls=%async_computation.3 | async-start | bytes 8388608 | tf_op jit(solution)/shard_map/all_to_all | solution.py:111
  273.7 4.7 %copy-start.6 = (bf16[512,512]{1,0:T(8,128)(2,1)S(1)}, bf16[512,512]{1,0:T(8,128)(2,1)}, u32[]{:S(2)}) copy-start(bf16[512,512]{1,0:T(8,128)(2,1)} %all-reduce.3.cloned.1.call-done) | copy-start | bytes 1572868
  278.4 1.2 copy-start.3
  278.5 1.9 copy-start.11
  280.4 2.9 copy-start.5
  289.9 2.4 copy-start.4
  295.0 21.0 %all-to-all-start.5 = ((f32[64,1,1024]{2,1,0:T(1,128)}), f32[64,1,1024]{2,1,0:T(1,128)S(1)}, u32[]{:S(2)}, u32[]{:S(2)}) async-start(f32[64,1,1024]{2,1,0:T(1,128)} %broadcast_in_dim.113), calls=%async_computation.5 | async-start | bytes 524288 | tf_op jit(solution)/shard_map/all_to_all | solution.py:136
Sparse Core Ops, SparseCore 0:
  58.6 45.5 all-reduce.2

commit v8 on v3

--- a/solution.py
+++ b/solution.py
@@ -120,7 +120,10 @@
     gain_terms = jnp.sum(query_back * query_hidden.astype(jnp.float32), axis=0) + jnp.sum(
         tool_back * tool_hidden.astype(jnp.float32), axis=0
     )
-    gain_grad = lax.psum(lax.psum(lax.psum(gain_terms, "dc"), "dy"), "dz")
+    pair_terms = lax.psum(gain_terms, "dc")
+    chips = lax.axis_size(DP[:2])
+    everyone = jnp.broadcast_to(pair_terms[None, :], (chips, gain_terms.shape[0]))
+    gain_grad = jnp.sum(lax.all_to_all(everyone, DP[:2], 0, 0, tiled=True), axis=0)
     return (query_grad, tool_grad, gain_grad)
 
 

time: 330 us -> 320 us (0.970); the launches traced: 326 us -> 320 us
  blocking collectives: 48.6 us -> 29 us
  waiting for transfers between devices: 178 us -> 186 us
  starting transfers between devices: 34.4 us -> 38.7 us
    psum x3 -> x1, blocking collectives: 25.9 us -> 6.09 us  [body(): pair_terms = lax.psum(gain_terms, 'dc')]
    all_to_all x0 -> x1, waiting for transfers between devices: none -> 8.12 us  [body(): lax.all_to_all(everyone, DP[:2], 0, 0, tiled=True)]
    all_to_all x0 -> x1, starting transfers between devices: none -> 4.3 us  [body(): lax.all_to_all(everyone, DP[:2], 0, 0, tiled=True)]
  transfers between devices with their start and end apart: 4 -> 5, of which waited for: 3 -> 4; matrix products, arithmetic and copies ran while one was open for 4% -> 5% of each run, Pallas kernels for 0% -> 0%
where the time goes in v8:
time: 320 us
  waiting for transfers between devices  186 us (58%)
  starting transfers between devices  38.7 us (12%)
  matrix products  30.2 us (9%)
  blocking collectives  29 us (9%)
  other arithmetic  16.4 us (5%)
  between operations  14.3 us (4%)
  local copies, waits for them, and re-layouts  4.72 us (1%)
    all_to_all x1, waiting for transfers between devices, body(): lax.all_to_all(sent_terms.reshape(group_size, capacity, features), DP, 0,...  87.2 us
    psum x1, waiting for transfers between devices, body(): lax.psum(local_part.astype(jnp.bfloat16), 'section').astype(jnp.float32)  47.2 us
    all_to_all x1, waiting for transfers between devices, body(): lax.all_to_all(answers.reshape(group_size, capacity, features), DP, 0, 0,...  43.9 us
    all_to_all x1, starting transfers between devices, body(): indices = lax.all_to_all(requests, DP, 0, 0, tiled=True).reshape(-1)  13.1 us
    all_to_all x1, starting transfers between devices, body(): lax.all_to_all(answers.reshape(group_size, capacity, features), DP, 0, 0,...  12.3 us
    all_to_all x1, starting transfers between devices, body(): lax.all_to_all(sent_terms.reshape(group_size, capacity, features), DP, 0,...  8.84 us
    psum x1, blocking collectives, body(): lax.psum((jnp.sum(query_scaled * query_scaled, axis=1), jnp.sum(tool_scal...  8.77 us
    all_to_all x1, waiting for transfers between devices, body(): lax.all_to_all(everyone, DP[:2], 0, 0, tiled=True)  8.12 us
  transfers between devices with their start and end apart: 5, of which 4 were waited for; matrix products, arithmetic and copies ran while one was open for 5% of the time, Pallas kernels for 0%

profile of v8, /device:TPU:1, one launch (start us, length us, event | category | flops | bytes accessed | tf_op | source)
XLA Modules:
  0.0 319.8 jit_solution(16528079204952759608)
XLA Ops:
  7.2 0.8 broadcast_compare_fusion
  8.4 0.8 copy.31
  9.4 0.8 copy.28
  11.0 1.1 select_reduce_fusion.2
  12.8 13.1 %all-to-all-start = ((s32[64,1,32]{2,1,0:T(1,128)}), s32[64,1,32]{2,1,0:T(1,128)S(1)}, u32[]{:S(2)}, u32[]{:S(2)}) async-start(s32[64,1,32]{2,1,0:T(1,128)} %bitcast), calls=%async_computation | async-start | bytes 65536 | tf_op jit(solution)/shard_map/all_to_all | solution.py:55
  26.0 2.2 fusion.9
  28.1 8.8 %all-reduce.1 = (f32[512]{0:T(512)S(1)}, f32[512]{0:T(512)S(1)}) all-reduce(f32[512]{0:T(512)S(1)} %get-tuple-element.8, f32[512]{0:T(512)S(1)} %get-tuple-element.7), channel_id=1, replica_groups=mesh['dz'=8,'dy'=4,'dc'=2,'section'=4] {'section'}, use_global_device_ids=true, to_apply=%region_3.4 | all-reduce | flops 1024 | bytes 8192 | tf_op jit(solution)/shard_map/psum | solution.py:59
  37.4 0.7 reduce.4
  38.2 4.2 %fusion.3 = bf16[2048,1024]{1,0:T(8,128)(2,1)} fusion(s32[2048]{0:T(1024)S(1)} %eq.70, bf16[512,1024]{1,0:T(8,128)(2,1)S(1)} %copy-done.1, f32[512]{0:T(512)S(1)} %add_sqrt_fusion, f32[1024]{0:T(1024)S(1)} %copy-done.7), kind=kOutput, calls=%fused_computation.11 | convolution fusion | flops 2152726528 | bytes 5257216 | tf_op jit(solution)/shard_map/dot_general | solution.py:72
  42.5 12.3 %all-to-all-start.1 = ((bf16[64,32,1024]{2,1,0:T(8,128)(2,1)}), bf16[64,32,1024]{2,1,0:T(8,128)(2,1)}, u32[]{:S(2)}, u32[]{:S(2)}) async-start(bf16[64,32,1024]{2,1,0:T(8,128)(2,1)} %bitcast.10), calls=%async_computation.1 | async-start | bytes 8388608 | tf_op jit(solution)/shard_map/all_to_all | solution.py:73
  54.9 1.6 convolution_convert_fusion.1
  56.9 47.2 %all-reduce.4.cloned.1.call-done = bf16[512,512]{1,0:T(8,128)(2,1)} async-done(((bf16[512,512]{1,0:T(8,128)(2,1)}), bf16[512,512]{1,0:T(8,128)(2,1)}) %all-reduce.4.cloned.1.call-update) | async-done | bytes 524304 | tf_op jit(solution)/shard_map/psum | solution.py:86
  104.1 1.5 fusion.16
  105.6 43.9 %all-to-all-done.1 = bf16[64,32,1024]{2,1,0:T(8,128)(2,1)} async-done(((bf16[64,32,1024]{2,1,0:T(8,128)(2,1)}), bf16[64,32,1024]{2,1,0:T(8,128)(2,1)}, u32[]{:S(2)}, u32[]{:S(2)}) %all-to-all-start.1) | async-done | bytes 4194336 | tf_op jit(solution)/shard_map/all_to_all | solution.py:73
  149.5 4.6 %fusion.37 = f32[512,2048]{1,0:T(8,128)S(1)} fusion(bf16[2048,1024]{1,0:T(8,128)(2,1)} %bitcast.2, f32[512]{0:T(512)S(1)} %add_sqrt_fusion.1, f32[1024]{0:T(1024)S(1)} %copy-done.7, bf16[512,1024]{1,0:T(8,128)(2,1)S(1)} %copy-done), kind=kOutput, calls=%fused_computation.65 | convolution fusion | flops 2149580800 | bytes 9443328 | tf_op jit(solution)/shard_map/dot_general | solution.py:81
  154.1 1.4 select_reduce_fusion.1
  155.5 6.2 %psum.52 = bf16[512,2]{0,1:T(2,128)(2,1)S(1)} all-reduce(bf16[512,2]{0,1:T(2,128)(2,1)S(1)} %select_reduce_fusion.1), channel_id=1, replica_groups=mesh['dz'=8,'dy'=4,'dc'=2,'section'=4] {'section'}, use_global_device_ids=true, to_apply=%region_10.11 | all-reduce | flops 1024 | bytes 4096 | tf_op jit(solution)/shard_map/psum | solution.py:87
  161.8 1.9 select_reduce_fusion
  163.7 4.5 %convolution_convert_fusion = bf16[2048,1024]{1,0:T(8,128)(2,1)} fusion(bf16[512,2048]{1,0:T(8,128)(2,1)S(1)} %select_reduce_fusion, f32[512]{0:T(512)S(1)} %add_sqrt_fusion.1, f32[1024]{0:T(1024)S(1)} %copy-done.7, bf16[512,1024]{1,0:T(8,128)(2,1)S(1)} %copy-done), kind=kOutput, calls=%fused_computation.12 | convolution fusion | flops 2151677952 | bytes 7346176 | tf_op jit(solution)/shard_map/dot_general | solution.py:96
  168.2 8.8 %all-to-all-start.2 = ((bf16[64,32,1024]{2,1,0:T(8,128)(2,1)}), bf16[64,32,1024]{2,1,0:T(8,128)(2,1)}, u32[]{:S(2)}, u32[]{:S(2)}) async-start(bf16[64,32,1024]{2,1,0:T(8,128)(2,1)} %bitcast.11), calls=%async_computation.2 | async-start | bytes 8388608 | tf_op jit(solution)/shard_map/all_to_all | solution.py:99
  177.0 5.2 %fusion.40 = f32[512,1024]{1,0:T(8,128)S(1)} fusion(bf16[512,2048]{1,0:T(8,128)(2,1)} %copy-done.4, bf16[2048,1024]{1,0:T(8,128)(2,1)} %bitcast.2), kind=kOutput, calls=%fused_computation.66 | convolution fusion | flops 2147483648 | bytes 8388608 | tf_op jit(solution)/shard_map/dot_general | solution.py:104
  182.2 2.4 convolution_add_fusion.1
  184.7 87.2 %all-to-all-done.2 = bf16[64,32,1024]{2,1,0:T(8,128)(2,1)} async-done(((bf16[64,32,1024]{2,1,0:T(8,128)(2,1)}), bf16[64,32,1024]{2,1,0:T(8,128)(2,1)}, u32[]{:S(2)}, u32[]{:S(2)}) %all-to-all-start.2) | async-done | bytes 4194336 | tf_op jit(solution)/shard_map/all_to_all | solution.py:99
  271.9 4.8 %fusion = f32[512,1024]{1,0:T(8,128)S(1)} fusion(bf16[2048,1024]{1,0:T(8,128)(2,1)} %bitcast.4, s32[2048]{0:T(1024)S(1)} %eq.70), kind=kOutput, calls=%fused_computation.6 | convolution fusion | flops 2148532224 | bytes 6299648 | tf_op jit(solution)/shard_map/dot_general | solution.py:108
  276.7 2.9 multiply_reduce_fusion
  279.6 7.9 %all-reduce = (f32[512]{0:T(512)S(1)}, f32[512]{0:T(512)S(1)}) all-reduce(f32[512]{0:T(512)S(1)} %get-tuple-element.6, f32[512]{0:T(512)S(1)} %get-tuple-element.5), channel_id=1, replica_groups=mesh['dz'=8,'dy'=4,'dc'=2,'section'=4] {'section'}, use_global_device_ids=true, to_apply=%region_14.15 | all-reduce | flops 1024 | bytes 8192 | tf_op jit(solution)/shard_map/psum | solution.py:112
  287.5 2.4 fusion.11
  289.9 1.9 fusion.10
  291.8 6.1 %psum.55 = f32[1024]{0:T(1024)S(1)} all-reduce(f32[1024]{0:T(1024)S(1)} %add.65), channel_id=1, replica_groups=mesh['dz'=8,'dy'=4,'dc'=2,'section'=4] {'dc'}, use_global_device_ids=true, to_apply=%region_19.20 | all-reduce | flops 1024 | bytes 8192 | tf_op jit(solution)/shard_map/psum | solution.py:123
  298.6 4.3 %all-to-all-start.3 = ((f32[32,1,1024]{2,1,0:T(1,128)}), f32[32,1,1024]{2,1,0:T(1,128)S(1)}, u32[]{:S(2)}, u32[]{:S(2)}) async-start(f32[32,1,1024]{2,1,0:T(1,128)} %broadcast_in_dim.99), calls=%async_computation.3 | async-start | bytes 262144 | tf_op jit(solution)/shard_map/all_to_all | solution.py:126
  302.9 1.2 multiply_convert_fusion.1
  304.1 8.1 %all-to-all-done.3 = f32[32,1,1024]{2,1,0:T(1,128)S(1)} async-done(((f32[32,1,1024]{2,1,0:T(1,128)}), f32[32,1,1024]{2,1,0:T(1,128)S(1)}, u32[]{:S(2)}, u32[]{:S(2)}) %all-to-all-start.3) | async-done | bytes 131104 | tf_op jit(solution)/shard_map/all_to_all | solution.py:126
  (43 shorter events, 4.5 us)
Async XLA Ops:
  7.2 31.1 %copy-start.7 = (f32[1024]{0:T(1024)S(1)}, f32[1024]{0:T(1024)}, u32[]{:S(2)}) copy-start(f32[1024]{0:T(1024)} %param.9) | copy-start | bytes 12292
  7.2 31.1 %copy-start.1 = (bf16[512,1024]{1,0:T(8,128)(2,1)S(1)}, bf16[512,1024]{1,0:T(8,128)(2,1)}, u32[]{:S(2)}) copy-start(bf16[512,1024]{1,0:T(8,128)(2,1)} %param.8) | copy-start | bytes 3145732
  12.8 24.1 %all-to-all-start = ((s32[64,1,32]{2,1,0:T(1,128)}), s32[64,1,32]{2,1,0:T(1,128)S(1)}, u32[]{:S(2)}, u32[]{:S(2)}) async-start(s32[64,1,32]{2,1,0:T(1,128)} %bitcast), calls=%async_computation | async-start | bytes 65536 | tf_op jit(solution)/shard_map/all_to_all | solution.py:55
  42.5 12.4 %copy-start = (bf16[512,1024]{1,0:T(8,128)(2,1)S(1)}, bf16[512,1024]{1,0:T(8,128)(2,1)}, u32[]{:S(2)}) copy-start(bf16[512,1024]{1,0:T(8,128)(2,1)} %param.7) | copy-start | bytes 3145732
  42.5 107.1 %all-to-all-start.1 = ((bf16[64,32,1024]{2,1,0:T(8,128)(2,1)}), bf16[64,32,1024]{2,1,0:T(8,128)(2,1)}, u32[]{:S(2)}, u32[]{:S(2)}) async-start(bf16[64,32,1024]{2,1,0:T(8,128)(2,1)} %bitcast.10), calls=%async_computation.1 | async-start | bytes 8388608 | tf_op jit(solution)/shard_map/all_to_all | solution.py:73
  54.8 49.3 %all-reduce.4.cloned.1.call-start = ((), (), s32[]{:S(2)}) async-start(), calls=%async_computation.4 | async-start | bytes 1048576 | tf_op jit(solution)/shard_map/psum | solution.py:86
  54.9 2.0 copy-start.6
  54.9 2.0 copy-start.8
  54.9 49.2 %copy-start.9 = (s32[512]{0:T(512)S(1)}, s32[512]{0:T(512)}, u32[]{:S(2)}) copy-start(s32[512]{0:T(512)} %param.10) | copy-start | bytes 6148
  163.7 4.5 %copy-start.4 = (bf16[512,2048]{1,0:T(8,128)(2,1)}, bf16[512,2048]{1,0:T(8,128)(2,1)S(1)}, u32[]{:S(2)}) copy-start(bf16[512,2048]{1,0:T(8,128)(2,1)S(1)} %select_reduce_fusion) | copy-start | bytes 6291460
  168.2 103.8 %all-to-all-start.2 = ((bf16[64,32,1024]{2,1,0:T(8,128)(2,1)}), bf16[64,32,1024]{2,1,0:T(8,128)(2,1)}, u32[]{:S(2)}, u32[]{:S(2)}) async-start(bf16[64,32,1024]{2,1,0:T(8,128)(2,1)} %bitcast.11), calls=%async_computation.2 | async-start | bytes 8388608 | tf_op jit(solution)/shard_map/all_to_all | solution.py:99
  177.0 5.2 %copy-start.5 = (bf16[512,512]{1,0:T(8,128)(2,1)S(1)}, bf16[512,512]{1,0:T(8,128)(2,1)}, u32[]{:S(2)}) copy-start(bf16[512,512]{1,0:T(8,128)(2,1)} %all-reduce.4.cloned.1.call-done) | copy-start | bytes 1572868
  271.9 4.8 %copy-start.2 = (f32[512,1024]{1,0:T(8,128)S(1)}, f32[512,1024]{1,0:T(8,128)}, u32[]{:S(2)}) copy-start(f32[512,1024]{1,0:T(8,128)} %convolution_add_fusion.1) | copy-start | bytes 6291460
  287.5 2.4 copy-start.3
  298.6 13.7 %all-to-all-start.3 = ((f32[32,1,1024]{2,1,0:T(1,128)}), f32[32,1,1024]{2,1,0:T(1,128)S(1)}, u32[]{:S(2)}, u32[]{:S(2)}) async-start(f32[32,1,1024]{2,1,0:T(1,128)} %broadcast_in_dim.99), calls=%async_computation.3 | async-start | bytes 262144 | tf_op jit(solution)/shard_map/all_to_all | solution.py:126
Sparse Core Ops, SparseCore 0:
  58.6 45.5 all-reduce.3

commit v9 on v6

--- a/solution.py
+++ b/solution.py
@@ -63,10 +63,10 @@
 
     query_scaled = query_hidden.astype(jnp.float32) * norm_gain
     tool_scaled = tool_hidden.astype(jnp.float32) * norm_gain
-    squares = section_sum(
-        jnp.stack([jnp.sum(query_scaled * query_scaled, axis=1), jnp.sum(tool_scaled * tool_scaled, axis=1)])
+    query_squares, tool_squares = lax.psum(
+        (jnp.sum(query_scaled * query_scaled, axis=1), jnp.sum(tool_scaled * tool_scaled, axis=1)),
+        "section",
     )
-    query_squares, tool_squares = squares[0], squares[1]
     query_norm = jnp.sqrt(query_squares + EPSILON)
     tool_norm = jnp.sqrt(tool_squares + EPSILON)
     query_unit32 = query_scaled / query_norm[:, None]
@@ -127,8 +127,10 @@
     gain_terms = jnp.sum(query_back * query_hidden.astype(jnp.float32), axis=0) + jnp.sum(
         tool_back * tool_hidden.astype(jnp.float32), axis=0
     )
-    everyone = jnp.broadcast_to(gain_terms[None, :], (group_size, gain_terms.shape[0]))
-    gain_grad = jnp.sum(lax.all_to_all(everyone, DP, 0, 0, tiled=True), axis=0)
+    pair_terms = lax.psum(gain_terms, "dc")
+    chips = lax.axis_size(DP[:2])
+    everyone = jnp.broadcast_to(pair_terms[None, :], (chips, gain_terms.shape[0]))
+    gain_grad = jnp.sum(lax.all_to_all(everyone, DP[:2], 0, 0, tiled=True), axis=0)
     return (query_grad, tool_grad, gain_grad)
 
 

time: 324 us -> 323 us (level)
  blocking collectives: 6.56 us -> 20.6 us
  waiting for transfers between devices: 206 us -> 192 us
    psum x0 -> x2, blocking collectives: none -> 14 us  [the longest x1 8.77 us: body(): lax.psum((jnp.sum(query_scaled * query_scaled, axis=1), jnp.sum(tool_scal...]
    all_to_all x1, waiting for transfers between devices: 9.28 us -> 0.01 us  [body(): indices = lax.all_to_all(requests, DP, 0, 0, tiled=True).reshape(-1)]
    all_to_all x1, starting transfers between devices: 5.83 us -> 12.3 us  [body(): lax.all_to_all(answers.reshape(group_size, capacity, features), DP, 0, 0,...]
    all_to_all x2 -> x1, starting transfers between devices: 8.26 us -> 3.43 us  [section_sum(): lax.all_to_all(jnp.broadcast_to(flat[None, :], (parts, flat.shape[0])), '...]
    all_to_all x1, waiting for transfers between devices: 11.8 us -> 8.12 us  [body(): lax.all_to_all(everyone, DP[:2], 0, 0, tiled=True)]
    all_to_all x1, starting transfers between devices: 7.88 us -> 4.31 us  [body(): lax.all_to_all(everyone, DP[:2], 0, 0, tiled=True)]
  transfers between devices with their start and end apart: 7 -> 6, of which waited for: 6 -> 4; matrix products, arithmetic and copies ran while one was open for 7% -> 7% of each run, Pallas kernels for 0% -> 0%
where the time goes in v9:
time: 323 us; the launch traced here: 322 us
  waiting for transfers between devices  192 us (59%)
  starting transfers between devices  41.5 us (13%)
  matrix products  30 us (9%)
  blocking collectives  20.6 us (6%)
  other arithmetic  17.2 us (5%)
  between operations  14.4 us (4%)
  local copies, waits for them, and re-layouts  7.09 us (2%)
    all_to_all x1, waiting for transfers between devices, body(): lax.all_to_all(answers.reshape(group_size, capacity, features), DP, 0, 0,...  92.6 us
    all_to_all x1, waiting for transfers between devices, body(): lax.all_to_all(sent_terms.reshape(group_size, capacity, features), DP, 0,...  88.4 us
    all_to_all x1, starting transfers between devices, body(): indices = lax.all_to_all(requests, DP, 0, 0, tiled=True).reshape(-1)  13.1 us
    all_to_all x1, starting transfers between devices, body(): lax.all_to_all(answers.reshape(group_size, capacity, features), DP, 0, 0,...  12.3 us
    psum x1, blocking collectives, body(): lax.psum((jnp.sum(query_scaled * query_scaled, axis=1), jnp.sum(tool_scal...  8.77 us
    all_to_all x1, starting transfers between devices, body(): lax.all_to_all(sent_terms.reshape(group_size, capacity, features), DP, 0,...  8.25 us
    all_to_all x1, waiting for transfers between devices, body(): lax.all_to_all(everyone, DP[:2], 0, 0, tiled=True)  8.12 us
    all_to_all x1, blocking collectives, section_sum(): lax.all_to_all(jnp.broadcast_to(flat[None, :], (parts, flat.shape[0])), '...  6.56 us
  transfers between devices with their start and end apart: 6, of which 4 were waited for; matrix products, arithmetic and copies ran while one was open for 7% of the time, Pallas kernels for 0%

profile of v9, /device:TPU:1, one launch (start us, length us, event | category | flops | bytes accessed | tf_op | source)
XLA Modules:
  0.0 322.3 jit_solution(15185136900107781963)
XLA Ops:
  7.2 0.8 broadcast_compare_fusion
  8.4 0.8 copy.47
  9.4 0.8 copy.44
  11.0 1.1 select_reduce_fusion.2
  12.8 13.1 %all-to-all-start = ((s32[64,1,32]{2,1,0:T(1,128)}), s32[64,1,32]{2,1,0:T(1,128)S(1)}, u32[]{:S(2)}, u32[]{:S(2)}) async-start(s32[64,1,32]{2,1,0:T(1,128)} %bitcast), calls=%async_computation | async-start | bytes 65536 | tf_op jit(solution)/shard_map/all_to_all | solution.py:62
  26.0 2.2 fusion.9
  28.1 8.8 %all-reduce = (f32[512]{0:T(512)S(1)}, f32[512]{0:T(512)S(1)}) all-reduce(f32[512]{0:T(512)S(1)} %get-tuple-element.8, f32[512]{0:T(512)S(1)} %get-tuple-element.7), channel_id=1, replica_groups=mesh['dz'=8,'dy'=4,'dc'=2,'section'=4] {'section'}, use_global_device_ids=true, to_apply=%region_3.4 | all-reduce | flops 1024 | bytes 8192 | tf_op jit(solution)/shard_map/psum | solution.py:66
  37.4 0.7 reduce.6
  38.2 4.2 %fusion.3 = bf16[2048,1024]{1,0:T(8,128)(2,1)} fusion(s32[2048]{0:T(1024)S(1)} %eq.70, bf16[512,1024]{1,0:T(8,128)(2,1)S(1)} %copy-done.1, f32[512]{0:T(512)S(1)} %add_sqrt_fusion, f32[1024]{0:T(1024)S(1)} %copy-done.7), kind=kOutput, calls=%fused_computation.11 | convolution fusion | flops 2152726528 | bytes 5257216 | tf_op jit(solution)/shard_map/dot_general | solution.py:79
  42.5 12.3 %all-to-all-start.1 = ((bf16[64,32,1024]{2,1,0:T(8,128)(2,1)}), bf16[64,32,1024]{2,1,0:T(8,128)(2,1)}, u32[]{:S(2)}, u32[]{:S(2)}) async-start(bf16[64,32,1024]{2,1,0:T(8,128)(2,1)} %bitcast.15), calls=%async_computation.1 | async-start | bytes 8388608 | tf_op jit(solution)/shard_map/all_to_all | solution.py:80
  54.9 1.6 convolution_convert_fusion.1
  56.9 92.6 %all-to-all-done.1 = bf16[64,32,1024]{2,1,0:T(8,128)(2,1)} async-done(((bf16[64,32,1024]{2,1,0:T(8,128)(2,1)}), bf16[64,32,1024]{2,1,0:T(8,128)(2,1)}, u32[]{:S(2)}, u32[]{:S(2)}) %all-to-all-start.1) | async-done | bytes 4194336 | tf_op jit(solution)/shard_map/all_to_all | solution.py:80
  149.5 4.6 %fusion.37 = f32[512,2048]{1,0:T(8,128)S(1)} fusion(bf16[2048,1024]{1,0:T(8,128)(2,1)} %bitcast.2, f32[512]{0:T(512)S(1)} %add_sqrt_fusion.1, f32[1024]{0:T(1024)S(1)} %copy-done.7, bf16[512,1024]{1,0:T(8,128)(2,1)S(1)} %copy-done), kind=kOutput, calls=%fused_computation.68 | convolution fusion | flops 2149580800 | bytes 9443328 | tf_op jit(solution)/shard_map/dot_general | solution.py:88
  154.1 1.4 select_reduce_fusion.1
  157.7 3.4 %all-to-all-start.2 = ((bf16[4,2,512]{2,1,0:T(2,128)(2,1)}), bf16[4,2,512]{2,1,0:T(2,128)(2,1)S(1)}, u32[]{:S(2)}, u32[]{:S(2)}) async-start(bf16[4,2,512]{2,1,0:T(2,128)(2,1)} %reshape.133), calls=%async_computation.2 | async-start | bytes 16384 | tf_op jit(solution)/shard_map/all_to_all | solution.py:37
  161.2 1.5 fusion.16
  162.7 2.4 all-to-all-done.2
  165.6 1.9 select_reduce_fusion
  167.5 4.5 %convolution_convert_fusion = bf16[2048,1024]{1,0:T(8,128)(2,1)} fusion(bf16[512,2048]{1,0:T(8,128)(2,1)S(1)} %select_reduce_fusion, f32[512]{0:T(512)S(1)} %add_sqrt_fusion.1, f32[1024]{0:T(1024)S(1)} %copy-done.7, bf16[512,1024]{1,0:T(8,128)(2,1)S(1)} %copy-done), kind=kOutput, calls=%fused_computation.12 | convolution fusion | flops 2151677952 | bytes 7346176 | tf_op jit(solution)/shard_map/dot_general | solution.py:103
  171.9 8.3 %all-to-all-start.3 = ((bf16[64,32,1024]{2,1,0:T(8,128)(2,1)}), bf16[64,32,1024]{2,1,0:T(8,128)(2,1)}, u32[]{:S(2)}, u32[]{:S(2)}) async-start(bf16[64,32,1024]{2,1,0:T(8,128)(2,1)} %bitcast.16), calls=%async_computation.3 | async-start | bytes 8388608 | tf_op jit(solution)/shard_map/all_to_all | solution.py:106
  180.2 6.5 %fusion.41 = f32[512,1024]{1,0:T(8,128)} fusion(bf16[512,2048]{1,0:T(8,128)(2,1)} %copy-done.4, bf16[2048,1024]{1,0:T(8,128)(2,1)} %bitcast.2), kind=kOutput, calls=%fused_computation.70 | convolution fusion | flops 2147483648 | bytes 8388608 | tf_op jit(solution)/shard_map/dot_general | solution.py:111
  186.7 88.4 %all-to-all-done.3 = bf16[64,32,1024]{2,1,0:T(8,128)(2,1)} async-done(((bf16[64,32,1024]{2,1,0:T(8,128)(2,1)}), bf16[64,32,1024]{2,1,0:T(8,128)(2,1)}, u32[]{:S(2)}, u32[]{:S(2)}) %all-to-all-start.3) | async-done | bytes 4194336 | tf_op jit(solution)/shard_map/all_to_all | solution.py:106
  275.1 4.7 %fusion = f32[512,1024]{1,0:T(8,128)S(1)} fusion(bf16[2048,1024]{1,0:T(8,128)(2,1)} %bitcast.5, s32[2048]{0:T(1024)S(1)} %eq.70), kind=kOutput, calls=%fused_computation.6 | convolution fusion | flops 2148532224 | bytes 6299648 | tf_op jit(solution)/shard_map/dot_general | solution.py:115
  279.8 1.1 convolution_add_fusion
  281.4 2.9 multiply_reduce_fusion.1
  284.3 6.6 %all_to_all.37 = f32[4,1,1024]{2,1,0:T(1,128)S(1)} all-to-all(f32[4,1,1024]{2,1,0:T(1,128)S(1)} %broadcast_in_dim.111), channel_id=1, replica_groups=mesh['dz'=8,'dy'=4,'dc'=2,'section'=4] {'section'}, dimensions={0} | all-to-all | bytes 32768 | tf_op jit(solution)/shard_map/all_to_all | solution.py:37
  290.9 2.4 fusion.11
  293.3 1.9 fusion.10
  295.2 5.2 %psum.31 = f32[1024]{0:T(1024)S(1)} all-reduce(f32[1024]{0:T(1024)S(1)} %add.59), channel_id=1, replica_groups=mesh['dz'=8,'dy'=4,'dc'=2,'section'=4] {'dc'}, use_global_device_ids=true, to_apply=%region_18.19 | all-reduce | flops 1024 | bytes 8192 | tf_op jit(solution)/shard_map/psum | solution.py:130
  301.1 4.3 %all-to-all-start.5 = ((f32[32,1,1024]{2,1,0:T(1,128)}), f32[32,1,1024]{2,1,0:T(1,128)S(1)}, u32[]{:S(2)}, u32[]{:S(2)}) async-start(f32[32,1,1024]{2,1,0:T(1,128)} %broadcast_in_dim.112), calls=%async_computation.5 | async-start | bytes 262144 | tf_op jit(solution)/shard_map/all_to_all | solution.py:133
  305.5 1.2 multiply_convert_fusion.1
  306.7 8.1 %all-to-all-done.5 = f32[32,1,1024]{2,1,0:T(1,128)S(1)} async-done(((f32[32,1,1024]{2,1,0:T(1,128)}), f32[32,1,1024]{2,1,0:T(1,128)S(1)}, u32[]{:S(2)}, u32[]{:S(2)}) %all-to-all-start.5) | async-done | bytes 131104 | tf_op jit(solution)/shard_map/all_to_all | solution.py:133
  (62 shorter events, 7.7 us)
Async XLA Ops:
  7.2 31.1 %copy-start.7 = (f32[1024]{0:T(1024)S(1)}, f32[1024]{0:T(1024)}, u32[]{:S(2)}) copy-start(f32[1024]{0:T(1024)} %param.9) | copy-start | bytes 12292
  7.2 31.1 %copy-start.1 = (bf16[512,1024]{1,0:T(8,128)(2,1)S(1)}, bf16[512,1024]{1,0:T(8,128)(2,1)}, u32[]{:S(2)}) copy-start(bf16[512,1024]{1,0:T(8,128)(2,1)} %param.8) | copy-start | bytes 3145732
  12.8 24.1 %all-to-all-start = ((s32[64,1,32]{2,1,0:T(1,128)}), s32[64,1,32]{2,1,0:T(1,128)S(1)}, u32[]{:S(2)}, u32[]{:S(2)}) async-start(s32[64,1,32]{2,1,0:T(1,128)} %bitcast), calls=%async_computation | async-start | bytes 65536 | tf_op jit(solution)/shard_map/all_to_all | solution.py:62
  42.5 12.4 %copy-start = (bf16[512,1024]{1,0:T(8,128)(2,1)S(1)}, bf16[512,1024]{1,0:T(8,128)(2,1)}, u32[]{:S(2)}) copy-start(bf16[512,1024]{1,0:T(8,128)(2,1)} %param.7) | copy-start | bytes 3145732
  42.5 107.1 %all-to-all-start.1 = ((bf16[64,32,1024]{2,1,0:T(8,128)(2,1)}), bf16[64,32,1024]{2,1,0:T(8,128)(2,1)}, u32[]{:S(2)}, u32[]{:S(2)}) async-start(bf16[64,32,1024]{2,1,0:T(8,128)(2,1)} %bitcast.15), calls=%async_computation.1 | async-start | bytes 8388608 | tf_op jit(solution)/shard_map/all_to_all | solution.py:80
  54.8 106.4 %all-reduce.3.cloned.1.call-start = ((), (), s32[]{:S(2)}) async-start(), calls=%async_computation.6 | async-start | bytes 1048576 | tf_op jit(solution)/shard_map/psum | solution.py:93
  54.9 2.0 copy-start.6
  54.9 2.0 copy-start.8
  154.1 7.1 %copy-start.9 = (s32[512]{0:T(512)S(1)}, s32[512]{0:T(512)}, u32[]{:S(2)}) copy-start(s32[512]{0:T(512)} %param.10) | copy-start | bytes 6148
  157.7 7.4 %all-to-all-start.2 = ((bf16[4,2,512]{2,1,0:T(2,128)(2,1)}), bf16[4,2,512]{2,1,0:T(2,128)(2,1)S(1)}, u32[]{:S(2)}, u32[]{:S(2)}) async-start(bf16[4,2,512]{2,1,0:T(2,128)(2,1)} %reshape.133), calls=%async_computation.2 | async-start | bytes 16384 | tf_op jit(solution)/shard_map/all_to_all | solution.py:37
  167.5 4.5 %copy-start.4 = (bf16[512,2048]{1,0:T(8,128)(2,1)}, bf16[512,2048]{1,0:T(8,128)(2,1)S(1)}, u32[]{:S(2)}) copy-start(bf16[512,2048]{1,0:T(8,128)(2,1)S(1)} %select_reduce_fusion) | copy-start | bytes 6291460
  171.9 103.2 %all-to-all-start.3 = ((bf16[64,32,1024]{2,1,0:T(8,128)(2,1)}), bf16[64,32,1024]{2,1,0:T(8,128)(2,1)}, u32[]{:S(2)}, u32[]{:S(2)}) async-start(bf16[64,32,1024]{2,1,0:T(8,128)(2,1)} %bitcast.16), calls=%async_computation.3 | async-start | bytes 8388608 | tf_op jit(solution)/shard_map/all_to_all | solution.py:106
  275.1 4.7 %copy-start.5 = (bf16[512,512]{1,0:T(8,128)(2,1)S(1)}, bf16[512,512]{1,0:T(8,128)(2,1)}, u32[]{:S(2)}) copy-start(bf16[512,512]{1,0:T(8,128)(2,1)} %all-reduce.3.cloned.1.call-done) | copy-start | bytes 1572868
  279.8 1.6 copy-start.10
  281.4 2.9 copy-start.3
  290.9 2.4 copy-start.2
  301.1 13.7 %all-to-all-start.5 = ((f32[32,1,1024]{2,1,0:T(1,128)}), f32[32,1,1024]{2,1,0:T(1,128)S(1)}, u32[]{:S(2)}, u32[]{:S(2)}) async-start(f32[32,1,1024]{2,1,0:T(1,128)} %broadcast_in_dim.112), calls=%async_computation.5 | async-start | bytes 262144 | tf_op jit(solution)/shard_map/all_to_all | solution.py:133
Sparse Core Ops, SparseCore 0:
  58.6 45.5 all-reduce.2

commit v10 on v8

--- a/solution.py
+++ b/solution.py
@@ -105,6 +105,7 @@
     tool_pull = lax.dot_general(
         shard_gradients, query_unit, (((0,), (0,)), ((), ())), preferred_element_type=jnp.float32
     )
+    arrived_terms, tool_pull, query_pull = lax.optimization_barrier((arrived_terms, tool_pull, query_pull))
     tool_pull = tool_pull + lax.dot_general(
         pick_tool, arrived_terms, (((0,), (0,)), ((), ())), preferred_element_type=jnp.float32
     )

time: 320 us -> 321 us (level)
  no operation moved by 1% of the time
where the time goes in v10:
time: 321 us; the launch traced here: 320 us
  waiting for transfers between devices  185 us (58%)
  starting transfers between devices  38.8 us (12%)
  matrix products  31.9 us (10%)
  blocking collectives  29 us (9%)
  other arithmetic  16.4 us (5%)
  between operations  14.3 us (4%)
  local copies, waits for them, and re-layouts  4.72 us (1%)
    all_to_all x1, waiting for transfers between devices, body(): lax.all_to_all(sent_terms.reshape(group_size, capacity, features), DP, 0,...  85.5 us
    psum x1, waiting for transfers between devices, body(): lax.psum(local_part.astype(jnp.bfloat16), 'section').astype(jnp.float32)  47.2 us
    all_to_all x1, waiting for transfers between devices, body(): lax.all_to_all(answers.reshape(group_size, capacity, features), DP, 0, 0,...  43.9 us
    all_to_all x1, starting transfers between devices, body(): indices = lax.all_to_all(requests, DP, 0, 0, tiled=True).reshape(-1)  13.1 us
    all_to_all x1, starting transfers between devices, body(): lax.all_to_all(answers.reshape(group_size, capacity, features), DP, 0, 0,...  12.3 us
    all_to_all x1, starting transfers between devices, body(): lax.all_to_all(sent_terms.reshape(group_size, capacity, features), DP, 0,...  8.97 us
    psum x1, blocking collectives, body(): lax.psum((jnp.sum(query_scaled * query_scaled, axis=1), jnp.sum(tool_scal...  8.77 us
    all_to_all x1, waiting for transfers between devices, body(): lax.all_to_all(everyone, DP[:2], 0, 0, tiled=True)  8.12 us
  transfers between devices with their start and end apart: 5, of which 4 were waited for; matrix products, arithmetic and copies ran while one was open for 5% of the time, Pallas kernels for 0%

profile of v10, /device:TPU:1, one launch (start us, length us, event | category | flops | bytes accessed | tf_op | source)
XLA Modules:
  0.0 319.9 jit_solution(11383434769325103689)
XLA Ops:
  7.2 0.8 broadcast_compare_fusion
  8.4 0.8 copy.31
  9.4 0.8 copy.28
  11.0 1.1 select_reduce_fusion.2
  12.8 13.1 %all-to-all-start = ((s32[64,1,32]{2,1,0:T(1,128)}), s32[64,1,32]{2,1,0:T(1,128)S(1)}, u32[]{:S(2)}, u32[]{:S(2)}) async-start(s32[64,1,32]{2,1,0:T(1,128)} %bitcast), calls=%async_computation | async-start | bytes 65536 | tf_op jit(solution)/shard_map/all_to_all | solution.py:55
  26.0 2.2 fusion.9
  28.1 8.8 %all-reduce.1 = (f32[512]{0:T(512)S(1)}, f32[512]{0:T(512)S(1)}) all-reduce(f32[512]{0:T(512)S(1)} %get-tuple-element.14, f32[512]{0:T(512)S(1)} %get-tuple-element.13), channel_id=1, replica_groups=mesh['dz'=8,'dy'=4,'dc'=2,'section'=4] {'section'}, use_global_device_ids=true, to_apply=%region_5.6 | all-reduce | flops 1024 | bytes 8192 | tf_op jit(solution)/shard_map/psum | solution.py:59
  37.4 0.7 reduce.4
  38.2 4.2 %fusion.3 = bf16[2048,1024]{1,0:T(8,128)(2,1)} fusion(s32[2048]{0:T(1024)S(1)} %eq.68, bf16[512,1024]{1,0:T(8,128)(2,1)S(1)} %copy-done.1, f32[512]{0:T(512)S(1)} %add_sqrt_fusion, f32[1024]{0:T(1024)S(1)} %copy-done.7), kind=kOutput, calls=%fused_computation.11 | convolution fusion | flops 2152726528 | bytes 5257216 | tf_op jit(solution)/shard_map/dot_general | solution.py:72
  42.5 12.3 %all-to-all-start.1 = ((bf16[64,32,1024]{2,1,0:T(8,128)(2,1)}), bf16[64,32,1024]{2,1,0:T(8,128)(2,1)}, u32[]{:S(2)}, u32[]{:S(2)}) async-start(bf16[64,32,1024]{2,1,0:T(8,128)(2,1)} %bitcast.10), calls=%async_computation.1 | async-start | bytes 8388608 | tf_op jit(solution)/shard_map/all_to_all | solution.py:73
  54.9 1.6 convolution_convert_fusion.1
  56.9 47.2 %all-reduce.4.cloned.1.call-done = bf16[512,512]{1,0:T(8,128)(2,1)} async-done(((bf16[512,512]{1,0:T(8,128)(2,1)}), bf16[512,512]{1,0:T(8,128)(2,1)}) %all-reduce.4.cloned.1.call-update) | async-done | bytes 524304 | tf_op jit(solution)/shard_map/psum | solution.py:86
  104.1 1.5 fusion.18
  105.6 43.9 %all-to-all-done.1 = bf16[64,32,1024]{2,1,0:T(8,128)(2,1)} async-done(((bf16[64,32,1024]{2,1,0:T(8,128)(2,1)}), bf16[64,32,1024]{2,1,0:T(8,128)(2,1)}, u32[]{:S(2)}, u32[]{:S(2)}) %all-to-all-start.1) | async-done | bytes 4194336 | tf_op jit(solution)/shard_map/all_to_all | solution.py:73
  149.5 4.6 %fusion.40 = f32[512,2048]{1,0:T(8,128)S(1)} fusion(bf16[2048,1024]{1,0:T(8,128)(2,1)} %bitcast.2, f32[512]{0:T(512)S(1)} %add_sqrt_fusion.1, f32[1024]{0:T(1024)S(1)} %copy-done.7, bf16[512,1024]{1,0:T(8,128)(2,1)S(1)} %copy-done), kind=kOutput, calls=%fused_computation.66 | convolution fusion | flops 2149580800 | bytes 9443328 | tf_op jit(solution)/shard_map/dot_general | solution.py:81
  154.1 1.4 select_reduce_fusion.1
  155.5 6.2 %psum.51 = bf16[512,2]{0,1:T(2,128)(2,1)S(1)} all-reduce(bf16[512,2]{0,1:T(2,128)(2,1)S(1)} %select_reduce_fusion.1), channel_id=1, replica_groups=mesh['dz'=8,'dy'=4,'dc'=2,'section'=4] {'section'}, use_global_device_ids=true, to_apply=%region_7.8 | all-reduce | flops 1024 | bytes 4096 | tf_op jit(solution)/shard_map/psum | solution.py:87
  161.8 1.9 select_reduce_fusion
  163.7 4.5 %convolution_convert_fusion = bf16[2048,1024]{1,0:T(8,128)(2,1)} fusion(bf16[512,2048]{1,0:T(8,128)(2,1)S(1)} %select_reduce_fusion, f32[512]{0:T(512)S(1)} %add_sqrt_fusion.1, f32[1024]{0:T(1024)S(1)} %copy-done.7, bf16[512,1024]{1,0:T(8,128)(2,1)S(1)} %copy-done), kind=kOutput, calls=%fused_computation.12 | convolution fusion | flops 2151677952 | bytes 7346176 | tf_op jit(solution)/shard_map/dot_general | solution.py:96
  168.2 9.0 %all-to-all-start.2 = ((bf16[64,32,1024]{2,1,0:T(8,128)(2,1)}), bf16[64,32,1024]{2,1,0:T(8,128)(2,1)}, u32[]{:S(2)}, u32[]{:S(2)}) async-start(bf16[64,32,1024]{2,1,0:T(8,128)(2,1)} %bitcast.11), calls=%async_computation.2 | async-start | bytes 8388608 | tf_op jit(solution)/shard_map/all_to_all | solution.py:99
  177.2 2.4 fusion.32
  179.5 4.5 %fusion.42 = f32[512,1024]{1,0:T(8,128)S(1)} fusion(bf16[512,2048]{1,0:T(8,128)(2,1)S(1)} %copy-done.4, bf16[2048,1024]{1,0:T(8,128)(2,1)} %bitcast.2), kind=kOutput, calls=%fused_computation.67 | convolution fusion | flops 2147483648 | bytes 8388608 | tf_op jit(solution)/shard_map/dot_general | solution.py:104
  184.1 2.4 convolution_add_fusion
  186.5 85.5 %all-to-all-done.2 = bf16[64,32,1024]{2,1,0:T(8,128)(2,1)} async-done(((bf16[64,32,1024]{2,1,0:T(8,128)(2,1)}), bf16[64,32,1024]{2,1,0:T(8,128)(2,1)}, u32[]{:S(2)}, u32[]{:S(2)}) %all-to-all-start.2) | async-done | bytes 4194336 | tf_op jit(solution)/shard_map/all_to_all | solution.py:99
  272.0 7.7 %multiply_reduce_fusion = (f32[512]{0:T(512)S(1)}, f32[512]{0:T(512)S(1)}, f32[512,1024]{1,0:T(8,128)}) fusion(f32[512]{0:T(512)S(1)} %add_sqrt_fusion, f32[1024]{0:T(1024)S(1)} %copy-done.7, bf16[512,1024]{1,0:T(8,128)(2,1)S(1)} %copy-done.1, f32[512,1024]{1,0:T(8,128)} %convolution_add_fusion, f32[512]{0:T(512)S(1)} %add_sqrt_fusion.1, ...), kind=kOutput, calls=%fused_computation.27 | convolution fusion | flops 2154298368 | bytes 12603392 | tf_op jit(solution)/shard_map/dot_general | solution.py:109
  279.7 7.9 %all-reduce = (f32[512]{0:T(512)S(1)}, f32[512]{0:T(512)S(1)}) all-reduce(f32[512]{0:T(512)S(1)} %get-tuple-element.12, f32[512]{0:T(512)S(1)} %get-tuple-element.11), channel_id=1, replica_groups=mesh['dz'=8,'dy'=4,'dc'=2,'section'=4] {'section'}, use_global_device_ids=true, to_apply=%region_14.15 | all-reduce | flops 1024 | bytes 8192 | tf_op jit(solution)/shard_map/psum | solution.py:113
  287.6 2.4 fusion.11
  290.0 1.9 fusion.10
  291.9 6.1 %psum.55 = f32[1024]{0:T(1024)S(1)} all-reduce(f32[1024]{0:T(1024)S(1)} %add.65), channel_id=1, replica_groups=mesh['dz'=8,'dy'=4,'dc'=2,'section'=4] {'dc'}, use_global_device_ids=true, to_apply=%region_19.20 | all-reduce | flops 1024 | bytes 8192 | tf_op jit(solution)/shard_map/psum | solution.py:124
  298.7 4.3 %all-to-all-start.3 = ((f32[32,1,1024]{2,1,0:T(1,128)}), f32[32,1,1024]{2,1,0:T(1,128)S(1)}, u32[]{:S(2)}, u32[]{:S(2)}) async-start(f32[32,1,1024]{2,1,0:T(1,128)} %broadcast_in_dim.99), calls=%async_computation.3 | async-start | bytes 262144 | tf_op jit(solution)/shard_map/all_to_all | solution.py:127
  303.0 1.2 multiply_convert_fusion.1
  304.2 8.1 %all-to-all-done.3 = f32[32,1,1024]{2,1,0:T(1,128)S(1)} async-done(((f32[32,1,1024]{2,1,0:T(1,128)}), f32[32,1,1024]{2,1,0:T(1,128)S(1)}, u32[]{:S(2)}, u32[]{:S(2)}) %all-to-all-start.3) | async-done | bytes 131104 | tf_op jit(solution)/shard_map/all_to_all | solution.py:127
  (43 shorter events, 4.5 us)
Async XLA Ops:
  7.2 31.1 %copy-start.7 = (f32[1024]{0:T(1024)S(1)}, f32[1024]{0:T(1024)}, u32[]{:S(2)}) copy-start(f32[1024]{0:T(1024)} %param.9) | copy-start | bytes 12292
  7.2 31.1 %copy-start.1 = (bf16[512,1024]{1,0:T(8,128)(2,1)S(1)}, bf16[512,1024]{1,0:T(8,128)(2,1)}, u32[]{:S(2)}) copy-start(bf16[512,1024]{1,0:T(8,128)(2,1)} %param.8) | copy-start | bytes 3145732
  12.8 24.1 %all-to-all-start = ((s32[64,1,32]{2,1,0:T(1,128)}), s32[64,1,32]{2,1,0:T(1,128)S(1)}, u32[]{:S(2)}, u32[]{:S(2)}) async-start(s32[64,1,32]{2,1,0:T(1,128)} %bitcast), calls=%async_computation | async-start | bytes 65536 | tf_op jit(solution)/shard_map/all_to_all | solution.py:55
  42.5 12.4 %copy-start = (bf16[512,1024]{1,0:T(8,128)(2,1)S(1)}, bf16[512,1024]{1,0:T(8,128)(2,1)}, u32[]{:S(2)}) copy-start(bf16[512,1024]{1,0:T(8,128)(2,1)} %param.7) | copy-start | bytes 3145732
  42.5 107.1 %all-to-all-start.1 = ((bf16[64,32,1024]{2,1,0:T(8,128)(2,1)}), bf16[64,32,1024]{2,1,0:T(8,128)(2,1)}, u32[]{:S(2)}, u32[]{:S(2)}) async-start(bf16[64,32,1024]{2,1,0:T(8,128)(2,1)} %bitcast.10), calls=%async_computation.1 | async-start | bytes 8388608 | tf_op jit(solution)/shard_map/all_to_all | solution.py:73
  54.8 49.3 %all-reduce.4.cloned.1.call-start = ((), (), s32[]{:S(2)}) async-start(), calls=%async_computation.4 | async-start | bytes 1048576 | tf_op jit(solution)/shard_map/psum | solution.py:86
  54.9 2.0 copy-start.6
  54.9 2.0 copy-start.8
  54.9 49.2 %copy-start.9 = (s32[512]{0:T(512)S(1)}, s32[512]{0:T(512)}, u32[]{:S(2)}) copy-start(s32[512]{0:T(512)} %param.10) | copy-start | bytes 6148
  163.7 4.5 %copy-start.3 = (bf16[512,2048]{1,0:T(8,128)(2,1)}, bf16[512,2048]{1,0:T(8,128)(2,1)S(1)}, u32[]{:S(2)}) copy-start(bf16[512,2048]{1,0:T(8,128)(2,1)S(1)} %select_reduce_fusion) | copy-start | bytes 6291460
  168.2 9.0 %copy-start.5 = (bf16[512,512]{1,0:T(8,128)(2,1)S(1)}, bf16[512,512]{1,0:T(8,128)(2,1)}, u32[]{:S(2)}) copy-start(bf16[512,512]{1,0:T(8,128)(2,1)} %all-reduce.4.cloned.1.call-done) | copy-start | bytes 1572868
  168.2 103.9 %all-to-all-start.2 = ((bf16[64,32,1024]{2,1,0:T(8,128)(2,1)}), bf16[64,32,1024]{2,1,0:T(8,128)(2,1)}, u32[]{:S(2)}, u32[]{:S(2)}) async-start(bf16[64,32,1024]{2,1,0:T(8,128)(2,1)} %bitcast.11), calls=%async_computation.2 | async-start | bytes 8388608 | tf_op jit(solution)/shard_map/all_to_all | solution.py:99
  177.1 2.4 copy-start.4
  287.6 2.4 copy-start.2
  298.7 13.7 %all-to-all-start.3 = ((f32[32,1,1024]{2,1,0:T(1,128)}), f32[32,1,1024]{2,1,0:T(1,128)S(1)}, u32[]{:S(2)}, u32[]{:S(2)}) async-start(f32[32,1,1024]{2,1,0:T(1,128)} %broadcast_in_dim.99), calls=%async_computation.3 | async-start | bytes 262144 | tf_op jit(solution)/shard_map/all_to_all | solution.py:127
Sparse Core Ops, SparseCore 0:
  58.6 45.5 all-reduce.3

commit v11 on v9

--- a/solution.py
+++ b/solution.py
@@ -91,7 +91,7 @@
     hard_part = jnp.sum(jnp.where(slot_grid, every_place[:, None, :], 0.0), axis=2)
     shard_scores, negative_scores = (
         lax.psum(local_part.astype(jnp.bfloat16), "section").astype(jnp.float32),
-        section_sum(hard_part.astype(jnp.bfloat16)),
+        lax.psum(hard_part.astype(jnp.bfloat16), "section").astype(jnp.float32),
     )
     shard_gradients, negative_gradients = softmax_grads(
         shard_scores, negative_scores, positive_tool, hard_valid

time: 323 us -> 321 us (level)
  blocking collectives: 20.6 us -> 27.5 us
  waiting for transfers between devices: 192 us -> 188 us
    all_to_all x1, waiting for transfers between devices: 92.6 us -> 43.9 us  [body(): lax.all_to_all(answers.reshape(group_size, capacity, features), DP, 0, 0,...]
    psum x1, waiting for transfers between devices: 0.02 us -> 47.2 us  [body(): lax.psum(local_part.astype(jnp.bfloat16), 'section').astype(jnp.float32)]
    psum x0 -> x1, blocking collectives: none -> 6.19 us  [body(): lax.psum(hard_part.astype(jnp.bfloat16), 'section').astype(jnp.float32)]
    all_to_all x1 -> x0, starting transfers between devices: 3.43 us -> none  [section_sum(): lax.all_to_all(jnp.broadcast_to(flat[None, :], (parts, flat.shape[0])), '...]
  transfers between devices with their start and end apart: 6 -> 5, of which waited for: 4 -> 4; matrix products, arithmetic and copies ran while one was open for 7% -> 4% of each run, Pallas kernels for 0% -> 0%
where the time goes in v11:
time: 321 us; the launch traced here: 320 us
  waiting for transfers between devices  188 us (59%)
  starting transfers between devices  38.7 us (12%)
  matrix products  30 us (9%)
  blocking collectives  27.5 us (9%)
  other arithmetic  16.5 us (5%)
  between operations  14.3 us (4%)
  local copies, waits for them, and re-layouts  5.25 us (2%)
    all_to_all x1, waiting for transfers between devices, body(): lax.all_to_all(sent_terms.reshape(group_size, capacity, features), DP, 0,...  88.4 us
    psum x1, waiting for transfers between devices, body(): lax.psum(local_part.astype(jnp.bfloat16), 'section').astype(jnp.float32)  47.2 us
    all_to_all x1, waiting for transfers between devices, body(): lax.all_to_all(answers.reshape(group_size, capacity, features), DP, 0, 0,...  43.9 us
    all_to_all x1, starting transfers between devices, body(): indices = lax.all_to_all(requests, DP, 0, 0, tiled=True).reshape(-1)  13.1 us
    all_to_all x1, starting transfers between devices, body(): lax.all_to_all(answers.reshape(group_size, capacity, features), DP, 0, 0,...  12.3 us
    all_to_all x1, starting transfers between devices, body(): lax.all_to_all(sent_terms.reshape(group_size, capacity, features), DP, 0,...  8.84 us
    psum x1, blocking collectives, body(): lax.psum((jnp.sum(query_scaled * query_scaled, axis=1), jnp.sum(tool_scal...  8.77 us
    all_to_all x1, waiting for transfers between devices, body(): lax.all_to_all(everyone, DP[:2], 0, 0, tiled=True)  8.12 us
  transfers between devices with their start and end apart: 5, of which 4 were waited for; matrix products, arithmetic and copies ran while one was open for 4% of the time, Pallas kernels for 0%

profile of v11, /device:TPU:1, one launch (start us, length us, event | category | flops | bytes accessed | tf_op | source)
XLA Modules:
  0.0 319.9 jit_solution(14729116447536624115)
XLA Ops:
  7.2 0.8 broadcast_compare_fusion
  8.4 0.8 copy.31
  9.4 0.8 copy.28
  11.0 1.1 select_reduce_fusion.2
  12.8 13.1 %all-to-all-start = ((s32[64,1,32]{2,1,0:T(1,128)}), s32[64,1,32]{2,1,0:T(1,128)S(1)}, u32[]{:S(2)}, u32[]{:S(2)}) async-start(s32[64,1,32]{2,1,0:T(1,128)} %bitcast), calls=%async_computation | async-start | bytes 65536 | tf_op jit(solution)/shard_map/all_to_all | solution.py:62
  26.0 2.2 fusion.9
  28.1 8.8 %all-reduce = (f32[512]{0:T(512)S(1)}, f32[512]{0:T(512)S(1)}) all-reduce(f32[512]{0:T(512)S(1)} %get-tuple-element.8, f32[512]{0:T(512)S(1)} %get-tuple-element.7), channel_id=1, replica_groups=mesh['dz'=8,'dy'=4,'dc'=2,'section'=4] {'section'}, use_global_device_ids=true, to_apply=%region_3.4 | all-reduce | flops 1024 | bytes 8192 | tf_op jit(solution)/shard_map/psum | solution.py:66
  37.4 0.7 reduce.5
  38.2 4.2 %fusion.3 = bf16[2048,1024]{1,0:T(8,128)(2,1)} fusion(s32[2048]{0:T(1024)S(1)} %eq.70, bf16[512,1024]{1,0:T(8,128)(2,1)S(1)} %copy-done.1, f32[512]{0:T(512)S(1)} %add_sqrt_fusion, f32[1024]{0:T(1024)S(1)} %copy-done.7), kind=kOutput, calls=%fused_computation.11 | convolution fusion | flops 2152726528 | bytes 5257216 | tf_op jit(solution)/shard_map/dot_general | solution.py:79
  42.5 12.3 %all-to-all-start.1 = ((bf16[64,32,1024]{2,1,0:T(8,128)(2,1)}), bf16[64,32,1024]{2,1,0:T(8,128)(2,1)}, u32[]{:S(2)}, u32[]{:S(2)}) async-start(bf16[64,32,1024]{2,1,0:T(8,128)(2,1)} %bitcast.15), calls=%async_computation.1 | async-start | bytes 8388608 | tf_op jit(solution)/shard_map/all_to_all | solution.py:80
  54.9 1.6 convolution_convert_fusion.1
  56.9 47.2 %all-reduce.3.cloned.1.call-done = bf16[512,512]{1,0:T(8,128)(2,1)} async-done(((bf16[512,512]{1,0:T(8,128)(2,1)}), bf16[512,512]{1,0:T(8,128)(2,1)}) %all-reduce.3.cloned.1.call-update) | async-done | bytes 524304 | tf_op jit(solution)/shard_map/psum | solution.py:93
  104.1 1.5 fusion.16
  105.6 43.9 %all-to-all-done.1 = bf16[64,32,1024]{2,1,0:T(8,128)(2,1)} async-done(((bf16[64,32,1024]{2,1,0:T(8,128)(2,1)}), bf16[64,32,1024]{2,1,0:T(8,128)(2,1)}, u32[]{:S(2)}, u32[]{:S(2)}) %all-to-all-start.1) | async-done | bytes 4194336 | tf_op jit(solution)/shard_map/all_to_all | solution.py:80
  149.5 4.6 %fusion.37 = f32[512,2048]{1,0:T(8,128)S(1)} fusion(bf16[2048,1024]{1,0:T(8,128)(2,1)} %bitcast.2, f32[512]{0:T(512)S(1)} %add_sqrt_fusion.1, f32[1024]{0:T(1024)S(1)} %copy-done.7, bf16[512,1024]{1,0:T(8,128)(2,1)S(1)} %copy-done), kind=kOutput, calls=%fused_computation.66 | convolution fusion | flops 2149580800 | bytes 9443328 | tf_op jit(solution)/shard_map/dot_general | solution.py:88
  154.1 1.4 select_reduce_fusion.1
  155.5 6.2 %psum.38 = bf16[512,2]{0,1:T(2,128)(2,1)S(1)} all-reduce(bf16[512,2]{0,1:T(2,128)(2,1)S(1)} %select_reduce_fusion.1), channel_id=1, replica_groups=mesh['dz'=8,'dy'=4,'dc'=2,'section'=4] {'section'}, use_global_device_ids=true, to_apply=%region_10.11 | all-reduce | flops 1024 | bytes 4096 | tf_op jit(solution)/shard_map/psum | solution.py:94
  161.8 1.9 select_reduce_fusion
  163.7 4.5 %convolution_convert_fusion = bf16[2048,1024]{1,0:T(8,128)(2,1)} fusion(bf16[512,2048]{1,0:T(8,128)(2,1)S(1)} %select_reduce_fusion, f32[512]{0:T(512)S(1)} %add_sqrt_fusion.1, f32[1024]{0:T(1024)S(1)} %copy-done.7, bf16[512,1024]{1,0:T(8,128)(2,1)S(1)} %copy-done), kind=kOutput, calls=%fused_computation.12 | convolution fusion | flops 2151677952 | bytes 7346176 | tf_op jit(solution)/shard_map/dot_general | solution.py:103
  168.2 8.8 %all-to-all-start.2 = ((bf16[64,32,1024]{2,1,0:T(8,128)(2,1)}), bf16[64,32,1024]{2,1,0:T(8,128)(2,1)}, u32[]{:S(2)}, u32[]{:S(2)}) async-start(bf16[64,32,1024]{2,1,0:T(8,128)(2,1)} %bitcast.16), calls=%async_computation.2 | async-start | bytes 8388608 | tf_op jit(solution)/shard_map/all_to_all | solution.py:106
  177.0 6.5 %fusion.41 = f32[512,1024]{1,0:T(8,128)} fusion(bf16[512,2048]{1,0:T(8,128)(2,1)} %copy-done.4, bf16[2048,1024]{1,0:T(8,128)(2,1)} %bitcast.2), kind=kOutput, calls=%fused_computation.68 | convolution fusion | flops 2147483648 | bytes 8388608 | tf_op jit(solution)/shard_map/dot_general | solution.py:111
  183.5 88.4 %all-to-all-done.2 = bf16[64,32,1024]{2,1,0:T(8,128)(2,1)} async-done(((bf16[64,32,1024]{2,1,0:T(8,128)(2,1)}), bf16[64,32,1024]{2,1,0:T(8,128)(2,1)}, u32[]{:S(2)}, u32[]{:S(2)}) %all-to-all-start.2) | async-done | bytes 4194336 | tf_op jit(solution)/shard_map/all_to_all | solution.py:106
  271.9 4.7 %fusion = f32[512,1024]{1,0:T(8,128)S(1)} fusion(bf16[2048,1024]{1,0:T(8,128)(2,1)} %bitcast.5, s32[2048]{0:T(1024)S(1)} %eq.70), kind=kOutput, calls=%fused_computation.6 | convolution fusion | flops 2148532224 | bytes 6299648 | tf_op jit(solution)/shard_map/dot_general | solution.py:115
  276.6 1.1 convolution_add_fusion
  278.2 2.9 multiply_reduce_fusion.1
  281.1 7.0 %all_to_all.31 = f32[4,1,1024]{2,1,0:T(1,128)S(1)} all-to-all(f32[4,1,1024]{2,1,0:T(1,128)S(1)} %broadcast_in_dim.105), channel_id=1, replica_groups=mesh['dz'=8,'dy'=4,'dc'=2,'section'=4] {'section'}, dimensions={0} | all-to-all | bytes 32768 | tf_op jit(solution)/shard_map/all_to_all | solution.py:37
  288.2 2.4 fusion.11
  290.6 1.9 fusion.10
  292.4 5.5 %psum.39 = f32[1024]{0:T(1024)S(1)} all-reduce(f32[1024]{0:T(1024)S(1)} %add.61), channel_id=1, replica_groups=mesh['dz'=8,'dy'=4,'dc'=2,'section'=4] {'dc'}, use_global_device_ids=true, to_apply=%region_18.19 | all-reduce | flops 1024 | bytes 8192 | tf_op jit(solution)/shard_map/psum | solution.py:130
  298.7 4.3 %all-to-all-start.4 = ((f32[32,1,1024]{2,1,0:T(1,128)}), f32[32,1,1024]{2,1,0:T(1,128)S(1)}, u32[]{:S(2)}, u32[]{:S(2)}) async-start(f32[32,1,1024]{2,1,0:T(1,128)} %broadcast_in_dim.106), calls=%async_computation.4 | async-start | bytes 262144 | tf_op jit(solution)/shard_map/all_to_all | solution.py:133
  303.0 1.2 multiply_convert_fusion.1
  304.2 8.1 %all-to-all-done.4 = f32[32,1,1024]{2,1,0:T(1,128)S(1)} async-done(((f32[32,1,1024]{2,1,0:T(1,128)}), f32[32,1,1024]{2,1,0:T(1,128)S(1)}, u32[]{:S(2)}, u32[]{:S(2)}) %all-to-all-start.4) | async-done | bytes 131104 | tf_op jit(solution)/shard_map/all_to_all | solution.py:133
  (50 shorter events, 5.1 us)
Async XLA Ops:
  7.2 31.1 %copy-start.7 = (f32[1024]{0:T(1024)S(1)}, f32[1024]{0:T(1024)}, u32[]{:S(2)}) copy-start(f32[1024]{0:T(1024)} %param.9) | copy-start | bytes 12292
  7.2 31.1 %copy-start.1 = (bf16[512,1024]{1,0:T(8,128)(2,1)S(1)}, bf16[512,1024]{1,0:T(8,128)(2,1)}, u32[]{:S(2)}) copy-start(bf16[512,1024]{1,0:T(8,128)(2,1)} %param.8) | copy-start | bytes 3145732
  12.8 24.1 %all-to-all-start = ((s32[64,1,32]{2,1,0:T(1,128)}), s32[64,1,32]{2,1,0:T(1,128)S(1)}, u32[]{:S(2)}, u32[]{:S(2)}) async-start(s32[64,1,32]{2,1,0:T(1,128)} %bitcast), calls=%async_computation | async-start | bytes 65536 | tf_op jit(solution)/shard_map/all_to_all | solution.py:62
  42.5 12.4 %copy-start = (bf16[512,1024]{1,0:T(8,128)(2,1)S(1)}, bf16[512,1024]{1,0:T(8,128)(2,1)}, u32[]{:S(2)}) copy-start(bf16[512,1024]{1,0:T(8,128)(2,1)} %param.7) | copy-start | bytes 3145732
  42.5 107.1 %all-to-all-start.1 = ((bf16[64,32,1024]{2,1,0:T(8,128)(2,1)}), bf16[64,32,1024]{2,1,0:T(8,128)(2,1)}, u32[]{:S(2)}, u32[]{:S(2)}) async-start(bf16[64,32,1024]{2,1,0:T(8,128)(2,1)} %bitcast.15), calls=%async_computation.1 | async-start | bytes 8388608 | tf_op jit(solution)/shard_map/all_to_all | solution.py:80
  54.8 49.3 %all-reduce.3.cloned.1.call-start = ((), (), s32[]{:S(2)}) async-start(), calls=%async_computation.5 | async-start | bytes 1048576 | tf_op jit(solution)/shard_map/psum | solution.py:93
  54.9 2.0 copy-start.6
  54.9 2.0 copy-start.8
  54.9 49.2 %copy-start.9 = (s32[512]{0:T(512)S(1)}, s32[512]{0:T(512)}, u32[]{:S(2)}) copy-start(s32[512]{0:T(512)} %param.10) | copy-start | bytes 6148
  163.7 4.5 %copy-start.4 = (bf16[512,2048]{1,0:T(8,128)(2,1)}, bf16[512,2048]{1,0:T(8,128)(2,1)S(1)}, u32[]{:S(2)}) copy-start(bf16[512,2048]{1,0:T(8,128)(2,1)S(1)} %select_reduce_fusion) | copy-start | bytes 6291460
  168.2 103.8 %all-to-all-start.2 = ((bf16[64,32,1024]{2,1,0:T(8,128)(2,1)}), bf16[64,32,1024]{2,1,0:T(8,128)(2,1)}, u32[]{:S(2)}, u32[]{:S(2)}) async-start(bf16[64,32,1024]{2,1,0:T(8,128)(2,1)} %bitcast.16), calls=%async_computation.2 | async-start | bytes 8388608 | tf_op jit(solution)/shard_map/all_to_all | solution.py:106
  271.9 4.7 %copy-start.5 = (bf16[512,512]{1,0:T(8,128)(2,1)S(1)}, bf16[512,512]{1,0:T(8,128)(2,1)}, u32[]{:S(2)}) copy-start(bf16[512,512]{1,0:T(8,128)(2,1)} %all-reduce.3.cloned.1.call-done) | copy-start | bytes 1572868
  276.6 1.6 copy-start.10
  278.2 2.9 copy-start.3
  288.2 2.4 copy-start.2
  298.7 13.7 %all-to-all-start.4 = ((f32[32,1,1024]{2,1,0:T(1,128)}), f32[32,1,1024]{2,1,0:T(1,128)S(1)}, u32[]{:S(2)}, u32[]{:S(2)}) async-start(f32[32,1,1024]{2,1,0:T(1,128)} %broadcast_in_dim.106), calls=%async_computation.4 | async-start | bytes 262144 | tf_op jit(solution)/shard_map/all_to_all | solution.py:133
Sparse Core Ops, SparseCore 0:
  58.6 45.5 all-reduce.2

commit v12 on v8

--- a/solution.py
+++ b/solution.py
@@ -74,6 +74,12 @@
         answers.reshape(group_size, capacity, features), DP, 0, 0, tiled=True
     ).reshape(places, features)
 
+    slot_of_query = slot_at.reshape(query_count, per_query, places).any(axis=1)
+    placed_queries = lax.dot_general(
+        slot_of_query.astype(jnp.bfloat16), query_unit, (((0,), (0,)), ((), ())),
+        preferred_element_type=jnp.float32,
+    ).astype(jnp.bfloat16)
+    back_unit, placed_queries = lax.optimization_barrier((back_unit, placed_queries))
     local_part = lax.dot_general(
         query_unit, tool_unit, (((1,), (1,)), ((), ())), preferred_element_type=jnp.float32
     )
@@ -93,9 +99,8 @@
         jnp.where(slot_grid, negative_gradients.astype(jnp.float32)[:, :, None], 0.0), axis=1
     ).astype(jnp.bfloat16)
 
-    sent_terms = lax.dot_general(
-        spread_grads, query_unit, (((0,), (0,)), ((), ())), preferred_element_type=jnp.float32
-    ).astype(jnp.bfloat16)
+    place_grads = jnp.sum(spread_grads.astype(jnp.float32), axis=0)
+    sent_terms = (place_grads[:, None] * placed_queries.astype(jnp.float32)).astype(jnp.bfloat16)
     arrived_terms = lax.all_to_all(
         sent_terms.reshape(group_size, capacity, features), DP, 0, 0, tiled=True
     ).reshape(places, features)

time: 320 us -> 319 us (level)
  waiting for transfers between devices: 186 us -> 181 us
  other arithmetic: 16.4 us -> 20.6 us
    psum x1, waiting for transfers between devices: 47.2 us -> 41.4 us  [body(): lax.psum(local_part.astype(jnp.bfloat16), 'section').astype(jnp.float32)]
  transfers between devices with their start and end apart: 5 -> 5, of which waited for: 4 -> 4; matrix products, arithmetic and copies ran while one was open for 5% -> 6% of each run, Pallas kernels for 0% -> 0%
where the time goes in v12:
time: 319 us; the launch traced here: 318 us
  waiting for transfers between devices  181 us (57%)
  starting transfers between devices  38.9 us (12%)
  matrix products  29.7 us (9%)
  blocking collectives  28.6 us (9%)
  other arithmetic  20.6 us (6%)
  between operations  14.3 us (4%)
  local copies, waits for them, and re-layouts  4.81 us (2%)
    all_to_all x1, waiting for transfers between devices, body(): lax.all_to_all(sent_terms.reshape(group_size, capacity, features), DP, 0,...  87.8 us
    all_to_all x1, waiting for transfers between devices, body(): lax.all_to_all(answers.reshape(group_size, capacity, features), DP, 0, 0,...  43.9 us
    psum x1, waiting for transfers between devices, body(): lax.psum(local_part.astype(jnp.bfloat16), 'section').astype(jnp.float32)  41.4 us
    all_to_all x1, starting transfers between devices, body(): indices = lax.all_to_all(requests, DP, 0, 0, tiled=True).reshape(-1)  13.1 us
    all_to_all x1, starting transfers between devices, body(): lax.all_to_all(answers.reshape(group_size, capacity, features), DP, 0, 0,...  12.3 us
    all_to_all x1, starting transfers between devices, body(): lax.all_to_all(sent_terms.reshape(group_size, capacity, features), DP, 0,...  8.85 us
    psum x1, blocking collectives, body(): lax.psum((jnp.sum(query_scaled * query_scaled, axis=1), jnp.sum(tool_scal...  8.77 us
    all_to_all x1, waiting for transfers between devices, body(): lax.all_to_all(everyone, DP[:2], 0, 0, tiled=True)  8.12 us
  transfers between devices with their start and end apart: 5, of which 4 were waited for; matrix products, arithmetic and copies ran while one was open for 6% of the time, Pallas kernels for 0%

profile of v12, /device:TPU:1, one launch (start us, length us, event | category | flops | bytes accessed | tf_op | source)
XLA Modules:
  0.0 318.1 jit_solution(16269188053900798501)
XLA Ops:
  7.2 0.9 copy.31
  9.4 0.8 copy.28
  11.0 1.1 select_reduce_fusion.2
  12.8 13.1 %all-to-all-start = ((s32[64,1,32]{2,1,0:T(1,128)}), s32[64,1,32]{2,1,0:T(1,128)S(1)}, u32[]{:S(2)}, u32[]{:S(2)}) async-start(s32[64,1,32]{2,1,0:T(1,128)} %bitcast), calls=%async_computation | async-start | bytes 65536 | tf_op jit(solution)/shard_map/all_to_all | solution.py:55
  26.0 2.2 fusion.10
  28.1 8.8 %all-reduce.1 = (f32[512]{0:T(512)S(1)}, f32[512]{0:T(512)S(1)}) all-reduce(f32[512]{0:T(512)S(1)} %get-tuple-element.12, f32[512]{0:T(512)S(1)} %get-tuple-element.11), channel_id=1, replica_groups=mesh['dz'=8,'dy'=4,'dc'=2,'section'=4] {'section'}, use_global_device_ids=true, to_apply=%region_3.4 | all-reduce | flops 1024 | bytes 8192 | tf_op jit(solution)/shard_map/psum | solution.py:59
  38.2 4.2 %fusion.4 = bf16[2048,1024]{1,0:T(8,128)(2,1)} fusion(s32[2048]{0:T(1024)S(1)} %eq.70, bf16[512,1024]{1,0:T(8,128)(2,1)S(1)} %copy-done.2, f32[512]{0:T(512)S(1)} %add_sqrt_fusion, f32[1024]{0:T(1024)S(1)} %copy-done.10), kind=kOutput, calls=%fused_computation.14 | convolution fusion | flops 2152726528 | bytes 5257216 | tf_op jit(solution)/shard_map/dot_general | solution.py:72
  42.5 12.3 %all-to-all-start.1 = ((bf16[64,32,1024]{2,1,0:T(8,128)(2,1)}), bf16[64,32,1024]{2,1,0:T(8,128)(2,1)}, u32[]{:S(2)}, u32[]{:S(2)}) async-start(bf16[64,32,1024]{2,1,0:T(8,128)(2,1)} %bitcast.11), calls=%async_computation.1 | async-start | bytes 8388608 | tf_op jit(solution)/shard_map/all_to_all | solution.py:73
  55.1 1.6 convolution_convert_fusion.1
  57.1 1.1 fusion
  58.2 4.5 %convolution_convert_fusion = bf16[2048,1024]{1,0:T(8,128)(2,1)} fusion(pred[512,2048]{1,0:T(8,128)(4,1)S(1)} %fusion, f32[512]{0:T(512)S(1)} %add_sqrt_fusion.1, f32[1024]{0:T(1024)S(1)} %copy-done.10, bf16[512,1024]{1,0:T(8,128)(2,1)S(1)} %copy-done.1), kind=kOutput, calls=%fused_computation.15 | convolution fusion | flops 2151677952 | bytes 6297600 | tf_op jit(solution)/shard_map/dot_general | solution.py:78
  62.7 41.4 %all-reduce.4.cloned.1.call-done = bf16[512,512]{1,0:T(8,128)(2,1)} async-done(((bf16[512,512]{1,0:T(8,128)(2,1)}), bf16[512,512]{1,0:T(8,128)(2,1)}) %all-reduce.4.cloned.1.call-update) | async-done | bytes 524304 | tf_op jit(solution)/shard_map/psum | solution.py:92
  104.1 1.5 fusion.17
  105.6 43.9 %all-to-all-done.1 = bf16[64,32,1024]{2,1,0:T(8,128)(2,1)} async-done(((bf16[64,32,1024]{2,1,0:T(8,128)(2,1)}), bf16[64,32,1024]{2,1,0:T(8,128)(2,1)}, u32[]{:S(2)}, u32[]{:S(2)}) %all-to-all-start.1) | async-done | bytes 4194336 | tf_op jit(solution)/shard_map/all_to_all | solution.py:73
  149.5 4.6 %fusion.36 = f32[512,2048]{1,0:T(8,128)S(1)} fusion(bf16[2048,1024]{1,0:T(8,128)(2,1)} %bitcast.2, f32[512]{0:T(512)S(1)} %add_sqrt_fusion.1, f32[1024]{0:T(1024)S(1)} %copy-done.10, bf16[512,1024]{1,0:T(8,128)(2,1)S(1)} %copy-done.1), kind=kOutput, calls=%fused_computation.67 | convolution fusion | flops 2149580800 | bytes 9443328 | tf_op jit(solution)/shard_map/dot_general | solution.py:87
  154.1 1.4 select_reduce_fusion.1
  155.5 6.0 %psum.52 = bf16[512,2]{0,1:T(2,128)(2,1)S(1)} all-reduce(bf16[512,2]{0,1:T(2,128)(2,1)S(1)} %select_reduce_fusion.1), channel_id=1, replica_groups=mesh['dz'=8,'dy'=4,'dc'=2,'section'=4] {'section'}, use_global_device_ids=true, to_apply=%region_11.12 | all-reduce | flops 1024 | bytes 4096 | tf_op jit(solution)/shard_map/psum | solution.py:93
  161.6 1.9 select_reduce_fusion
  163.9 2.7 multiply_convert_fusion
  166.6 8.9 %all-to-all-start.2 = ((bf16[64,32,1024]{2,1,0:T(8,128)(2,1)}), bf16[64,32,1024]{2,1,0:T(8,128)(2,1)}, u32[]{:S(2)}, u32[]{:S(2)}) async-start(bf16[64,32,1024]{2,1,0:T(8,128)(2,1)} %bitcast.10), calls=%async_computation.2 | async-start | bytes 8388608 | tf_op jit(solution)/shard_map/all_to_all | solution.py:104
  175.5 4.6 %fusion.40 = f32[512,1024]{1,0:T(8,128)S(1)} fusion(bf16[512,2048]{1,0:T(8,128)(2,1)S(1)} %select_reduce_fusion, bf16[2048,1024]{1,0:T(8,128)(2,1)} %bitcast.2), kind=kOutput, calls=%fused_computation.68 | convolution fusion | flops 2147483648 | bytes 8388608 | tf_op jit(solution)/shard_map/dot_general | solution.py:109
  180.1 2.4 convolution_add_fusion.1
  182.6 87.8 %all-to-all-done.2 = bf16[64,32,1024]{2,1,0:T(8,128)(2,1)} async-done(((bf16[64,32,1024]{2,1,0:T(8,128)(2,1)}), bf16[64,32,1024]{2,1,0:T(8,128)(2,1)}, u32[]{:S(2)}, u32[]{:S(2)}) %all-to-all-start.2) | async-done | bytes 4194336 | tf_op jit(solution)/shard_map/all_to_all | solution.py:104
  270.4 4.8 %fusion.1 = f32[512,1024]{1,0:T(8,128)S(1)} fusion(bf16[2048,1024]{1,0:T(8,128)(2,1)} %bitcast.4, s32[2048]{0:T(1024)S(1)} %eq.70), kind=kOutput, calls=%fused_computation.9 | convolution fusion | flops 2148532224 | bytes 6299648 | tf_op jit(solution)/shard_map/dot_general | solution.py:113
  275.2 2.9 multiply_reduce_fusion
  278.1 7.7 %all-reduce = (f32[512]{0:T(512)S(1)}, f32[512]{0:T(512)S(1)}) all-reduce(f32[512]{0:T(512)S(1)} %get-tuple-element.10, f32[512]{0:T(512)S(1)} %get-tuple-element.9), channel_id=1, replica_groups=mesh['dz'=8,'dy'=4,'dc'=2,'section'=4] {'section'}, use_global_device_ids=true, to_apply=%region_15.16 | all-reduce | flops 1024 | bytes 8192 | tf_op jit(solution)/shard_map/psum | solution.py:117
  285.8 2.4 fusion.12
  288.2 1.9 fusion.11
  290.1 6.1 %psum.55 = f32[1024]{0:T(1024)S(1)} all-reduce(f32[1024]{0:T(1024)S(1)} %add.65), channel_id=1, replica_groups=mesh['dz'=8,'dy'=4,'dc'=2,'section'=4] {'dc'}, use_global_device_ids=true, to_apply=%region_21.22 | all-reduce | flops 1024 | bytes 8192 | tf_op jit(solution)/shard_map/psum | solution.py:128
  296.9 4.3 %all-to-all-start.3 = ((f32[32,1,1024]{2,1,0:T(1,128)}), f32[32,1,1024]{2,1,0:T(1,128)S(1)}, u32[]{:S(2)}, u32[]{:S(2)}) async-start(f32[32,1,1024]{2,1,0:T(1,128)} %broadcast_in_dim.100), calls=%async_computation.3 | async-start | bytes 262144 | tf_op jit(solution)/shard_map/all_to_all | solution.py:131
  301.2 1.2 multiply_convert_fusion.2
  302.4 8.1 %all-to-all-done.3 = f32[32,1,1024]{2,1,0:T(1,128)S(1)} async-done(((f32[32,1,1024]{2,1,0:T(1,128)}), f32[32,1,1024]{2,1,0:T(1,128)S(1)}, u32[]{:S(2)}, u32[]{:S(2)}) %all-to-all-start.3) | async-done | bytes 131104 | tf_op jit(solution)/shard_map/all_to_all | solution.py:131
  (52 shorter events, 6.5 us)
Async XLA Ops:
  7.2 31.1 %copy-start.2 = (bf16[512,1024]{1,0:T(8,128)(2,1)S(1)}, bf16[512,1024]{1,0:T(8,128)(2,1)}, u32[]{:S(2)}) copy-start(bf16[512,1024]{1,0:T(8,128)(2,1)} %param.8) | copy-start | bytes 3145732
  7.2 31.1 %copy-start.10 = (f32[1024]{0:T(1024)S(1)}, f32[1024]{0:T(1024)}, u32[]{:S(2)}) copy-start(f32[1024]{0:T(1024)} %param.9) | copy-start | bytes 12292
  12.8 24.1 %all-to-all-start = ((s32[64,1,32]{2,1,0:T(1,128)}), s32[64,1,32]{2,1,0:T(1,128)S(1)}, u32[]{:S(2)}, u32[]{:S(2)}) async-start(s32[64,1,32]{2,1,0:T(1,128)} %bitcast), calls=%async_computation | async-start | bytes 65536 | tf_op jit(solution)/shard_map/all_to_all | solution.py:55
  42.5 12.6 %copy-start.1 = (bf16[512,1024]{1,0:T(8,128)(2,1)S(1)}, bf16[512,1024]{1,0:T(8,128)(2,1)}, u32[]{:S(2)}) copy-start(bf16[512,1024]{1,0:T(8,128)(2,1)} %param.7) | copy-start | bytes 3145732
  42.5 107.0 %all-to-all-start.1 = ((bf16[64,32,1024]{2,1,0:T(8,128)(2,1)}), bf16[64,32,1024]{2,1,0:T(8,128)(2,1)}, u32[]{:S(2)}, u32[]{:S(2)}) async-start(bf16[64,32,1024]{2,1,0:T(8,128)(2,1)} %bitcast.11), calls=%async_computation.1 | async-start | bytes 8388608 | tf_op jit(solution)/shard_map/all_to_all | solution.py:73
  54.8 49.3 %all-reduce.4.cloned.1.call-start = ((), (), s32[]{:S(2)}) async-start(), calls=%async_computation.4 | async-start | bytes 1048576 | tf_op jit(solution)/shard_map/psum | solution.py:92
  55.1 2.0 copy-start.9
  55.1 2.0 copy-start.11
  58.2 45.9 %copy-start.12 = (s32[512]{0:T(512)S(1)}, s32[512]{0:T(512)}, u32[]{:S(2)}) copy-start(s32[512]{0:T(512)} %param.10) | copy-start | bytes 6148
  161.6 2.3 copy-start
  166.6 103.8 %all-to-all-start.2 = ((bf16[64,32,1024]{2,1,0:T(8,128)(2,1)}), bf16[64,32,1024]{2,1,0:T(8,128)(2,1)}, u32[]{:S(2)}, u32[]{:S(2)}) async-start(bf16[64,32,1024]{2,1,0:T(8,128)(2,1)} %bitcast.10), calls=%async_computation.2 | async-start | bytes 8388608 | tf_op jit(solution)/shard_map/all_to_all | solution.py:104
  175.4 4.7 %copy-start.3 = (bf16[512,1024]{1,0:T(8,128)(2,1)S(1)}, bf16[512,1024]{1,0:T(8,128)(2,1)}, u32[]{:S(2)}) copy-start(bf16[512,1024]{1,0:T(8,128)(2,1)} %param.8) | copy-start | bytes 3145732
  175.5 4.7 %copy-start.7 = (bf16[512,512]{1,0:T(8,128)(2,1)S(1)}, bf16[512,512]{1,0:T(8,128)(2,1)}, u32[]{:S(2)}) copy-start(bf16[512,512]{1,0:T(8,128)(2,1)} %all-reduce.4.cloned.1.call-done) | copy-start | bytes 1572868
  270.3 4.8 %copy-start.4 = (bf16[512,1024]{1,0:T(8,128)(2,1)S(1)}, bf16[512,1024]{1,0:T(8,128)(2,1)}, u32[]{:S(2)}) copy-start(bf16[512,1024]{1,0:T(8,128)(2,1)} %param.8) | copy-start | bytes 3145732
  270.3 4.8 %copy-start.5 = (f32[512,1024]{1,0:T(8,128)S(1)}, f32[512,1024]{1,0:T(8,128)}, u32[]{:S(2)}) copy-start(f32[512,1024]{1,0:T(8,128)} %convolution_add_fusion.1) | copy-start | bytes 6291460
  270.3 4.8 %copy-start.8 = (bf16[512,512]{1,0:T(8,128)(2,1)S(1)}, bf16[512,512]{1,0:T(8,128)(2,1)}, u32[]{:S(2)}) copy-start(bf16[512,512]{1,0:T(8,128)(2,1)} %all-reduce.4.cloned.1.call-done) | copy-start | bytes 1572868
  285.8 2.4 copy-start.6
  296.9 13.7 %all-to-all-start.3 = ((f32[32,1,1024]{2,1,0:T(1,128)}), f32[32,1,1024]{2,1,0:T(1,128)S(1)}, u32[]{:S(2)}, u32[]{:S(2)}) async-start(f32[32,1,1024]{2,1,0:T(1,128)} %broadcast_in_dim.100), calls=%async_computation.3 | async-start | bytes 262144 | tf_op jit(solution)/shard_map/all_to_all | solution.py:131
Sparse Core Ops, SparseCore 0:
  58.6 45.5 all-reduce.3

commit v13 on v12

--- a/solution.py
+++ b/solution.py
@@ -29,6 +29,13 @@
         jnp.bfloat16
     )
     return (shard_gradients, negative_gradients)
+
+
+def section_sum(value):
+    parts = lax.axis_size("section")
+    flat = value.reshape(-1)
+    gathered = lax.all_to_all(jnp.broadcast_to(flat[None, :], (parts, flat.shape[0])), "section", 0, 0, tiled=True)
+    return jnp.sum(gathered.astype(jnp.float32), axis=0).reshape(value.shape)
 
 
 def body(query_hidden, tool_hidden, norm_gain, positive_tool, hard_owner, hard_row, hard_valid):
@@ -90,7 +97,7 @@
     hard_part = jnp.sum(jnp.where(slot_grid, every_place[:, None, :], 0.0), axis=2)
     shard_scores, negative_scores = (
         lax.psum(local_part.astype(jnp.bfloat16), "section").astype(jnp.float32),
-        lax.psum(hard_part.astype(jnp.bfloat16), "section").astype(jnp.float32),
+        section_sum(hard_part.astype(jnp.bfloat16)),
     )
     shard_gradients, negative_gradients = softmax_grads(
         shard_scores, negative_scores, positive_tool, hard_valid

time: 319 us -> 321 us (level)
  blocking collectives: 28.6 us -> 21.7 us
  waiting for transfers between devices: 181 us -> 185 us
    all_to_all x1, waiting for transfers between devices: 43.9 us -> 86.8 us  [body(): lax.all_to_all(answers.reshape(group_size, capacity, features), DP, 0, 0,...]
    psum x1, waiting for transfers between devices: 41.4 us -> 0.02 us  [body(): lax.psum(local_part.astype(jnp.bfloat16), 'section').astype(jnp.float32)]
    psum x1 -> x0, blocking collectives: 6.01 us -> none  [body(): lax.psum(hard_part.astype(jnp.bfloat16), 'section').astype(jnp.float32)]
    all_to_all x0 -> x1, starting transfers between devices: none -> 3.25 us  [section_sum(): lax.all_to_all(jnp.broadcast_to(flat[None, :], (parts, flat.shape[0])), '...]
  transfers between devices with their start and end apart: 5 -> 6, of which waited for: 4 -> 4; matrix products, arithmetic and copies ran while one was open for 6% -> 9% of each run, Pallas kernels for 0% -> 0%
where the time goes in v13:
time: 321 us
  waiting for transfers between devices  185 us (58%)
  starting transfers between devices  41.5 us (13%)
  matrix products  29.7 us (9%)
  blocking collectives  21.7 us (7%)
  other arithmetic  21.3 us (7%)
  between operations  14.4 us (4%)
  local copies, waits for them, and re-layouts  6.65 us (2%)
    all_to_all x1, waiting for transfers between devices, body(): lax.all_to_all(sent_terms.reshape(group_size, capacity, features), DP, 0,...  87.8 us
    all_to_all x1, waiting for transfers between devices, body(): lax.all_to_all(answers.reshape(group_size, capacity, features), DP, 0, 0,...  86.8 us
    all_to_all x1, starting transfers between devices, body(): indices = lax.all_to_all(requests, DP, 0, 0, tiled=True).reshape(-1)  13.1 us
    all_to_all x1, starting transfers between devices, body(): lax.all_to_all(answers.reshape(group_size, capacity, features), DP, 0, 0,...  12.3 us
    psum x1, blocking collectives, body(): lax.psum((jnp.sum(query_scaled * query_scaled, axis=1), jnp.sum(tool_scal...  8.77 us
    all_to_all x1, starting transfers between devices, body(): lax.all_to_all(sent_terms.reshape(group_size, capacity, features), DP, 0,...  8.27 us
    all_to_all x1, waiting for transfers between devices, body(): lax.all_to_all(everyone, DP[:2], 0, 0, tiled=True)  8.12 us
    psum x1, blocking collectives, body(): lax.psum((jnp.sum(query_unit32 * query_pull, axis=1), jnp.sum(tool_unit32...  6.85 us
  transfers between devices with their start and end apart: 6, of which 4 were waited for; matrix products, arithmetic and copies ran while one was open for 9% of the time, Pallas kernels for 0%

profile of v13, /device:TPU:1, one launch (start us, length us, event | category | flops | bytes accessed | tf_op | source)
XLA Modules:
  0.0 320.6 jit_solution(11834985501411357785)
XLA Ops:
  7.2 0.9 copy.46
  9.4 0.8 copy.43
  11.0 1.1 select_reduce_fusion.2
  12.8 13.1 %all-to-all-start = ((s32[64,1,32]{2,1,0:T(1,128)}), s32[64,1,32]{2,1,0:T(1,128)S(1)}, u32[]{:S(2)}, u32[]{:S(2)}) async-start(s32[64,1,32]{2,1,0:T(1,128)} %bitcast), calls=%async_computation | async-start | bytes 65536 | tf_op jit(solution)/shard_map/all_to_all | solution.py:62
  26.0 2.2 fusion.10
  28.1 8.8 %all-reduce.1 = (f32[512]{0:T(512)S(1)}, f32[512]{0:T(512)S(1)}) all-reduce(f32[512]{0:T(512)S(1)} %get-tuple-element.12, f32[512]{0:T(512)S(1)} %get-tuple-element.11), channel_id=1, replica_groups=mesh['dz'=8,'dy'=4,'dc'=2,'section'=4] {'section'}, use_global_device_ids=true, to_apply=%region_3.4 | all-reduce | flops 1024 | bytes 8192 | tf_op jit(solution)/shard_map/psum | solution.py:66
  38.2 4.2 %fusion.4 = bf16[2048,1024]{1,0:T(8,128)(2,1)} fusion(s32[2048]{0:T(1024)S(1)} %eq.70, bf16[512,1024]{1,0:T(8,128)(2,1)S(1)} %copy-done.2, f32[512]{0:T(512)S(1)} %add_sqrt_fusion, f32[1024]{0:T(1024)S(1)} %copy-done.10), kind=kOutput, calls=%fused_computation.14 | convolution fusion | flops 2152726528 | bytes 5257216 | tf_op jit(solution)/shard_map/dot_general | solution.py:79
  42.5 12.3 %all-to-all-start.1 = ((bf16[64,32,1024]{2,1,0:T(8,128)(2,1)}), bf16[64,32,1024]{2,1,0:T(8,128)(2,1)}, u32[]{:S(2)}, u32[]{:S(2)}) async-start(bf16[64,32,1024]{2,1,0:T(8,128)(2,1)} %bitcast.11), calls=%async_computation.1 | async-start | bytes 8388608 | tf_op jit(solution)/shard_map/all_to_all | solution.py:80
  55.1 1.6 convolution_convert_fusion.1
  57.1 1.1 fusion
  58.2 4.5 %convolution_convert_fusion = bf16[2048,1024]{1,0:T(8,128)(2,1)} fusion(pred[512,2048]{1,0:T(8,128)(4,1)S(1)} %fusion, f32[512]{0:T(512)S(1)} %add_sqrt_fusion.1, f32[1024]{0:T(1024)S(1)} %copy-done.10, bf16[512,1024]{1,0:T(8,128)(2,1)S(1)} %copy-done.1), kind=kOutput, calls=%fused_computation.15 | convolution fusion | flops 2151677952 | bytes 6297600 | tf_op jit(solution)/shard_map/dot_general | solution.py:85
  62.7 86.8 %all-to-all-done.1 = bf16[64,32,1024]{2,1,0:T(8,128)(2,1)} async-done(((bf16[64,32,1024]{2,1,0:T(8,128)(2,1)}), bf16[64,32,1024]{2,1,0:T(8,128)(2,1)}, u32[]{:S(2)}, u32[]{:S(2)}) %all-to-all-start.1) | async-done | bytes 4194336 | tf_op jit(solution)/shard_map/all_to_all | solution.py:80
  149.5 4.6 %fusion.36 = f32[512,2048]{1,0:T(8,128)S(1)} fusion(bf16[2048,1024]{1,0:T(8,128)(2,1)} %bitcast.2, f32[512]{0:T(512)S(1)} %add_sqrt_fusion.1, f32[1024]{0:T(1024)S(1)} %copy-done.10, bf16[512,1024]{1,0:T(8,128)(2,1)S(1)} %copy-done.1), kind=kOutput, calls=%fused_computation.69 | convolution fusion | flops 2149580800 | bytes 9443328 | tf_op jit(solution)/shard_map/dot_general | solution.py:94
  154.1 1.4 select_reduce_fusion.1
  157.8 3.2 %all-to-all-start.2 = ((bf16[4,2,512]{2,1,0:T(2,128)(2,1)}), bf16[4,2,512]{2,1,0:T(2,128)(2,1)S(1)}, u32[]{:S(2)}, u32[]{:S(2)}) async-start(bf16[4,2,512]{2,1,0:T(2,128)(2,1)} %reshape.122), calls=%async_computation.2 | async-start | bytes 16384 | tf_op jit(solution)/shard_map/all_to_all | solution.py:37
  161.0 1.5 fusion.17
  162.5 2.6 all-to-all-done.2
  165.6 1.9 select_reduce_fusion
  167.9 2.7 multiply_convert_fusion
  170.6 8.3 %all-to-all-start.3 = ((bf16[64,32,1024]{2,1,0:T(8,128)(2,1)}), bf16[64,32,1024]{2,1,0:T(8,128)(2,1)}, u32[]{:S(2)}, u32[]{:S(2)}) async-start(bf16[64,32,1024]{2,1,0:T(8,128)(2,1)} %bitcast.10), calls=%async_computation.3 | async-start | bytes 8388608 | tf_op jit(solution)/shard_map/all_to_all | solution.py:111
  178.9 4.6 %fusion.40 = f32[512,1024]{1,0:T(8,128)S(1)} fusion(bf16[512,2048]{1,0:T(8,128)(2,1)S(1)} %select_reduce_fusion, bf16[2048,1024]{1,0:T(8,128)(2,1)} %bitcast.2), kind=kOutput, calls=%fused_computation.70 | convolution fusion | flops 2147483648 | bytes 8388608 | tf_op jit(solution)/shard_map/dot_general | solution.py:116
  183.5 2.4 convolution_add_fusion.1
  186.0 87.8 %all-to-all-done.3 = bf16[64,32,1024]{2,1,0:T(8,128)(2,1)} async-done(((bf16[64,32,1024]{2,1,0:T(8,128)(2,1)}), bf16[64,32,1024]{2,1,0:T(8,128)(2,1)}, u32[]{:S(2)}, u32[]{:S(2)}) %all-to-all-start.3) | async-done | bytes 4194336 | tf_op jit(solution)/shard_map/all_to_all | solution.py:111
  273.7 4.8 %fusion.1 = f32[512,1024]{1,0:T(8,128)S(1)} fusion(bf16[2048,1024]{1,0:T(8,128)(2,1)} %bitcast.4, s32[2048]{0:T(1024)S(1)} %eq.70), kind=kOutput, calls=%fused_computation.9 | convolution fusion | flops 2148532224 | bytes 6299648 | tf_op jit(solution)/shard_map/dot_general | solution.py:120
  278.6 2.9 multiply_reduce_fusion
  281.5 6.8 %all-reduce = (f32[512]{0:T(512)S(1)}, f32[512]{0:T(512)S(1)}) all-reduce(f32[512]{0:T(512)S(1)} %get-tuple-element.10, f32[512]{0:T(512)S(1)} %get-tuple-element.9), channel_id=1, replica_groups=mesh['dz'=8,'dy'=4,'dc'=2,'section'=4] {'section'}, use_global_device_ids=true, to_apply=%region_15.16 | all-reduce | flops 1024 | bytes 8192 | tf_op jit(solution)/shard_map/psum | solution.py:124
  288.3 2.4 fusion.12
  290.7 1.9 fusion.11
  292.6 6.1 %psum.47 = f32[1024]{0:T(1024)S(1)} all-reduce(f32[1024]{0:T(1024)S(1)} %add.63), channel_id=1, replica_groups=mesh['dz'=8,'dy'=4,'dc'=2,'section'=4] {'dc'}, use_global_device_ids=true, to_apply=%region_21.22 | all-reduce | flops 1024 | bytes 8192 | tf_op jit(solution)/shard_map/psum | solution.py:135
  299.4 4.3 %all-to-all-start.4 = ((f32[32,1,1024]{2,1,0:T(1,128)}), f32[32,1,1024]{2,1,0:T(1,128)S(1)}, u32[]{:S(2)}, u32[]{:S(2)}) async-start(f32[32,1,1024]{2,1,0:T(1,128)} %broadcast_in_dim.106), calls=%async_computation.4 | async-start | bytes 262144 | tf_op jit(solution)/shard_map/all_to_all | solution.py:138
  303.7 1.2 multiply_convert_fusion.2
  304.9 8.1 %all-to-all-done.4 = f32[32,1,1024]{2,1,0:T(1,128)S(1)} async-done(((f32[32,1,1024]{2,1,0:T(1,128)}), f32[32,1,1024]{2,1,0:T(1,128)S(1)}, u32[]{:S(2)}, u32[]{:S(2)}) %all-to-all-start.4) | async-done | bytes 131104 | tf_op jit(solution)/shard_map/all_to_all | solution.py:138
  (64 shorter events, 9.1 us)
Async XLA Ops:
  7.2 31.1 %copy-start.2 = (bf16[512,1024]{1,0:T(8,128)(2,1)S(1)}, bf16[512,1024]{1,0:T(8,128)(2,1)}, u32[]{:S(2)}) copy-start(bf16[512,1024]{1,0:T(8,128)(2,1)} %param.8) | copy-start | bytes 3145732
  7.2 31.1 %copy-start.10 = (f32[1024]{0:T(1024)S(1)}, f32[1024]{0:T(1024)}, u32[]{:S(2)}) copy-start(f32[1024]{0:T(1024)} %param.9) | copy-start | bytes 12292
  12.8 24.1 %all-to-all-start = ((s32[64,1,32]{2,1,0:T(1,128)}), s32[64,1,32]{2,1,0:T(1,128)S(1)}, u32[]{:S(2)}, u32[]{:S(2)}) async-start(s32[64,1,32]{2,1,0:T(1,128)} %bitcast), calls=%async_computation | async-start | bytes 65536 | tf_op jit(solution)/shard_map/all_to_all | solution.py:62
  42.5 12.6 %copy-start.1 = (bf16[512,1024]{1,0:T(8,128)(2,1)S(1)}, bf16[512,1024]{1,0:T(8,128)(2,1)}, u32[]{:S(2)}) copy-start(bf16[512,1024]{1,0:T(8,128)(2,1)} %param.7) | copy-start | bytes 3145732
  42.5 107.0 %all-to-all-start.1 = ((bf16[64,32,1024]{2,1,0:T(8,128)(2,1)}), bf16[64,32,1024]{2,1,0:T(8,128)(2,1)}, u32[]{:S(2)}, u32[]{:S(2)}) async-start(bf16[64,32,1024]{2,1,0:T(8,128)(2,1)} %bitcast.11), calls=%async_computation.1 | async-start | bytes 8388608 | tf_op jit(solution)/shard_map/all_to_all | solution.py:80
  54.8 106.2 %all-reduce.4.cloned.1.call-start = ((), (), s32[]{:S(2)}) async-start(), calls=%async_computation.5 | async-start | bytes 1048576 | tf_op jit(solution)/shard_map/psum | solution.py:99
  55.1 2.0 copy-start.9
  55.1 2.0 copy-start.11
  154.1 6.9 %copy-start.12 = (s32[512]{0:T(512)S(1)}, s32[512]{0:T(512)}, u32[]{:S(2)}) copy-start(s32[512]{0:T(512)} %param.10) | copy-start | bytes 6148
  157.8 7.4 %all-to-all-start.2 = ((bf16[4,2,512]{2,1,0:T(2,128)(2,1)}), bf16[4,2,512]{2,1,0:T(2,128)(2,1)S(1)}, u32[]{:S(2)}, u32[]{:S(2)}) async-start(bf16[4,2,512]{2,1,0:T(2,128)(2,1)} %reshape.122), calls=%async_computation.2 | async-start | bytes 16384 | tf_op jit(solution)/shard_map/all_to_all | solution.py:37
  165.6 2.3 copy-start
  170.6 103.2 %all-to-all-start.3 = ((bf16[64,32,1024]{2,1,0:T(8,128)(2,1)}), bf16[64,32,1024]{2,1,0:T(8,128)(2,1)}, u32[]{:S(2)}, u32[]{:S(2)}) async-start(bf16[64,32,1024]{2,1,0:T(8,128)(2,1)} %bitcast.10), calls=%async_computation.3 | async-start | bytes 8388608 | tf_op jit(solution)/shard_map/all_to_all | solution.py:111
  178.8 4.7 %copy-start.3 = (bf16[512,1024]{1,0:T(8,128)(2,1)S(1)}, bf16[512,1024]{1,0:T(8,128)(2,1)}, u32[]{:S(2)}) copy-start(bf16[512,1024]{1,0:T(8,128)(2,1)} %param.8) | copy-start | bytes 3145732
  178.9 4.7 %copy-start.7 = (bf16[512,512]{1,0:T(8,128)(2,1)S(1)}, bf16[512,512]{1,0:T(8,128)(2,1)}, u32[]{:S(2)}) copy-start(bf16[512,512]{1,0:T(8,128)(2,1)} %all-reduce.4.cloned.1.call-done) | copy-start | bytes 1572868
  273.7 4.8 %copy-start.4 = (bf16[512,1024]{1,0:T(8,128)(2,1)S(1)}, bf16[512,1024]{1,0:T(8,128)(2,1)}, u32[]{:S(2)}) copy-start(bf16[512,1024]{1,0:T(8,128)(2,1)} %param.8) | copy-start | bytes 3145732
  273.7 4.8 %copy-start.5 = (f32[512,1024]{1,0:T(8,128)S(1)}, f32[512,1024]{1,0:T(8,128)}, u32[]{:S(2)}) copy-start(f32[512,1024]{1,0:T(8,128)} %convolution_add_fusion.1) | copy-start | bytes 6291460
  273.7 4.8 %copy-start.8 = (bf16[512,512]{1,0:T(8,128)(2,1)S(1)}, bf16[512,512]{1,0:T(8,128)(2,1)}, u32[]{:S(2)}) copy-start(bf16[512,512]{1,0:T(8,128)(2,1)} %all-reduce.4.cloned.1.call-done) | copy-start | bytes 1572868
  288.3 2.4 copy-start.6
  299.4 13.7 %all-to-all-start.4 = ((f32[32,1,1024]{2,1,0:T(1,128)}), f32[32,1,1024]{2,1,0:T(1,128)S(1)}, u32[]{:S(2)}, u32[]{:S(2)}) async-start(f32[32,1,1024]{2,1,0:T(1,128)} %broadcast_in_dim.106), calls=%async_computation.4 | async-start | bytes 262144 | tf_op jit(solution)/shard_map/all_to_all | solution.py:138
Sparse Core Ops, SparseCore 0:
  58.6 45.5 all-reduce.3

commit v14 on v12

--- a/solution.py
+++ b/solution.py
@@ -107,6 +107,11 @@
 
     query_pull = jnp.dot(shard_gradients, tool_unit, preferred_element_type=jnp.float32)
     query_pull = query_pull + jnp.dot(spread_grads, back_unit, preferred_element_type=jnp.float32)
+    query_inner = lax.psum(jnp.sum(query_unit32 * query_pull, axis=1), "section")
+    query_back = (query_pull - query_unit32 * query_inner[:, None]) / query_norm[:, None]
+    query_grad = (query_back * norm_gain).astype(jnp.bfloat16)
+    query_gain = jnp.sum(query_back * query_hidden.astype(jnp.float32), axis=0)
+    arrived_terms, query_grad, query_gain = lax.optimization_barrier((arrived_terms, query_grad, query_gain))
     tool_pull = lax.dot_general(
         shard_gradients, query_unit, (((0,), (0,)), ((), ())), preferred_element_type=jnp.float32
     )
@@ -114,17 +119,10 @@
         pick_tool, arrived_terms, (((0,), (0,)), ((), ())), preferred_element_type=jnp.float32
     )
 
-    query_inner, tool_inner = lax.psum(
-        (jnp.sum(query_unit32 * query_pull, axis=1), jnp.sum(tool_unit32 * tool_pull, axis=1)),
-        "section",
-    )
-    query_back = (query_pull - query_unit32 * query_inner[:, None]) / query_norm[:, None]
+    tool_inner = lax.psum(jnp.sum(tool_unit32 * tool_pull, axis=1), "section")
     tool_back = (tool_pull - tool_unit32 * tool_inner[:, None]) / tool_norm[:, None]
-    query_grad = (query_back * norm_gain).astype(jnp.bfloat16)
     tool_grad = (tool_back * norm_gain).astype(jnp.bfloat16)
-    gain_terms = jnp.sum(query_back * query_hidden.astype(jnp.float32), axis=0) + jnp.sum(
-        tool_back * tool_hidden.astype(jnp.float32), axis=0
-    )
+    gain_terms = query_gain + jnp.sum(tool_back * tool_hidden.astype(jnp.float32), axis=0)
     pair_terms = lax.psum(gain_terms, "dc")
     chips = lax.axis_size(DP[:2])
     everyone = jnp.broadcast_to(pair_terms[None, :], (chips, gain_terms.shape[0]))

time: 319 us -> 317 us (level)
  waiting for transfers between devices: 181 us -> 172 us
  blocking collectives: 28.6 us -> 37.1 us
    all_to_all x1, waiting for transfers between devices: 87.8 us -> 78.6 us  [body(): lax.all_to_all(sent_terms.reshape(group_size, capacity, features), DP, 0,...]
    psum x1 -> x2, blocking collectives: 7.7 us -> 16.2 us  [the longest x1 8.52 us: body(): lax.psum(jnp.sum(query_unit32 * query_pull, axis=1), 'section')]
where the time goes in v14:
time: 317 us; the launch traced here: 316 us
  waiting for transfers between devices  172 us (54%)
  starting transfers between devices  38.9 us (12%)
  blocking collectives  37.1 us (12%)
  matrix products  28.1 us (9%)
  other arithmetic  20.7 us (7%)
  between operations  14.3 us (5%)
  local copies, waits for them, and re-layouts  4.81 us (2%)
    all_to_all x1, waiting for transfers between devices, body(): lax.all_to_all(sent_terms.reshape(group_size, capacity, features), DP, 0,...  78.6 us
    all_to_all x1, waiting for transfers between devices, body(): lax.all_to_all(answers.reshape(group_size, capacity, features), DP, 0, 0,...  43.9 us
    psum x1, waiting for transfers between devices, body(): lax.psum(local_part.astype(jnp.bfloat16), 'section').astype(jnp.float32)  41.4 us
    all_to_all x1, starting transfers between devices, body(): indices = lax.all_to_all(requests, DP, 0, 0, tiled=True).reshape(-1)  13.1 us
    all_to_all x1, starting transfers between devices, body(): lax.all_to_all(answers.reshape(group_size, capacity, features), DP, 0, 0,...  12.3 us
    all_to_all x1, starting transfers between devices, body(): lax.all_to_all(sent_terms.reshape(group_size, capacity, features), DP, 0,...  8.85 us
    psum x1, blocking collectives, body(): lax.psum((jnp.sum(query_scaled * query_scaled, axis=1), jnp.sum(tool_scal...  8.77 us
    psum x1, blocking collectives, body(): lax.psum(jnp.sum(query_unit32 * query_pull, axis=1), 'section')  8.52 us
  transfers between devices with their start and end apart: 5, of which 4 were waited for; matrix products, arithmetic and copies ran while one was open for 6% of the time, Pallas kernels for 0%

profile of v14, /device:TPU:1, one launch (start us, length us, event | category | flops | bytes accessed | tf_op | source)
XLA Modules:
  0.0 316.0 jit_solution(7179788888642880320)
XLA Ops:
  7.2 0.9 copy.28
  11.0 1.1 select_reduce_fusion.2
  12.8 13.1 %all-to-all-start = ((s32[64,1,32]{2,1,0:T(1,128)}), s32[64,1,32]{2,1,0:T(1,128)S(1)}, u32[]{:S(2)}, u32[]{:S(2)}) async-start(s32[64,1,32]{2,1,0:T(1,128)} %bitcast), calls=%async_computation | async-start | bytes 65536 | tf_op jit(solution)/shard_map/all_to_all | solution.py:55
  26.0 2.2 fusion.10
  28.1 8.8 %all-reduce = (f32[512]{0:T(512)S(1)}, f32[512]{0:T(512)S(1)}) all-reduce(f32[512]{0:T(512)S(1)} %get-tuple-element.16, f32[512]{0:T(512)S(1)} %get-tuple-element.15), channel_id=1, replica_groups=mesh['dz'=8,'dy'=4,'dc'=2,'section'=4] {'section'}, use_global_device_ids=true, to_apply=%region_5.6 | all-reduce | flops 1024 | bytes 8192 | tf_op jit(solution)/shard_map/psum | solution.py:59
  38.2 4.2 %fusion.4 = bf16[2048,1024]{1,0:T(8,128)(2,1)} fusion(s32[2048]{0:T(1024)S(1)} %eq.68, bf16[512,1024]{1,0:T(8,128)(2,1)S(1)} %copy-done.2, f32[512]{0:T(512)S(1)} %add_sqrt_fusion, f32[1024]{0:T(1024)S(1)} %copy-done.7), kind=kOutput, calls=%fused_computation.14 | convolution fusion | flops 2152726528 | bytes 5257216 | tf_op jit(solution)/shard_map/dot_general | solution.py:72
  42.5 12.3 %all-to-all-start.1 = ((bf16[64,32,1024]{2,1,0:T(8,128)(2,1)}), bf16[64,32,1024]{2,1,0:T(8,128)(2,1)}, u32[]{:S(2)}, u32[]{:S(2)}) async-start(bf16[64,32,1024]{2,1,0:T(8,128)(2,1)} %bitcast.11), calls=%async_computation.1 | async-start | bytes 8388608 | tf_op jit(solution)/shard_map/all_to_all | solution.py:73
  55.1 1.6 convolution_convert_fusion.1
  57.1 1.1 fusion
  58.2 4.5 %convolution_convert_fusion = bf16[2048,1024]{1,0:T(8,128)(2,1)} fusion(pred[512,2048]{1,0:T(8,128)(4,1)S(1)} %fusion, f32[512]{0:T(512)S(1)} %add_sqrt_fusion.1, f32[1024]{0:T(1024)S(1)} %copy-done.7, bf16[512,1024]{1,0:T(8,128)(2,1)S(1)} %copy-done.1), kind=kOutput, calls=%fused_computation.15 | convolution fusion | flops 2151677952 | bytes 6297600 | tf_op jit(solution)/shard_map/dot_general | solution.py:78
  62.7 41.4 %all-reduce.3.cloned.1.call-done = bf16[512,512]{1,0:T(8,128)(2,1)} async-done(((bf16[512,512]{1,0:T(8,128)(2,1)}), bf16[512,512]{1,0:T(8,128)(2,1)}) %all-reduce.3.cloned.1.call-update) | async-done | bytes 524304 | tf_op jit(solution)/shard_map/psum | solution.py:92
  104.1 1.5 fusion.18
  105.6 43.9 %all-to-all-done.1 = bf16[64,32,1024]{2,1,0:T(8,128)(2,1)} async-done(((bf16[64,32,1024]{2,1,0:T(8,128)(2,1)}), bf16[64,32,1024]{2,1,0:T(8,128)(2,1)}, u32[]{:S(2)}, u32[]{:S(2)}) %all-to-all-start.1) | async-done | bytes 4194336 | tf_op jit(solution)/shard_map/all_to_all | solution.py:73
  149.5 4.6 %fusion.37 = f32[512,2048]{1,0:T(8,128)S(1)} fusion(bf16[2048,1024]{1,0:T(8,128)(2,1)} %bitcast.2, f32[512]{0:T(512)S(1)} %add_sqrt_fusion.1, f32[1024]{0:T(1024)S(1)} %copy-done.7, bf16[512,1024]{1,0:T(8,128)(2,1)S(1)} %copy-done.1), kind=kOutput, calls=%fused_computation.67 | convolution fusion | flops 2149580800 | bytes 9443328 | tf_op jit(solution)/shard_map/dot_general | solution.py:87
  154.1 1.4 select_reduce_fusion.1
  155.5 6.0 %psum.51 = bf16[512,2]{0,1:T(2,128)(2,1)S(1)} all-reduce(bf16[512,2]{0,1:T(2,128)(2,1)S(1)} %select_reduce_fusion.1), channel_id=1, replica_groups=mesh['dz'=8,'dy'=4,'dc'=2,'section'=4] {'section'}, use_global_device_ids=true, to_apply=%region_8.9 | all-reduce | flops 1024 | bytes 4096 | tf_op jit(solution)/shard_map/psum | solution.py:93
  161.6 1.9 select_reduce_fusion
  163.9 2.7 multiply_convert_fusion
  166.6 8.8 %all-to-all-start.2 = ((bf16[64,32,1024]{2,1,0:T(8,128)(2,1)}), bf16[64,32,1024]{2,1,0:T(8,128)(2,1)}, u32[]{:S(2)}, u32[]{:S(2)}) async-start(bf16[64,32,1024]{2,1,0:T(8,128)(2,1)} %bitcast.10), calls=%async_computation.2 | async-start | bytes 8388608 | tf_op jit(solution)/shard_map/all_to_all | solution.py:104
  175.5 4.6 %fusion.40 = f32[512,1024]{1,0:T(8,128)S(1)} fusion(bf16[512,2048]{1,0:T(8,128)(2,1)S(1)} %select_reduce_fusion, bf16[2048,1024]{1,0:T(8,128)(2,1)} %bitcast.2), kind=kOutput, calls=%fused_computation.68 | convolution fusion | flops 2147483648 | bytes 8388608 | tf_op jit(solution)/shard_map/dot_general | solution.py:109
  180.1 1.3 multiply_reduce_fusion.1
  181.4 8.5 %psum.53 = f32[512]{0:T(512)S(1)} all-reduce(f32[512]{0:T(512)S(1)} %get-tuple-element.25), channel_id=1, replica_groups=mesh['dz'=8,'dy'=4,'dc'=2,'section'=4] {'section'}, use_global_device_ids=true, to_apply=%region_16.17 | all-reduce | flops 512 | bytes 4096 | tf_op jit(solution)/shard_map/psum | solution.py:110
  190.6 1.2 multiply_convert_fusion.2
  191.8 78.6 %all-to-all-done.2 = bf16[64,32,1024]{2,1,0:T(8,128)(2,1)} async-done(((bf16[64,32,1024]{2,1,0:T(8,128)(2,1)}), bf16[64,32,1024]{2,1,0:T(8,128)(2,1)}, u32[]{:S(2)}, u32[]{:S(2)}) %all-to-all-start.2) | async-done | bytes 4194336 | tf_op jit(solution)/shard_map/all_to_all | solution.py:104
  270.3 4.7 %fusion.1 = f32[512,1024]{1,0:T(8,128)S(1)} fusion(bf16[2048,1024]{1,0:T(8,128)(2,1)} %bitcast.4, s32[2048]{0:T(1024)S(1)} %eq.68), kind=kOutput, calls=%fused_computation.9 | convolution fusion | flops 2148532224 | bytes 6299648 | tf_op jit(solution)/shard_map/dot_general | solution.py:118
  275.1 2.6 multiply_reduce_fusion
  277.7 7.7 %psum.54 = f32[512]{0:T(512)S(1)} all-reduce(f32[512]{0:T(512)S(1)} %get-tuple-element.27), channel_id=1, replica_groups=mesh['dz'=8,'dy'=4,'dc'=2,'section'=4] {'section'}, use_global_device_ids=true, to_apply=%region_19.20 | all-reduce | flops 512 | bytes 4096 | tf_op jit(solution)/shard_map/psum | solution.py:122
  285.4 2.6 fusion.12
  287.9 6.1 %psum.55 = f32[1024]{0:T(1024)S(1)} all-reduce(f32[1024]{0:T(1024)S(1)} %add.65), channel_id=1, replica_groups=mesh['dz'=8,'dy'=4,'dc'=2,'section'=4] {'dc'}, use_global_device_ids=true, to_apply=%region_21.22 | all-reduce | flops 1024 | bytes 8192 | tf_op jit(solution)/shard_map/psum | solution.py:126
  294.8 4.3 %all-to-all-start.3 = ((f32[32,1,1024]{2,1,0:T(1,128)}), f32[32,1,1024]{2,1,0:T(1,128)S(1)}, u32[]{:S(2)}, u32[]{:S(2)}) async-start(f32[32,1,1024]{2,1,0:T(1,128)} %broadcast_in_dim.100), calls=%async_computation.3 | async-start | bytes 262144 | tf_op jit(solution)/shard_map/all_to_all | solution.py:129
  299.1 1.2 multiply_convert_fusion.1
  300.3 8.1 %all-to-all-done.3 = f32[32,1,1024]{2,1,0:T(1,128)S(1)} async-done(((f32[32,1,1024]{2,1,0:T(1,128)}), f32[32,1,1024]{2,1,0:T(1,128)S(1)}, u32[]{:S(2)}, u32[]{:S(2)}) %all-to-all-start.3) | async-done | bytes 131104 | tf_op jit(solution)/shard_map/all_to_all | solution.py:129
  (50 shorter events, 8.0 us)
Async XLA Ops:
  7.2 31.1 %copy-start.2 = (bf16[512,1024]{1,0:T(8,128)(2,1)S(1)}, bf16[512,1024]{1,0:T(8,128)(2,1)}, u32[]{:S(2)}) copy-start(bf16[512,1024]{1,0:T(8,128)(2,1)} %param.8) | copy-start | bytes 3145732
  7.2 31.1 %copy-start.7 = (f32[1024]{0:T(1024)S(1)}, f32[1024]{0:T(1024)}, u32[]{:S(2)}) copy-start(f32[1024]{0:T(1024)} %param.9) | copy-start | bytes 12292
  12.8 24.1 %all-to-all-start = ((s32[64,1,32]{2,1,0:T(1,128)}), s32[64,1,32]{2,1,0:T(1,128)S(1)}, u32[]{:S(2)}, u32[]{:S(2)}) async-start(s32[64,1,32]{2,1,0:T(1,128)} %bitcast), calls=%async_computation | async-start | bytes 65536 | tf_op jit(solution)/shard_map/all_to_all | solution.py:55
  42.5 12.6 %copy-start.1 = (bf16[512,1024]{1,0:T(8,128)(2,1)S(1)}, bf16[512,1024]{1,0:T(8,128)(2,1)}, u32[]{:S(2)}) copy-start(bf16[512,1024]{1,0:T(8,128)(2,1)} %param.7) | copy-start | bytes 3145732
  42.5 107.1 %all-to-all-start.1 = ((bf16[64,32,1024]{2,1,0:T(8,128)(2,1)}), bf16[64,32,1024]{2,1,0:T(8,128)(2,1)}, u32[]{:S(2)}, u32[]{:S(2)}) async-start(bf16[64,32,1024]{2,1,0:T(8,128)(2,1)} %bitcast.11), calls=%async_computation.1 | async-start | bytes 8388608 | tf_op jit(solution)/shard_map/all_to_all | solution.py:73
  54.8 49.3 %all-reduce.3.cloned.1.call-start = ((), (), s32[]{:S(2)}) async-start(), calls=%async_computation.4 | async-start | bytes 1048576 | tf_op jit(solution)/shard_map/psum | solution.py:92
  55.1 2.0 copy-start.8
  55.1 2.0 copy-start.9
  58.2 45.9 %copy-start.10 = (s32[512]{0:T(512)S(1)}, s32[512]{0:T(512)}, u32[]{:S(2)}) copy-start(s32[512]{0:T(512)} %param.10) | copy-start | bytes 6148
  161.6 2.3 copy-start
  166.6 103.7 %all-to-all-start.2 = ((bf16[64,32,1024]{2,1,0:T(8,128)(2,1)}), bf16[64,32,1024]{2,1,0:T(8,128)(2,1)}, u32[]{:S(2)}, u32[]{:S(2)}) async-start(bf16[64,32,1024]{2,1,0:T(8,128)(2,1)} %bitcast.10), calls=%async_computation.2 | async-start | bytes 8388608 | tf_op jit(solution)/shard_map/all_to_all | solution.py:104
  175.4 4.7 %copy-start.3 = (bf16[512,1024]{1,0:T(8,128)(2,1)S(1)}, bf16[512,1024]{1,0:T(8,128)(2,1)}, u32[]{:S(2)}) copy-start(bf16[512,1024]{1,0:T(8,128)(2,1)} %param.8) | copy-start | bytes 3145732
  175.5 4.7 %copy-start.5 = (bf16[512,512]{1,0:T(8,128)(2,1)S(1)}, bf16[512,512]{1,0:T(8,128)(2,1)}, u32[]{:S(2)}) copy-start(bf16[512,512]{1,0:T(8,128)(2,1)} %all-reduce.3.cloned.1.call-done) | copy-start | bytes 1572868
  270.3 4.8 %copy-start.4 = (bf16[512,1024]{1,0:T(8,128)(2,1)S(1)}, bf16[512,1024]{1,0:T(8,128)(2,1)}, u32[]{:S(2)}) copy-start(bf16[512,1024]{1,0:T(8,128)(2,1)} %param.8) | copy-start | bytes 3145732
  270.3 4.8 %copy-start.6 = (bf16[512,512]{1,0:T(8,128)(2,1)S(1)}, bf16[512,512]{1,0:T(8,128)(2,1)}, u32[]{:S(2)}) copy-start(bf16[512,512]{1,0:T(8,128)(2,1)} %all-reduce.3.cloned.1.call-done) | copy-start | bytes 1572868
  294.8 13.7 %all-to-all-start.3 = ((f32[32,1,1024]{2,1,0:T(1,128)}), f32[32,1,1024]{2,1,0:T(1,128)S(1)}, u32[]{:S(2)}, u32[]{:S(2)}) async-start(f32[32,1,1024]{2,1,0:T(1,128)} %broadcast_in_dim.100), calls=%async_computation.3 | async-start | bytes 262144 | tf_op jit(solution)/shard_map/all_to_all | solution.py:129
Sparse Core Ops, SparseCore 0:
  58.6 45.5 all-reduce.2
